TPU v7x, 32 devices: a whole 2x2x4 slice. The times are simulated.
32 devices in a mesh: blade: 4 (over z), inst: 4 (over x, core), cell: 2 (over y).
Axes of the slice: x: 2, y: 2, z: 4, core: 2. Of those that a mesh axis runs over, the one named last changes fastest.
Arguments:
- cell_coords: float32 [3, 320, 512], P(None, ('blade', 'cell'), 'inst'), may hold values from 0 to 1
- centre_points: float32 [3, 4096], P(None, ('blade', 'inst', 'cell')), may hold values from 0 to 1
- coefficients: float32 [24, 4096], P(None, ('blade', 'inst', 'cell')), may hold values from -1.2 to 1.2
- tile_lists: int32 [320, 4, 4], P(('blade', 'cell'), 'inst'), may hold values from 0 to 31, as said below
Outputs:
- displaced: float32 [8, 3, 320, 512], P('inst', None, ('blade', 'cell'))
- grid_velocity: float32 [8, 3, 320, 512], P('inst', None, ('blade', 'cell'))
Inputs may be any that keep to these rules, and one draw needn't show every extreme that they name: `tile_lists`: entry k of every list lies in k * 8 to (k + 1) * 8 - 1, so each cell tile draws centre tiles from every blade.
All inputs are finite; a program needn't handle non-finite values.
Results may differ from a plain program's by a relative error of at most 0.0003.
Values sent between devices are 32-bit elements; how exact they have to be, the bound alone decides.
No kernel may reach another device: no remote copies, remote signals or barrier semaphores. Data moves between devices by JAX's collectives and lax.ppermute only.
A program may use at most 64 MiB of HBM per device.

v0:
```python
import jax
import jax.numpy as jnp
from jax import lax
from jax.sharding import PartitionSpec as P

NT = 8
TILE = 128


def wendland(cell_tiles, near_points):
    squared = jnp.zeros(near_points.shape[1:] + cell_tiles.shape[-1:], jnp.float32)
    for axis_id in range(3):
        offset = near_points[axis_id][..., :, None] - cell_tiles[axis_id][:, None, None, :]
        squared = squared + offset * offset
    scaled = jnp.sqrt(squared) / 0.4
    margin = jnp.maximum(1.0 - scaled, 0.0)
    margin_sq = margin * margin
    return margin_sq * margin_sq * (1.0 + 4.0 * scaled)


def tile_sums(cell_tiles, list_rows, point_tiles, coef_tiles):
    near_points = point_tiles[:, list_rows]
    near_coefs = coef_tiles[:, list_rows]
    weights = wendland(cell_tiles, near_points)
    return jnp.einsum("amkj,mkjc->amc", near_coefs, weights, precision=lax.Precision.HIGHEST)


def block_sums(cell_tiles, list_rows, point_tiles, coef_tiles, width):
    groups = cell_tiles.shape[1] // width
    cell_groups = jnp.moveaxis(cell_tiles.reshape(3, groups, width, cell_tiles.shape[2]), 1, 0)
    list_groups = list_rows.reshape(groups, width, list_rows.shape[1])

    def one_group(operands):
        return tile_sums(operands[0], operands[1], point_tiles, coef_tiles)

    tile_totals = lax.map(one_group, (cell_groups, list_groups))
    return jnp.moveaxis(tile_totals, 0, 1).reshape(
        coef_tiles.shape[0], cell_tiles.shape[1], cell_tiles.shape[2]
    )


def spectral_matrix(instances):
    later = jnp.arange(instances, dtype=jnp.int32)[:, None]
    earlier = jnp.arange(instances, dtype=jnp.int32)[None, :]
    distance = (later - earlier).astype(jnp.float32)
    parity = jnp.where((later - earlier) % 2 == 0, 1.0, -1.0).astype(jnp.float32)
    guarded = jnp.where(distance == 0, 0.5, jnp.pi * distance / instances)
    values = 0.5 * parity * jnp.cos(guarded) / jnp.sin(guarded)
    return jnp.where(distance == 0, 0.0, values)


def on_device(cell_coords, centre_points, coefficients, tile_lists):
    coef_all, point_all = (
        lax.all_gather(coefficients, ("blade", "inst", "cell"), axis=1, tiled=True),
        lax.all_gather(centre_points, ("blade", "inst", "cell"), axis=1, tiled=True),
    )
    point_tiles = point_all.reshape(3, point_all.shape[1] // TILE, TILE)
    coef_tiles = coef_all.reshape(NT * 3, coef_all.shape[1] // TILE, TILE)
    row_count = cell_coords.shape[1]
    matrix = spectral_matrix(NT)
    shift = block_sums(cell_coords, tile_lists[:, 0, :], point_tiles, coef_tiles, 4)
    shift = shift.reshape(NT, 3, row_count, TILE)
    moved_points = cell_coords[None] + shift
    velocity_local = jnp.einsum("ts,sarc->tarc", matrix, shift, precision=lax.Precision.HIGHEST)
    displaced, grid_velocity = (
        lax.all_to_all(moved_points, "inst", split_axis=0, concat_axis=3, tiled=True),
        lax.all_to_all(velocity_local, "inst", split_axis=0, concat_axis=3, tiled=True),
    )
    return (displaced, grid_velocity)


def solution(mesh):
    in_specs = (
        P(None, ("blade", "cell"), "inst"),
        P(None, ("blade", "inst", "cell")),
        P(None, ("blade", "inst", "cell")),
        P(("blade", "cell"), "inst", None),
    )
    out_specs = (P("inst", None, ("blade", "cell"), None), P("inst", None, ("blade", "cell"), None))
    return jax.shard_map(
        on_device, mesh=mesh, in_specs=in_specs, out_specs=out_specs, check_vma=False
    )
```

profile of v0, /device:TPU:0, one launch (start us, length us, event | category | flops | bytes accessed | tf_op | source)
XLA Modules:
  0.0 199.8 jit_solution(7670787411031908554)
XLA Ops:
  0.6 72.0 %all_gather.7 = f32[24,4096]{1,0:T(8,128)S(1)} all-gather(f32[24,128]{1,0:T(8,128)} %param.8), channel_id=1, replica_groups=mesh['blade'=4,'inst'=4,'cell'=2] {'blade','inst','cell'}, dimensions={1}, use_global_device_ids=true | all-gather | bytes 405504 | tf_op jit(solution)/shard_map/all_gather | solution.py:54
  72.7 0.0 copy-start.1
  72.7 0.7 copy-done.1
  73.3 0.0 copy-start.2
  73.3 0.0 copy-start
  73.3 63.8 %all_gather.6 = f32[3,4096]{1,0:T(4,128)S(1)} all-gather(f32[3,128]{1,0:T(4,128)S(1)} %copy-done.1), channel_id=1, replica_groups=mesh['blade'=4,'inst'=4,'cell'=2] {'blade','inst','cell'}, dimensions={1}, use_global_device_ids=true | all-gather | bytes 50688 | tf_op jit(solution)/shard_map/all_gather | solution.py:55
  137.1 0.0 copy-done.2
  137.1 0.1 copy.23
  137.2 0.0 copy-done
  137.2 36.3 %while.12 = (s32[]{:T(128)}, f32[10,24,4,128]{3,1,2,0:T(8,128)S(1)}, s32[10,4,4]{2,1,0:T(4,128)S(1)}, f32[3,32,128]{2,0,1:T(4,128)S(1)}, f32[10,3,4,128]{3,2,0,1...) while((s32[]{:T(128)}, f32[10,24,4,128]{3,1,2,0:T(8,128)S(1)}, s32[10,4,4]{2,1,0:T(4,128)S(1)}, ...), condition=%wide.region_1.2_spmd, body=%wide.region_0.1_spmd.sunk | while | flops 79692848 | bytes 797209 | solution.py:36
  137.2 0.1 reshape.93
  137.3 0.6 gather_fusion.1
  137.9 0.6 gather_fusion
  138.5 2.3 %fusion.79 = f32[10,24,4,128]{3,1,2,0:T(8,128)S(1)} fusion(f32[10,24,4,128]{3,1,2,0:T(8,128)S(1)} %get-tuple-element.173, s32[]{:T(128)} %get-tuple-element.172, f32[24,4,4,128]{3,0,2,1:T(8,128)S(1)} %bitcast.82, f32[4,128]{1,0:T(4,128)S(1)} %get-tuple-element.159, f32[4,4,128]{2,1,0:T(4,128)S(1)} %bitcast.94, f32[4,128]{1,0:T(4,128)S(1)} %get-tuple-element.161, ...), kind=kOutput, calls=%fused_computation.3.clone.1 | convolution fusion | flops 79691776 | bytes 276484 | tf_op jit(solution)/shard_map/while/body/eval_jaxpr/amkj,mkjc->amc/dot_general | solution.py:25
  140.9 0.1 reshape.93
  141.0 0.6 gather_fusion.1
  141.6 0.6 gather_fusion
  142.2 2.3 %fusion.79 = f32[10,24,4,128]{3,1,2,0:T(8,128)S(1)} fusion(f32[10,24,4,128]{3,1,2,0:T(8,128)S(1)} %get-tuple-element.173, s32[]{:T(128)} %get-tuple-element.172, f32[24,4,4,128]{3,0,2,1:T(8,128)S(1)} %bitcast.82, f32[4,128]{1,0:T(4,128)S(1)} %get-tuple-element.159, f32[4,4,128]{2,1,0:T(4,128)S(1)} %bitcast.94, f32[4,128]{1,0:T(4,128)S(1)} %get-tuple-element.161, ...), kind=kOutput, calls=%fused_computation.3.clone.1 | convolution fusion | flops 79691776 | bytes 276484 | tf_op jit(solution)/shard_map/while/body/eval_jaxpr/amkj,mkjc->amc/dot_general | solution.py:25
  144.5 0.1 reshape.93
  144.6 0.6 gather_fusion.1
  145.2 0.6 gather_fusion
  145.8 2.3 %fusion.79 = f32[10,24,4,128]{3,1,2,0:T(8,128)S(1)} fusion(f32[10,24,4,128]{3,1,2,0:T(8,128)S(1)} %get-tuple-element.173, s32[]{:T(128)} %get-tuple-element.172, f32[24,4,4,128]{3,0,2,1:T(8,128)S(1)} %bitcast.82, f32[4,128]{1,0:T(4,128)S(1)} %get-tuple-element.159, f32[4,4,128]{2,1,0:T(4,128)S(1)} %bitcast.94, f32[4,128]{1,0:T(4,128)S(1)} %get-tuple-element.161, ...), kind=kOutput, calls=%fused_computation.3.clone.1 | convolution fusion | flops 79691776 | bytes 276484 | tf_op jit(solution)/shard_map/while/body/eval_jaxpr/amkj,mkjc->amc/dot_general | solution.py:25
  148.1 0.1 reshape.93
  148.2 0.6 gather_fusion.1
  148.8 0.6 gather_fusion
  149.4 2.3 %fusion.79 = f32[10,24,4,128]{3,1,2,0:T(8,128)S(1)} fusion(f32[10,24,4,128]{3,1,2,0:T(8,128)S(1)} %get-tuple-element.173, s32[]{:T(128)} %get-tuple-element.172, f32[24,4,4,128]{3,0,2,1:T(8,128)S(1)} %bitcast.82, f32[4,128]{1,0:T(4,128)S(1)} %get-tuple-element.159, f32[4,4,128]{2,1,0:T(4,128)S(1)} %bitcast.94, f32[4,128]{1,0:T(4,128)S(1)} %get-tuple-element.161, ...), kind=kOutput, calls=%fused_computation.3.clone.1 | convolution fusion | flops 79691776 | bytes 276484 | tf_op jit(solution)/shard_map/while/body/eval_jaxpr/amkj,mkjc->amc/dot_general | solution.py:25
  151.7 0.1 reshape.93
  151.8 0.6 gather_fusion.1
  152.5 0.6 gather_fusion
  153.1 2.3 %fusion.79 = f32[10,24,4,128]{3,1,2,0:T(8,128)S(1)} fusion(f32[10,24,4,128]{3,1,2,0:T(8,128)S(1)} %get-tuple-element.173, s32[]{:T(128)} %get-tuple-element.172, f32[24,4,4,128]{3,0,2,1:T(8,128)S(1)} %bitcast.82, f32[4,128]{1,0:T(4,128)S(1)} %get-tuple-element.159, f32[4,4,128]{2,1,0:T(4,128)S(1)} %bitcast.94, f32[4,128]{1,0:T(4,128)S(1)} %get-tuple-element.161, ...), kind=kOutput, calls=%fused_computation.3.clone.1 | convolution fusion | flops 79691776 | bytes 276484 | tf_op jit(solution)/shard_map/while/body/eval_jaxpr/amkj,mkjc->amc/dot_general | solution.py:25
  155.4 0.1 reshape.93
  155.5 0.6 gather_fusion.1
  156.1 0.6 gather_fusion
  156.7 2.3 %fusion.79 = f32[10,24,4,128]{3,1,2,0:T(8,128)S(1)} fusion(f32[10,24,4,128]{3,1,2,0:T(8,128)S(1)} %get-tuple-element.173, s32[]{:T(128)} %get-tuple-element.172, f32[24,4,4,128]{3,0,2,1:T(8,128)S(1)} %bitcast.82, f32[4,128]{1,0:T(4,128)S(1)} %get-tuple-element.159, f32[4,4,128]{2,1,0:T(4,128)S(1)} %bitcast.94, f32[4,128]{1,0:T(4,128)S(1)} %get-tuple-element.161, ...), kind=kOutput, calls=%fused_computation.3.clone.1 | convolution fusion | flops 79691776 | bytes 276484 | tf_op jit(solution)/shard_map/while/body/eval_jaxpr/amkj,mkjc->amc/dot_general | solution.py:25
  159.0 0.1 reshape.93
  159.1 0.6 gather_fusion.1
  159.7 0.6 gather_fusion
  160.3 2.3 %fusion.79 = f32[10,24,4,128]{3,1,2,0:T(8,128)S(1)} fusion(f32[10,24,4,128]{3,1,2,0:T(8,128)S(1)} %get-tuple-element.173, s32[]{:T(128)} %get-tuple-element.172, f32[24,4,4,128]{3,0,2,1:T(8,128)S(1)} %bitcast.82, f32[4,128]{1,0:T(4,128)S(1)} %get-tuple-element.159, f32[4,4,128]{2,1,0:T(4,128)S(1)} %bitcast.94, f32[4,128]{1,0:T(4,128)S(1)} %get-tuple-element.161, ...), kind=kOutput, calls=%fused_computation.3.clone.1 | convolution fusion | flops 79691776 | bytes 276484 | tf_op jit(solution)/shard_map/while/body/eval_jaxpr/amkj,mkjc->amc/dot_general | solution.py:25
  162.6 0.1 reshape.93
  162.7 0.6 gather_fusion.1
  163.3 0.6 gather_fusion
  163.9 2.3 %fusion.79 = f32[10,24,4,128]{3,1,2,0:T(8,128)S(1)} fusion(f32[10,24,4,128]{3,1,2,0:T(8,128)S(1)} %get-tuple-element.173, s32[]{:T(128)} %get-tuple-element.172, f32[24,4,4,128]{3,0,2,1:T(8,128)S(1)} %bitcast.82, f32[4,128]{1,0:T(4,128)S(1)} %get-tuple-element.159, f32[4,4,128]{2,1,0:T(4,128)S(1)} %bitcast.94, f32[4,128]{1,0:T(4,128)S(1)} %get-tuple-element.161, ...), kind=kOutput, calls=%fused_computation.3.clone.1 | convolution fusion | flops 79691776 | bytes 276484 | tf_op jit(solution)/shard_map/while/body/eval_jaxpr/amkj,mkjc->amc/dot_general | solution.py:25
  166.3 0.1 reshape.93
  166.4 0.6 gather_fusion.1
  167.0 0.6 gather_fusion
  167.6 2.3 %fusion.79 = f32[10,24,4,128]{3,1,2,0:T(8,128)S(1)} fusion(f32[10,24,4,128]{3,1,2,0:T(8,128)S(1)} %get-tuple-element.173, s32[]{:T(128)} %get-tuple-element.172, f32[24,4,4,128]{3,0,2,1:T(8,128)S(1)} %bitcast.82, f32[4,128]{1,0:T(4,128)S(1)} %get-tuple-element.159, f32[4,4,128]{2,1,0:T(4,128)S(1)} %bitcast.94, f32[4,128]{1,0:T(4,128)S(1)} %get-tuple-element.161, ...), kind=kOutput, calls=%fused_computation.3.clone.1 | convolution fusion | flops 79691776 | bytes 276484 | tf_op jit(solution)/shard_map/while/body/eval_jaxpr/amkj,mkjc->amc/dot_general | solution.py:25
  169.9 0.1 reshape.93
  170.0 0.6 gather_fusion.1
  170.6 0.6 gather_fusion
  171.2 2.3 %fusion.79 = f32[10,24,4,128]{3,1,2,0:T(8,128)S(1)} fusion(f32[10,24,4,128]{3,1,2,0:T(8,128)S(1)} %get-tuple-element.173, s32[]{:T(128)} %get-tuple-element.172, f32[24,4,4,128]{3,0,2,1:T(8,128)S(1)} %bitcast.82, f32[4,128]{1,0:T(4,128)S(1)} %get-tuple-element.159, f32[4,4,128]{2,1,0:T(4,128)S(1)} %bitcast.94, f32[4,128]{1,0:T(4,128)S(1)} %get-tuple-element.161, ...), kind=kOutput, calls=%fused_computation.3.clone.1 | convolution fusion | flops 79691776 | bytes 276484 | tf_op jit(solution)/shard_map/while/body/eval_jaxpr/amkj,mkjc->amc/dot_general | solution.py:25
  173.5 0.1 copy.26
  173.6 0.6 fusion.32
  174.2 0.9 copy.29
  175.1 3.5 %all-to-all-start.1 = ((f32[8,3,40,128]{3,2,1,0:T(8,128)}), f32[8,3,40,128]{3,2,1,0:T(8,128)S(1)}, u32[]{:S(2)}, u32[]{:S(2)}) async-start(f32[8,3,40,128]{3,2,1,0:T(8,128)} %copy.29), calls=%async_computation.1 | async-start | bytes 983040 | tf_op jit(solution)/shard_map/all_to_all | solution.py:67
  178.6 0.8 broadcast_add_fusion
  179.4 7.6 %all-to-all-done.1 = f32[8,3,40,128]{3,2,1,0:T(8,128)S(1)} async-done(((f32[8,3,40,128]{3,2,1,0:T(8,128)}), f32[8,3,40,128]{3,2,1,0:T(8,128)S(1)}, u32[]{:S(2)}, u32[]{:S(2)}) %all-to-all-start.1) | async-done | bytes 491552 | tf_op jit(solution)/shard_map/all_to_all | solution.py:67
  187.0 3.5 %all-to-all-start = ((f32[8,3,40,128]{3,2,1,0:T(8,128)}), f32[8,3,40,128]{3,2,1,0:T(8,128)S(1)}, u32[]{:S(2)}, u32[]{:S(2)}) async-start(f32[8,3,40,128]{3,2,1,0:T(8,128)} %broadcast_add_fusion), calls=%async_computation | async-start | bytes 983040 | tf_op jit(solution)/shard_map/all_to_all | solution.py:66
  190.5 0.8 copy.42
  191.3 7.6 %all-to-all-done = f32[8,3,40,128]{3,2,1,0:T(8,128)S(1)} async-done(((f32[8,3,40,128]{3,2,1,0:T(8,128)}), f32[8,3,40,128]{3,2,1,0:T(8,128)S(1)}, u32[]{:S(2)}, u32[]{:S(2)}) %all-to-all-start) | async-done | bytes 491552 | tf_op jit(solution)/shard_map/all_to_all | solution.py:66
  198.9 0.8 copy.43
  (52 shorter events, 0.5 us)
Async XLA Ops:
  72.7 0.7 copy-start.1
  73.3 63.8 %copy-start.2 = (s32[40,1,4]{0,2,1:T(4,128)S(1)}, s32[40,1,4]{0,2,1:T(4,128)}, u32[]{:S(2)}) copy-start(s32[40,1,4]{0,2,1:T(4,128)} %param.9) | copy-start | bytes 1924
  73.3 63.9 %copy-start = (f32[3,40,128]{2,1,0:T(8,128)S(1)}, f32[3,40,128]{2,1,0:T(8,128)}, u32[]{:S(2)}) copy-start(f32[3,40,128]{2,1,0:T(8,128)} %param.6) | copy-start | bytes 184324
  175.1 11.9 %all-to-all-start.1 = ((f32[8,3,40,128]{3,2,1,0:T(8,128)}), f32[8,3,40,128]{3,2,1,0:T(8,128)S(1)}, u32[]{:S(2)}, u32[]{:S(2)}) async-start(f32[8,3,40,128]{3,2,1,0:T(8,128)} %copy.29), calls=%async_computation.1 | async-start | bytes 983040 | tf_op jit(solution)/shard_map/all_to_all | solution.py:67
  187.0 11.9 %all-to-all-start = ((f32[8,3,40,128]{3,2,1,0:T(8,128)}), f32[8,3,40,128]{3,2,1,0:T(8,128)S(1)}, u32[]{:S(2)}, u32[]{:S(2)}) async-start(f32[8,3,40,128]{3,2,1,0:T(8,128)} %broadcast_add_fusion), calls=%async_computation | async-start | bytes 983040 | tf_op jit(solution)/shard_map/all_to_all | solution.py:66
where the time goes:
time: 200 us
  blocking collectives  136 us (68%)
  matrix products  23.4 us (12%)
  local copies, waits for them, and re-layouts  16.1 us (8%)
  waiting for transfers between devices  15.2 us (8%)
  starting transfers between devices  6.94 us (3%)
    all_gather x1, blocking collectives, on_device(): lax.all_gather(coefficients, ('blade', 'inst', 'cell'), axis=1, tiled=True)  72 us
    all_gather x1, blocking collectives, on_device(): lax.all_gather(centre_points, ('blade', 'inst', 'cell'), axis=1, tiled=True)  63.8 us
    dot_general x10, matrix products, tile_sums(): jnp.einsum('amkj,mkjc->amc', near_coefs, weights, precision=lax.Precision...  22.8 us
    all_to_all x1, waiting for transfers between devices, on_device(): lax.all_to_all(velocity_local, 'inst', split_axis=0, concat_axis=3, tiled...  7.61 us
    all_to_all x1, waiting for transfers between devices, on_device(): lax.all_to_all(moved_points, 'inst', split_axis=0, concat_axis=3, tiled=T...  7.59 us
    gather x10, local copies, waits for them, and re-layouts, tile_sums(): near_points = point_tiles[:, list_rows]  5.88 us
    gather x10, local copies, waits for them, and re-layouts, tile_sums(): near_coefs = coef_tiles[:, list_rows]  5.66 us
  transfers between devices with their start and end apart: 2, of which 2 were waited for; matrix products, arithmetic and copies ran while one was open for 1% of the time, Pallas kernels for 0%

commit v1 on v0

v1 whole, which is shorter than its diff:
```python
import functools

import jax
import jax.numpy as jnp
import numpy as np
from jax import lax
from jax.experimental import pallas as pl
from jax.experimental.pallas import tpu as pltpu
from jax.sharding import PartitionSpec as P

NT = 8
TILE = 128
RADIUS = 0.4
EDGE = 4.0**0.2
SCALE = (EDGE / RADIUS) ** 2
FEATURES = 48
BOTH_MINOR = (((1,), (1,)), ((), ()))
F32 = jnp.float32
BF16 = jnp.bfloat16


def spectral_rows(instances, groups):
    later = np.arange(instances)[:, None]
    earlier = np.arange(instances)[None, :]
    distance = (later - earlier).astype(np.float64)
    guarded = np.where(distance == 0, 0.5, np.pi * distance / instances)
    parity = np.where((later - earlier) % 2 == 0, 1.0, -1.0)
    matrix = np.where(distance == 0, 0.0, 0.5 * parity * np.cos(guarded) / np.sin(guarded))
    per = instances // groups
    rows = []
    for group in range(groups):
        own = slice(group * per, (group + 1) * per)
        rows.append(np.concatenate([np.eye(instances)[own], matrix[own]], axis=0))
    return np.stack([np.kron(block, np.eye(3)) for block in rows]).astype(np.float32)


def split3(value):
    high = value.astype(BF16).astype(F32)
    rest = value - high
    middle = rest.astype(BF16).astype(F32)
    return high, middle, rest - middle


def flip(size, bit):
    return [(i, i ^ bit) for i in range(size)]


def bits_of(size):
    return [1 << b for b in range(size.bit_length() - 1)]


def cell_prep_kernel(own_ref, other_ref, feature_ref, coord_ref, *, rows, slots):
    for slot in range(slots):
        source = own_ref if slot == 0 else other_ref.at[slot - 1]

        def one_row(r, carry):
            value = source[r]
            high, middle, low = split3(value)
            stacked = jnp.concatenate([high, middle, low, high, middle, high], axis=0)
            feature_ref[slot, r] = stacked.T.astype(BF16)
            coord_ref[slot, pl.ds(r, 8, stride=rows), :] = value
            return carry

        lax.fori_loop(0, rows, one_row, 0, unroll=4)


def sums_kernel(
    list_ref, mix_ref, block_ref, feature_ref, coord_ref, own_ref, peer_ref,
    centre_ref, coef_ref, total_ref, dist0, dist1, weight0, weight1, *, rows, slots, terms, half,
):
    tiles = block_ref.shape[0]
    combos = 2 * half

    def one_tile(p, carry):
        high, middle, low = split3(block_ref[p, 3 * NT : 3 * NT + 8, :])
        centre_ref[p] = jnp.concatenate([high, high, high, middle, middle, low], axis=0).astype(BF16)
        mixed = jnp.dot(
            mix_ref[...], block_ref[p, : 3 * NT, :],
            preferred_element_type=F32, precision=lax.Precision.HIGHEST,
        )
        mixed_high = mixed.astype(BF16).astype(F32)
        coef_ref[p] = jnp.concatenate([mixed_high, mixed - mixed_high], axis=0).astype(BF16)
        return carry

    lax.fori_loop(0, tiles, one_tile, 0, unroll=4)

    def tile_pair(r, slot, pair):
        base = (slot * rows + r) * terms + 2 * pair
        return list_ref[base], list_ref[base + 1]

    def distances(r, slot, out):
        for pair in range(terms // 2):
            a, b = tile_pair(r, slot, pair)
            out[pair] = jnp.dot(
                feature_ref[slot, r], jnp.concatenate([centre_ref[a], centre_ref[b]], axis=1),
                preferred_element_type=F32,
            )

    def weights(source, out):
        for pair in range(terms // 2):
            squared = jnp.maximum(source[pair], 1e-12)
            margin = jnp.maximum(EDGE - squared * lax.rsqrt(squared), 0.0)
            margin_sq = margin * margin
            weight = (margin_sq * margin_sq) * (1.25 * EDGE - margin)
            high = weight.astype(BF16)
            out[pair, :TILE] = high
            out[pair, TILE:] = (weight - high.astype(F32)).astype(BF16)

    def contract(r, slot, source):
        total = None
        for pair in range(terms // 2):
            a, b = tile_pair(r, slot, pair)
            part = lax.dot_general(
                jnp.concatenate([coef_ref[a], coef_ref[b]], axis=1), source[pair], BOTH_MINOR,
                preferred_element_type=F32,
            )
            total = part if total is None else total + part
        total = total[:combos, :TILE] + total[combos:, :TILE] + total[:combos, TILE:]
        for group in range(combos // 8):
            total_ref[slot, pl.ds(r + group * 8 * rows, 8, stride=rows), :] = total[group * 8 : group * 8 + 8]

    distances(0, 0, dist0)

    def one_row(r, carry):
        contract(jnp.maximum(r - 1, 0), 1, weight1)
        distances(r, 1, dist1)
        weights(dist0, weight0)
        contract(r, 0, weight0)
        distances(jnp.minimum(r + 1, rows - 1), 0, dist0)
        weights(dist1, weight1)
        return carry

    lax.fori_loop(0, rows, one_row, 0, unroll=2)
    contract(rows - 1, 1, weight1)

    shifts = half // 2
    for slot in range(slots):
        for out, first in ((own_ref, 0), (peer_ref, half)):
            for c in range(half):
                value = total_ref[slot, (first + c) * rows : (first + c + 1) * rows, :]
                if c < shifts:
                    value = value + (coord_ref[slot, (c % 3) * rows : (c % 3 + 1) * rows, :] + 0.5)
                out[slot, c] = value


def merge_kernel(place_ref, own_ref, peer_ref, moved_ref, velocity_ref, sems, *, slots, half):
    shifts = half // 2
    copies = []
    for which, source in enumerate((own_ref, peer_ref)):
        for slot in range(slots):
            lane = pl.multiple_of(place_ref[which * slots + slot] * TILE, TILE)
            for part, out in enumerate((moved_ref, velocity_ref)):
                copies.append(
                    pltpu.make_async_copy(
                        source.at[slot, pl.ds(part * shifts, shifts)],
                        out.at[:, :, pl.ds(lane, TILE)],
                        sems.at[len(copies)],
                    )
                )
    for copy in copies:
        copy.start()
    for copy in copies:
        copy.wait()


def vmem():
    return pl.BlockSpec(memory_space=pltpu.VMEM)


def smem():
    return pl.BlockSpec(memory_space=pltpu.SMEM)


def hbm():
    return pl.BlockSpec(memory_space=pl.ANY)


def on_device(cell_coords, centre_points, coefficients, tile_lists, *, sizes):
    n_blade, n_inst, n_cell = sizes["blade"], sizes["inst"], sizes["cell"]
    rows = cell_coords.shape[1]
    terms = tile_lists.shape[2]
    width = centre_points.shape[1]
    slots = n_inst // 2
    half = 2 * 3 * (NT // n_inst)
    inst = lax.axis_index("inst")
    device = (lax.axis_index("blade") * n_inst + inst) * n_cell + lax.axis_index("cell")

    centred = centre_points - 0.5
    block = jnp.concatenate(
        [
            coefficients,
            (-2.0 * SCALE) * centred,
            SCALE * jnp.sum(centred * centred, axis=0, keepdims=True),
            jnp.ones((1, width), F32),
            jnp.zeros((3, width), F32),
        ],
        axis=0,
    )
    cells = cell_coords - 0.5
    list_row = jnp.pad(tile_lists[:, 0, :].astype(F32), ((0, 0), (0, TILE - terms)))
    blank = jnp.zeros_like(list_row)
    cell_rows = jnp.stack(
        [cells[0], cells[1], cells[2], blank + 1.0, SCALE * jnp.sum(cells * cells, axis=0), list_row, blank, blank],
        axis=1,
    )

    others = [lax.ppermute(cell_rows, "inst", flip(n_inst, 2 * s)) for s in range(1, slots)]

    phases = [("blade", n_blade, b, b * n_inst * n_cell) for b in reversed(bits_of(n_blade))]
    phases += [("cell", n_cell, b, b) for b in bits_of(n_cell)]
    phases += [("inst", n_inst, b, b * n_cell) for b in reversed(bits_of(n_inst))]
    blocks = block[None]
    for axis, size, bit, _ in phases:
        blocks = jnp.concatenate([blocks, lax.ppermute(blocks, axis, flip(size, bit))], axis=0)

    def position(index):
        relative = index ^ device
        return sum(((relative // mask) & 1) << k for k, (_, _, _, mask) in enumerate(phases))

    lists = jnp.stack(
        [tile_lists[:, 0, :]] + [o[:, 5, :terms].astype(jnp.int32) for o in others], axis=0
    )
    if width == TILE:
        lists = position(lists)
    else:
        per_tile = TILE // width
        blocks = jnp.take(blocks, position(jnp.arange(blocks.shape[0])), axis=0)
        blocks = blocks.reshape(-1, per_tile, 3 * NT + 8, width)
        blocks = jnp.moveaxis(blocks, 1, 2).reshape(-1, 3 * NT + 8, TILE)
    n_tiles = blocks.shape[0]

    features, coords = pl.pallas_call(
        functools.partial(cell_prep_kernel, rows=rows, slots=slots),
        out_shape=(
            jax.ShapeDtypeStruct((slots, rows, TILE, FEATURES), BF16),
            jax.ShapeDtypeStruct((slots, 8 * rows, TILE), F32),
        ),
        in_specs=[vmem(), vmem()],
        out_specs=(vmem(), vmem()),
        name="cell_prep",
    )(cell_rows, jnp.stack(others))

    mix_all = jnp.asarray(spectral_rows(NT, n_inst))
    mix = jnp.concatenate([mix_all[inst], mix_all[inst ^ 1]], axis=0)
    own, peer = pl.pallas_call(
        functools.partial(sums_kernel, rows=rows, slots=slots, terms=terms, half=half),
        out_shape=(jax.ShapeDtypeStruct((slots, half, rows, TILE), F32),) * 2,
        in_specs=[smem(), vmem(), vmem(), vmem(), vmem()],
        out_specs=(vmem(), vmem()),
        scratch_shapes=[
            pltpu.VMEM((n_tiles, FEATURES, TILE), BF16),
            pltpu.VMEM((n_tiles, 4 * half, TILE), BF16),
            pltpu.VMEM((slots, 2 * half * rows, TILE), F32),
            pltpu.VMEM((terms // 2, TILE, 2 * TILE), F32),
            pltpu.VMEM((terms // 2, TILE, 2 * TILE), F32),
            pltpu.VMEM((terms // 2, 2 * TILE, 2 * TILE), BF16),
            pltpu.VMEM((terms // 2, 2 * TILE, 2 * TILE), BF16),
        ],
        name="rbf_sums",
    )(lists.reshape(-1), mix, blocks, features, coords)

    received = lax.ppermute(peer, "inst", flip(n_inst, 1))
    slot_bits = 2 * jnp.arange(slots, dtype=jnp.int32)
    places = jnp.concatenate([inst ^ slot_bits, inst ^ 1 ^ slot_bits])
    out = jax.ShapeDtypeStruct((half // 2, rows, n_inst * TILE), F32)
    moved, velocity = pl.pallas_call(
        functools.partial(merge_kernel, slots=slots, half=half),
        out_shape=(out, out),
        in_specs=[smem(), hbm(), hbm()],
        out_specs=(hbm(), hbm()),
        scratch_shapes=[pltpu.SemaphoreType.DMA((4 * slots,))],
        name="merge",
    )(places, own, received)
    shape = (NT // n_inst, 3, rows, n_inst * TILE)
    return (moved.reshape(shape), velocity.reshape(shape))


def solution(mesh):
    sizes = dict(mesh.shape)
    in_specs = (
        P(None, ("blade", "cell"), "inst"),
        P(None, ("blade", "inst", "cell")),
        P(None, ("blade", "inst", "cell")),
        P(("blade", "cell"), "inst", None),
    )
    out_specs = (P("inst", None, ("blade", "cell"), None), P("inst", None, ("blade", "cell"), None))
    return jax.shard_map(
        functools.partial(on_device, sizes=sizes),
        mesh=mesh, in_specs=in_specs, out_specs=out_specs, check_vma=False,
    )
```

time: 200 us -> 83.9 us (0.42)
  blocking collectives: 136 us -> 0 us
  Pallas kernels: 0 us -> 53.8 us
  matrix products: 23.4 us -> 0 us
  local copies, waits for them, and re-layouts: 16.1 us -> 4.4 us
  waiting for transfers between devices: 15.2 us -> 10.5 us
  other arithmetic: 0.99 us -> 4.07 us
  starting transfers between devices: 6.94 us -> 9.94 us
    all_gather x2 -> x0, blocking collectives: 136 us -> none  [the longest x1 72 us: on_device(): lax.all_gather(coefficients, ('blade', 'inst', 'cell'), axis=1, tiled=True)]
    pallas_call x0 -> x3, Pallas kernels: none -> 53.8 us  [the longest x1 31.6 us: on_device(): pl.pallas_call(functools.partial(merge_kernel, slots=slots, half=half), o...]
    dot_general x11 -> x0, matrix products: 23.4 us -> none  [the longest x10 22.8 us: tile_sums(): jnp.einsum('amkj,mkjc->amc', near_coefs, weights, precision=lax.Precision...]
    all_to_all x2 -> x0, waiting for transfers between devices: 15.2 us -> none  [the longest x1 7.61 us: on_device(): lax.all_to_all(velocity_local, 'inst', split_axis=0, concat_axis=3, tiled...]
    gather x20 -> x0, local copies, waits for them, and re-layouts: 11.5 us -> none  [the longest x10 5.88 us: tile_sums(): near_points = point_tiles[:, list_rows]]
    ppermute x0 -> x7, waiting for transfers between devices: none -> 10.5 us  [the longest x5 9.37 us: on_device(): lax.ppermute(blocks, axis, flip(size, bit))]
    ppermute x0 -> x7, starting transfers between devices: none -> 9.94 us  [the longest x5 7.89 us: on_device(): lax.ppermute(blocks, axis, flip(size, bit))]
    all_to_all x2 -> x0, starting transfers between devices: 6.94 us -> none  [the longest x1 3.47 us: on_device(): lax.all_to_all(moved_points, 'inst', split_axis=0, concat_axis=3, tiled=T...]
  transfers between devices with their start and end apart: 2 -> 7, of which waited for: 2 -> 4; matrix products, arithmetic and copies ran while one was open for 1% -> 6% of each run, Pallas kernels for 0% -> 6%
where the time goes in v1:
time: 83.9 us; the launch traced here: 83.5 us
  Pallas kernels  53.8 us (64%)
  waiting for transfers between devices  10.5 us (13%)
  starting transfers between devices  9.94 us (12%)
  local copies, waits for them, and re-layouts  4.4 us (5%)
  other arithmetic  4.07 us (5%)
    pallas_call x1, Pallas kernels, on_device(): pl.pallas_call(functools.partial(merge_kernel, slots=slots, half=half), o...  31.6 us
    pallas_call x1, Pallas kernels, on_device(): pl.pallas_call(functools.partial(sums_kernel, rows=rows, slots=slots, ter...  17.5 us
    ppermute x5, waiting for transfers between devices, on_device(): lax.ppermute(blocks, axis, flip(size, bit))  9.37 us
    ppermute x5, starting transfers between devices, on_device(): lax.ppermute(blocks, axis, flip(size, bit))  7.89 us
    pallas_call x1, Pallas kernels, on_device(): pl.pallas_call(functools.partial(cell_prep_kernel, rows=rows, slots=slots...  4.67 us
    unnamed x13, local copies, waits for them, and re-layouts  2.38 us
  transfers between devices with their start and end apart: 7, of which 4 were waited for; matrix products, arithmetic and copies ran while one was open for 6% of the time, Pallas kernels for 6%

profile of v1, /device:TPU:0, one launch (start us, length us, event | category | flops | bytes accessed | tf_op | source)
XLA Modules:
  0.0 83.5 jit_solution(16715440914614790463)
XLA Ops:
  0.6 0.7 multiply_reduce_fusion.1
  1.3 0.7 concatenate.30
  2.1 4.1 %collective-permute-start.1 = (f32[1,32,128]{2,1,0:T(8,128)S(1)}, f32[1,32,128]{2,1,0:T(8,128)S(1)}, u32[]{:S(2)}, u32[]{:S(2)}) collective-permute-start(f32[1,32,128]{2,1,0:T(8,128)S(1)} %bitcast.25), channel_id=1, source_target_pairs={{0,16},{8,24},{16,0},{24,8},{1,17},{9,25},{17,1},{25,9},{2,18},{10... | collective-permute-start | bytes 49160 | tf_op jit(solution)/shard_map/ppermute | solution.py:214
  6.2 0.8 copy.15
  7.0 0.8 %multiply_reduce_fusion = (f32[40,128]{1,0:T(8,128)S(1)}, f32[3,40,128]{2,1,0:T(8,128)S(1)}) fusion(f32[3,40,128]{2,1,0:T(8,128)} %param.5), kind=kLoop, calls=%fused_computation.2 | loop fusion | flops 40960 | bytes 143360 | tf_op jit(solution)/shard_map/reduce_sum | solution.py:203
  7.9 0.2 stack.23.own_ref
  8.1 0.0 copy-start
  8.1 1.6 %collective-permute-start = (f32[40,8,128]{2,1,0:T(8,128)S(1)}, f32[40,8,128]{2,1,0:T(8,128)S(1)}, u32[]{:S(2)}, u32[]{:S(2)}) collective-permute-start(f32[40,8,128]{2,1,0:T(8,128)S(1)} %stack.23.own_ref), channel_id=1, source_target_pairs={{0,4},{2,6},{4,0},{6,2},{1,5},{3,7},{5,1},{7,3},{8,12},{10,14},{12... | collective-permute-start | bytes 491528 | tf_op jit(solution)/shard_map/ppermute | solution.py:207
  9.7 0.7 dynamic-slice_bitcast_fusion.1
  10.4 0.6 pad_maximum_fusion.3.mix_ref
  11.0 0.0 collective-permute-done.1
  11.0 1.6 %collective-permute-start.2 = (f32[2,32,128]{2,1,0:T(8,128)S(1)}, f32[2,32,128]{2,1,0:T(8,128)S(1)}, u32[]{:S(2)}, u32[]{:S(2)}) collective-permute-start(f32[2,32,128]{2,1,0:T(8,128)S(1)} %pad_maximum_fusion.2), channel_id=1, source_target_pairs={{0,8},{8,0},{16,24},{24,16},{1,9},{9,1},{17,25},{25,17},{2,10},{10... | collective-permute-start | bytes 98312 | tf_op jit(solution)/shard_map/ppermute | solution.py:214
  12.6 2.3 %collective-permute-done.2 = f32[2,32,128]{2,1,0:T(8,128)S(1)} collective-permute-done((f32[2,32,128]{2,1,0:T(8,128)S(1)}, f32[2,32,128]{2,1,0:T(8,128)S(1)}, u32[]{:S(2)}, u32[]{:S(2)}) %collective-permute-start.2) | collective-permute-done | bytes 32800 | tf_op jit(solution)/shard_map/ppermute | solution.py:214
  14.9 1.5 %collective-permute-start.3 = (f32[4,32,128]{2,1,0:T(8,128)S(1)}, f32[4,32,128]{2,1,0:T(8,128)S(1)}, u32[]{:S(2)}, u32[]{:S(2)}) collective-permute-start(f32[4,32,128]{2,1,0:T(8,128)S(1)} %pad_maximum_fusion.1), channel_id=1, source_target_pairs={{0,1},{1,0},{2,3},{3,2},{4,5},{5,4},{6,7},{7,6},{8,9},{9,8},{10,11... | collective-permute-start | bytes 196616 | tf_op jit(solution)/shard_map/ppermute | solution.py:214
  16.5 2.7 %collective-permute-done.3 = f32[4,32,128]{2,1,0:T(8,128)S(1)} collective-permute-done((f32[4,32,128]{2,1,0:T(8,128)S(1)}, f32[4,32,128]{2,1,0:T(8,128)S(1)}, u32[]{:S(2)}, u32[]{:S(2)}) %collective-permute-start.3) | collective-permute-done | bytes 65568 | tf_op jit(solution)/shard_map/ppermute | solution.py:214
  19.2 0.6 collective-permute-start.4
  19.8 0.0 collective-permute-done
  19.8 0.0 copy-start.3
  19.9 0.1 copy.18
  20.0 4.3 %collective-permute-done.4 = f32[8,32,128]{2,1,0:T(8,128)S(1)} collective-permute-done((f32[8,32,128]{2,1,0:T(8,128)S(1)}, f32[8,32,128]{2,1,0:T(8,128)S(1)}, u32[]{:S(2)}, u32[]{:S(2)}) %collective-permute-start.4) | collective-permute-done | bytes 131104 | tf_op jit(solution)/shard_map/ppermute | solution.py:214
  24.3 0.1 collective-permute-start.5
  24.4 0.7 add_xor_fusion
  25.0 0.1 copy.19
  25.1 0.1 xor.33
  25.3 0.0 copy-done
  25.3 0.0 copy-done.3
  25.3 4.7 %cell_prep.1 = (bf16[2,40,128,48]{3,2,1,0:T(8,128)(2,1)}, f32[2,320,128]{2,1,0:T(8,128)}) custom-call(f32[40,8,128]{2,1,0:T(8,128)} %copy-done, f32[1,40,8,128]{3,2,1,0:T(8,128)} %bitcast.29), custom_call_target="tpu_custom_call" | custom-call | tf_op jit(solution)/shard_map/cell_prep/pallas_call | solution.py:232
  29.9 0.6 fusion.6.list_ref
  30.6 0.0 collective-permute-done.5
  30.6 0.0 copy-start.1
  30.6 0.8 copy-done.1
  31.4 17.5 %rbf_sums.1 = (f32[2,12,40,128]{3,2,1,0:T(8,128)}, f32[2,12,40,128]{3,2,1,0:T(8,128)}) custom-call(s32[320]{0:T(512)} %fusion.6.list_ref, f32[24,24]{1,0:T(8,128)} %pad_maximum_fusion.3.mix_ref, f32[32,32,128]{2,1,0:T(8,128)} %copy-done.1, bf16[2,40,128,48]{3,2,1,0:T(8,128)(2,1)} %get-tuple-element.8.feature_ref, f32[2,320,128]{2,1,0:T(8,128)} %get-tuple-element.9.coord_ref), custom_call_target="tpu_custom_call" | custom-call | tf_op jit(solution)/shard_map/rbf_sums/pallas_call | solution.py:245
  48.9 0.5 collective-permute-start.6
  49.4 0.6 pad_add_fusion.place_ref
  50.0 1.1 %collective-permute-done.6.peer_ref = f32[2,12,40,128]{3,2,1,0:T(8,128)S(1)} collective-permute-done((f32[2,12,40,128]{3,2,1,0:T(8,128)}, f32[2,12,40,128]{3,2,1,0:T(8,128)S(1)}, u32[]{:S(2)}, u32[]{:S(2)}) %collective-permute-start.6) | collective-permute-done | bytes 491552 | tf_op jit(solution)/shard_map/ppermute | solution.py:262
  51.1 0.0 copy-start.2
  51.1 0.8 copy-done.2
  51.9 31.6 %merge.1 = (f32[6,40,512]{2,1,0:T(8,128)}, f32[6,40,512]{2,1,0:T(8,128)}) custom-call(s32[4]{0:T(128)} %pad_add_fusion.place_ref, f32[2,12,40,128]{3,2,1,0:T(8,128)} %get-tuple-element.10.own_ref, f32[2,12,40,128]{3,2,1,0:T(8,128)} %copy-done.2), custom_call_target="tpu_custom_call" | custom-call | tf_op jit(solution)/shard_map/merge/pallas_call | solution.py:266
  (20 shorter events, 0.2 us)
Async XLA Ops:
  2.1 8.9 %collective-permute-start.1 = (f32[1,32,128]{2,1,0:T(8,128)S(1)}, f32[1,32,128]{2,1,0:T(8,128)S(1)}, u32[]{:S(2)}, u32[]{:S(2)}) collective-permute-start(f32[1,32,128]{2,1,0:T(8,128)S(1)} %bitcast.25), channel_id=1, source_target_pairs={{0,16},{8,24},{16,0},{24,8},{1,17},{9,25},{17,1},{25,9},{2,18},{10... | collective-permute-start | bytes 49160 | tf_op jit(solution)/shard_map/ppermute | solution.py:214
  8.1 17.1 %copy-start = (f32[40,8,128]{2,1,0:T(8,128)}, f32[40,8,128]{2,1,0:T(8,128)S(1)}, u32[]{:S(2)}) copy-start(f32[40,8,128]{2,1,0:T(8,128)S(1)} %stack.23.own_ref) | copy-start | bytes 491524
  8.1 11.7 %collective-permute-start = (f32[40,8,128]{2,1,0:T(8,128)S(1)}, f32[40,8,128]{2,1,0:T(8,128)S(1)}, u32[]{:S(2)}, u32[]{:S(2)}) collective-permute-start(f32[40,8,128]{2,1,0:T(8,128)S(1)} %stack.23.own_ref), channel_id=1, source_target_pairs={{0,4},{2,6},{4,0},{6,2},{1,5},{3,7},{5,1},{7,3},{8,12},{10,14},{12... | collective-permute-start | bytes 491528 | tf_op jit(solution)/shard_map/ppermute | solution.py:207
  11.0 3.9 %collective-permute-start.2 = (f32[2,32,128]{2,1,0:T(8,128)S(1)}, f32[2,32,128]{2,1,0:T(8,128)S(1)}, u32[]{:S(2)}, u32[]{:S(2)}) collective-permute-start(f32[2,32,128]{2,1,0:T(8,128)S(1)} %pad_maximum_fusion.2), channel_id=1, source_target_pairs={{0,8},{8,0},{16,24},{24,16},{1,9},{9,1},{17,25},{25,17},{2,10},{10... | collective-permute-start | bytes 98312 | tf_op jit(solution)/shard_map/ppermute | solution.py:214
  14.9 4.3 %collective-permute-start.3 = (f32[4,32,128]{2,1,0:T(8,128)S(1)}, f32[4,32,128]{2,1,0:T(8,128)S(1)}, u32[]{:S(2)}, u32[]{:S(2)}) collective-permute-start(f32[4,32,128]{2,1,0:T(8,128)S(1)} %pad_maximum_fusion.1), channel_id=1, source_target_pairs={{0,1},{1,0},{2,3},{3,2},{4,5},{5,4},{6,7},{7,6},{8,9},{9,8},{10,11... | collective-permute-start | bytes 196616 | tf_op jit(solution)/shard_map/ppermute | solution.py:214
  19.2 5.0 %collective-permute-start.4 = (f32[8,32,128]{2,1,0:T(8,128)S(1)}, f32[8,32,128]{2,1,0:T(8,128)S(1)}, u32[]{:S(2)}, u32[]{:S(2)}) collective-permute-start(f32[8,32,128]{2,1,0:T(8,128)S(1)} %pad_maximum_fusion), channel_id=1, source_target_pairs={{0,4},{2,6},{4,0},{6,2},{1,5},{3,7},{5,1},{7,3},{8,12},{10,14},{12... | collective-permute-start | bytes 393224 | tf_op jit(solution)/shard_map/ppermute | solution.py:214
  19.8 5.4 %copy-start.3 = (f32[40,8,128]{2,1,0:T(8,128)}, f32[40,8,128]{2,1,0:T(8,128)S(1)}, u32[]{:S(2)}) copy-start(f32[40,8,128]{2,1,0:T(8,128)S(1)} %collective-permute-done) | copy-start | bytes 491524
  24.3 6.3 %collective-permute-start.5 = (f32[16,32,128]{2,1,0:T(8,128)S(1)}, f32[16,32,128]{2,1,0:T(8,128)S(1)}, u32[]{:S(2)}, u32[]{:S(2)}) collective-permute-start(f32[16,32,128]{2,1,0:T(8,128)S(1)} %get-tuple-element.14), channel_id=1, source_target_pairs={{0,2},{2,0},{4,6},{6,4},{1,3},{3,1},{5,7},{7,5},{8,10},{10,8},{12,... | collective-permute-start | bytes 786440 | tf_op jit(solution)/shard_map/ppermute | solution.py:214
  30.6 0.8 copy-start.1
  48.9 2.2 %collective-permute-start.6 = (f32[2,12,40,128]{3,2,1,0:T(8,128)}, f32[2,12,40,128]{3,2,1,0:T(8,128)S(1)}, u32[]{:S(2)}, u32[]{:S(2)}) collective-permute-start(f32[2,12,40,128]{3,2,1,0:T(8,128)} %get-tuple-element.11), channel_id=1, source_target_pairs={{0,2},{2,0},{4,6},{6,4},{1,3},{3,1},{5,7},{7,5},{8,10},{10,8},{12,... | collective-permute-start | bytes 1474568 | tf_op jit(solution)/shard_map/ppermute | solution.py:262
  51.1 0.8 copy-start.2

commit v2 on v1

--- a/solution.py
+++ b/solution.py
@@ -49,19 +49,34 @@
     return [1 << b for b in range(size.bit_length() - 1)]
 
 
-def cell_prep_kernel(own_ref, other_ref, feature_ref, coord_ref, *, rows, slots):
+def cell_prep_kernel(*refs, rows, slots, terms, sizes, masks):
+    sources, (feature_ref, coord_ref, place_ref) = refs[:slots], refs[slots:]
+    n_inst, n_cell = sizes["inst"], sizes["cell"]
+    device = (lax.axis_index("blade") * n_inst + lax.axis_index("inst")) * n_cell + lax.axis_index("cell")
+    row_id = lax.broadcasted_iota(jnp.int32, (8, TILE), 0)
+    diagonal = lax.broadcasted_iota(jnp.int32, (TILE, TILE), 0) == lax.broadcasted_iota(jnp.int32, (TILE, TILE), 1)
+    identity = jnp.where(diagonal, 1.0, 0.0).astype(BF16)
     for slot in range(slots):
-        source = own_ref if slot == 0 else other_ref.at[slot - 1]
+        source = sources[slot]
 
         def one_row(r, carry):
             value = source[r]
+            coord_ref[slot, pl.ds(r, 8, stride=rows), :] = value
+            centred = jnp.where(row_id < 3, value - 0.5, 0.0)
+            length = SCALE * jnp.sum(centred * centred, axis=0, keepdims=True)
+            value = jnp.where(row_id == 3, 1.0, jnp.where(row_id == 4, length, centred))
             high, middle, low = split3(value)
-            stacked = jnp.concatenate([high, middle, low, high, middle, high], axis=0)
-            feature_ref[slot, r] = stacked.T.astype(BF16)
-            coord_ref[slot, pl.ds(r, 8, stride=rows), :] = value
+            stacked = jnp.concatenate([high, middle, low, high, middle, high], axis=0).astype(BF16)
+            turned = lax.dot_general(identity, stacked, BOTH_MINOR, preferred_element_type=F32)
+            feature_ref[slot, r] = turned.astype(BF16)
             return carry
 
-        lax.fori_loop(0, rows, one_row, 0, unroll=4)
+        lax.fori_loop(0, rows, one_row, 0, unroll=8)
+        tile = coord_ref[slot, 3 * rows : 4 * rows, :].astype(jnp.int32)
+        if masks is not None:
+            relative = tile ^ device
+            tile = sum((lax.shift_right_logical(relative, m) & 1) << k for k, m in enumerate(masks))
+        place_ref[slot] = tile
 
 
 def sums_kernel(
@@ -70,12 +85,19 @@
 ):
     tiles = block_ref.shape[0]
     combos = 2 * half
+    row_id = lax.broadcasted_iota(jnp.int32, (8, TILE), 0)
+    inst = lax.axis_index("inst")
+    mix = jnp.concatenate([mix_ref[inst], mix_ref[inst ^ 1]], axis=0)
 
     def one_tile(p, carry):
-        high, middle, low = split3(block_ref[p, 3 * NT : 3 * NT + 8, :])
+        value = block_ref[p, 3 * NT : 3 * NT + 8, :]
+        centred = jnp.where(row_id < 3, value - 0.5, 0.0)
+        length = SCALE * jnp.sum(centred * centred, axis=0, keepdims=True)
+        value = jnp.where(row_id == 3, length, jnp.where(row_id == 4, 1.0, (-2.0 * SCALE) * centred))
+        high, middle, low = split3(value)
         centre_ref[p] = jnp.concatenate([high, high, high, middle, middle, low], axis=0).astype(BF16)
         mixed = jnp.dot(
-            mix_ref[...], block_ref[p, : 3 * NT, :],
+            mix, block_ref[p, : 3 * NT, :],
             preferred_element_type=F32, precision=lax.Precision.HIGHEST,
         )
         mixed_high = mixed.astype(BF16).astype(F32)
@@ -85,8 +107,7 @@
     lax.fori_loop(0, tiles, one_tile, 0, unroll=4)
 
     def tile_pair(r, slot, pair):
-        base = (slot * rows + r) * terms + 2 * pair
-        return list_ref[base], list_ref[base + 1]
+        return list_ref[slot, r, 2 * pair], list_ref[slot, r, 2 * pair + 1]
 
     def distances(r, slot, out):
         for pair in range(terms // 2):
@@ -130,7 +151,7 @@
         weights(dist1, weight1)
         return carry
 
-    lax.fori_loop(0, rows, one_row, 0, unroll=2)
+    lax.fori_loop(0, rows, one_row, 0, unroll=4)
     contract(rows - 1, 1, weight1)
 
     shifts = half // 2
@@ -139,28 +160,18 @@
             for c in range(half):
                 value = total_ref[slot, (first + c) * rows : (first + c + 1) * rows, :]
                 if c < shifts:
-                    value = value + (coord_ref[slot, (c % 3) * rows : (c % 3 + 1) * rows, :] + 0.5)
+                    value = value + coord_ref[slot, (c % 3) * rows : (c % 3 + 1) * rows, :]
                 out[slot, c] = value
 
 
-def merge_kernel(place_ref, own_ref, peer_ref, moved_ref, velocity_ref, sems, *, slots, half):
+def merge_kernel(own_ref, peer_ref, moved_ref, velocity_ref, *, slots, half):
     shifts = half // 2
-    copies = []
+    inst = lax.axis_index("inst")
     for which, source in enumerate((own_ref, peer_ref)):
         for slot in range(slots):
-            lane = pl.multiple_of(place_ref[which * slots + slot] * TILE, TILE)
-            for part, out in enumerate((moved_ref, velocity_ref)):
-                copies.append(
-                    pltpu.make_async_copy(
-                        source.at[slot, pl.ds(part * shifts, shifts)],
-                        out.at[:, :, pl.ds(lane, TILE)],
-                        sems.at[len(copies)],
-                    )
-                )
-    for copy in copies:
-        copy.start()
-    for copy in copies:
-        copy.wait()
+            lane = pl.multiple_of((inst ^ which ^ (2 * slot)) * TILE, TILE)
+            moved_ref[:, :, pl.ds(lane, TILE)] = source[slot, :shifts]
+            velocity_ref[:, :, pl.ds(lane, TILE)] = source[slot, shifts:]
 
 
 def vmem():
@@ -169,10 +180,6 @@
 
 def smem():
     return pl.BlockSpec(memory_space=pltpu.SMEM)
-
-
-def hbm():
-    return pl.BlockSpec(memory_space=pl.ANY)
 
 
 def on_device(cell_coords, centre_points, coefficients, tile_lists, *, sizes):
@@ -182,66 +189,47 @@
     width = centre_points.shape[1]
     slots = n_inst // 2
     half = 2 * 3 * (NT // n_inst)
-    inst = lax.axis_index("inst")
-    device = (lax.axis_index("blade") * n_inst + inst) * n_cell + lax.axis_index("cell")
-
-    centred = centre_points - 0.5
-    block = jnp.concatenate(
-        [
-            coefficients,
-            (-2.0 * SCALE) * centred,
-            SCALE * jnp.sum(centred * centred, axis=0, keepdims=True),
-            jnp.ones((1, width), F32),
-            jnp.zeros((3, width), F32),
-        ],
-        axis=0,
-    )
-    cells = cell_coords - 0.5
+    block = jnp.concatenate([coefficients, centre_points, jnp.zeros((5, width), F32)], axis=0)
     list_row = jnp.pad(tile_lists[:, 0, :].astype(F32), ((0, 0), (0, TILE - terms)))
     blank = jnp.zeros_like(list_row)
-    cell_rows = jnp.stack(
-        [cells[0], cells[1], cells[2], blank + 1.0, SCALE * jnp.sum(cells * cells, axis=0), list_row, blank, blank],
-        axis=1,
-    )
+    cell_rows = jnp.stack([cell_coords[0], cell_coords[1], cell_coords[2], list_row] + [blank] * 4, axis=1)
 
     others = [lax.ppermute(cell_rows, "inst", flip(n_inst, 2 * s)) for s in range(1, slots)]
 
     phases = [("blade", n_blade, b, b * n_inst * n_cell) for b in reversed(bits_of(n_blade))]
     phases += [("cell", n_cell, b, b) for b in bits_of(n_cell)]
     phases += [("inst", n_inst, b, b * n_cell) for b in reversed(bits_of(n_inst))]
-    blocks = block[None]
-    for axis, size, bit, _ in phases:
-        blocks = jnp.concatenate([blocks, lax.ppermute(blocks, axis, flip(size, bit))], axis=0)
-
-    def position(index):
-        relative = index ^ device
-        return sum(((relative // mask) & 1) << k for k, (_, _, _, mask) in enumerate(phases))
-
-    lists = jnp.stack(
-        [tile_lists[:, 0, :]] + [o[:, 5, :terms].astype(jnp.int32) for o in others], axis=0
-    )
-    if width == TILE:
-        lists = position(lists)
-    else:
-        per_tile = TILE // width
-        blocks = jnp.take(blocks, position(jnp.arange(blocks.shape[0])), axis=0)
-        blocks = blocks.reshape(-1, per_tile, 3 * NT + 8, width)
-        blocks = jnp.moveaxis(blocks, 1, 2).reshape(-1, 3 * NT + 8, TILE)
-    n_tiles = blocks.shape[0]
-
-    features, coords = pl.pallas_call(
-        functools.partial(cell_prep_kernel, rows=rows, slots=slots),
+    masks = [mask.bit_length() - 1 for _, _, _, mask in phases]
+
+    features, coords, places = pl.pallas_call(
+        functools.partial(
+            cell_prep_kernel, rows=rows, slots=slots, terms=terms, sizes=sizes,
+            masks=masks if width == TILE else None,
+        ),
         out_shape=(
             jax.ShapeDtypeStruct((slots, rows, TILE, FEATURES), BF16),
             jax.ShapeDtypeStruct((slots, 8 * rows, TILE), F32),
+            jax.ShapeDtypeStruct((slots, rows, TILE), jnp.int32),
         ),
-        in_specs=[vmem(), vmem()],
-        out_specs=(vmem(), vmem()),
+        in_specs=[vmem()] * slots,
+        out_specs=(vmem(),) * 3,
         name="cell_prep",
-    )(cell_rows, jnp.stack(others))
-
-    mix_all = jnp.asarray(spectral_rows(NT, n_inst))
-    mix = jnp.concatenate([mix_all[inst], mix_all[inst ^ 1]], axis=0)
+    )(cell_rows, *others)
+
+    blocks = block[None]
+    for index, (axis, size, bit, _) in enumerate(phases):
+        arrived = lax.ppermute(blocks, axis, flip(size, bit))
+        if index == len(phases) - 2:
+            arrived, features, coords, places = lax.optimization_barrier((arrived, features, coords, places))
+        blocks = jnp.concatenate([blocks, arrived], axis=0)
+    if width < TILE:
+        device = (lax.axis_index("blade") * n_inst + lax.axis_index("inst")) * n_cell + lax.axis_index("cell")
+        relative = jnp.arange(blocks.shape[0]) ^ device
+        order = sum(((relative >> m) & 1) << k for k, m in enumerate(masks))
+        blocks = jnp.take(blocks, order, axis=0).reshape(-1, TILE // width, 3 * NT + 8, width)
+        blocks = jnp.moveaxis(blocks, 1, 2).reshape(-1, 3 * NT + 8, TILE)
+    n_tiles = blocks.shape[0]
+
     own, peer = pl.pallas_call(
         functools.partial(sums_kernel, rows=rows, slots=slots, terms=terms, half=half),
         out_shape=(jax.ShapeDtypeStruct((slots, half, rows, TILE), F32),) * 2,
@@ -257,20 +245,17 @@
             pltpu.VMEM((terms // 2, 2 * TILE, 2 * TILE), BF16),
         ],
         name="rbf_sums",
-    )(lists.reshape(-1), mix, blocks, features, coords)
+    )(places, jnp.asarray(spectral_rows(NT, n_inst)), blocks, features, coords)
 
     received = lax.ppermute(peer, "inst", flip(n_inst, 1))
-    slot_bits = 2 * jnp.arange(slots, dtype=jnp.int32)
-    places = jnp.concatenate([inst ^ slot_bits, inst ^ 1 ^ slot_bits])
     out = jax.ShapeDtypeStruct((half // 2, rows, n_inst * TILE), F32)
     moved, velocity = pl.pallas_call(
         functools.partial(merge_kernel, slots=slots, half=half),
         out_shape=(out, out),
-        in_specs=[smem(), hbm(), hbm()],
-        out_specs=(hbm(), hbm()),
-        scratch_shapes=[pltpu.SemaphoreType.DMA((4 * slots,))],
+        in_specs=[vmem(), vmem()],
+        out_specs=(vmem(), vmem()),
         name="merge",
-    )(places, own, received)
+    )(own, received)
     shape = (NT // n_inst, 3, rows, n_inst * TILE)
     return (moved.reshape(shape), velocity.reshape(shape))
 

time: 83.9 us -> 47.7 us (0.57)
  Pallas kernels: 53.8 us -> 23.6 us
  waiting for transfers between devices: 10.5 us -> 7.75 us
  other arithmetic: 4.07 us -> 1.61 us
    pallas_call x1, Pallas kernels: 31.6 us -> 2.24 us  [on_device(): pl.pallas_call(functools.partial(merge_kernel, slots=slots, half=half), o...]
    ppermute x5, waiting for transfers between devices: 9.37 us -> 5.81 us  [on_device(): arrived = lax.ppermute(blocks, axis, flip(size, bit))]
    reduce_sum x2 -> x0, other arithmetic: 1.54 us -> none  [the longest x1 0.84 us: on_device(): jnp.sum(cells * cells, axis=0)]
    concatenate x5 -> x3, other arithmetic: 1.18 us -> 0.02 us  [on_device(): blocks = jnp.concatenate([blocks, arrived], axis=0)]
    pallas_call x1, Pallas kernels: 17.5 us -> 16.6 us  [on_device(): pl.pallas_call(functools.partial(sums_kernel, rows=rows, slots=slots, ter...]
    unnamed x13 -> x12, local copies, waits for them, and re-layouts: 2.38 us -> 3.02 us
  transfers between devices with their start and end apart: 7 -> 7, of which waited for: 4 -> 4; matrix products, arithmetic and copies ran while one was open for 6% -> 5% of each run, Pallas kernels for 6% -> 10%
where the time goes in v2:
time: 47.7 us; the launch traced here: 47.3 us
  Pallas kernels  23.6 us (49%)
  starting transfers between devices  9.53 us (20%)
  waiting for transfers between devices  7.75 us (16%)
  local copies, waits for them, and re-layouts  4.08 us (9%)
  other arithmetic  1.61 us (3%)
  between operations  0.74 us (2%)
    pallas_call x1, Pallas kernels, on_device(): pl.pallas_call(functools.partial(sums_kernel, rows=rows, slots=slots, ter...  16.6 us
    ppermute x5, starting transfers between devices, on_device(): arrived = lax.ppermute(blocks, axis, flip(size, bit))  7.83 us
    ppermute x5, waiting for transfers between devices, on_device(): arrived = lax.ppermute(blocks, axis, flip(size, bit))  5.81 us
    pallas_call x1, Pallas kernels, on_device(): pl.pallas_call(functools.partial(cell_prep_kernel, rows=rows, slots=slots...  4.78 us
    unnamed x12, local copies, waits for them, and re-layouts  3.02 us
    pallas_call x1, Pallas kernels, on_device(): pl.pallas_call(functools.partial(merge_kernel, slots=slots, half=half), o...  2.24 us
    ppermute x1, waiting for transfers between devices, on_device(): received = lax.ppermute(peer, 'inst', flip(n_inst, 1))  1.93 us
    ppermute x1, starting transfers between devices, on_device(): lax.ppermute(cell_rows, 'inst', flip(n_inst, 2 * s))  1.56 us
  transfers between devices with their start and end apart: 7, of which 4 were waited for; matrix products, arithmetic and copies ran while one was open for 5% of the time, Pallas kernels for 10%

profile of v2, /device:TPU:0, one launch (start us, length us, event | category | flops | bytes accessed | tf_op | source)
XLA Modules:
  0.0 47.3 jit_solution(1017158591635731372)
XLA Ops:
  0.6 0.1 pad.16.clone
  0.7 0.8 %maximum_bitcast_fusion = f32[1,32,128]{2,1,0:T(8,128)S(1)} fusion(f32[3,128]{1,0:T(4,128)} %param.6, f32[24,128]{1,0:T(8,128)} %param.7, f32[32]{0:T(128)S(1)} %pad.16.clone), kind=kLoop, calls=%fused_computation.15 | loop fusion | flops 8192 | bytes 30336 | tf_op jit(solution)/shard_map/broadcast_in_dim | solution.py:219
  1.5 4.1 %collective-permute-start = (f32[1,32,128]{2,1,0:T(8,128)S(1)}, f32[1,32,128]{2,1,0:T(8,128)S(1)}, u32[]{:S(2)}, u32[]{:S(2)}) collective-permute-start(f32[1,32,128]{2,1,0:T(8,128)S(1)} %maximum_bitcast_fusion), channel_id=1, source_target_pairs={{0,16},{8,24},{16,0},{24,8},{1,17},{9,25},{17,1},{25,9},{2,18},{10... | collective-permute-start | bytes 49160 | tf_op jit(solution)/shard_map/ppermute | solution.py:221
  5.6 0.8 %copy.7 = s32[40,1,4]{2,0,1:T(8,128)S(1)} copy(s32[40,1,4]{0,2,1:T(4,128)} %param.8) | data formatting | bytes 1280 | tf_op args[3]
  6.3 0.8 %fusion = (f32[1,40,128]{2,1,0:T(8,128)S(1)}, f32[1,40,128]{2,1,0:T(8,128)S(1)}, f32[1,40,128]{2,1,0:T(8,128)S(1)}) fusion(f32[3,40,128]{2,1,0:T(8,128)} %param.5), kind=kLoop, calls=%fused_computation.16 | loop fusion | bytes 122880 | tf_op jit(solution)/shard_map/slice | solution.py:195
  7.1 0.2 stack.11.refs_0_
  7.3 0.0 copy-start
  7.3 1.6 %collective-permute-start.4 = (f32[40,8,128]{2,1,0:T(8,128)S(1)}, f32[40,8,128]{2,1,0:T(8,128)S(1)}, u32[]{:S(2)}, u32[]{:S(2)}) collective-permute-start(f32[40,8,128]{2,1,0:T(8,128)S(1)} %stack.11.refs_0_), channel_id=1, source_target_pairs={{0,4},{2,6},{4,0},{6,2},{1,5},{3,7},{5,1},{7,3},{8,12},{10,14},{12... | collective-permute-start | bytes 491528 | tf_op jit(solution)/shard_map/ppermute | solution.py:197
  8.9 0.0 collective-permute-done
  8.9 1.6 %collective-permute-start.1 = (f32[2,32,128]{2,1,0:T(8,128)S(1)}, f32[2,32,128]{2,1,0:T(8,128)S(1)}, u32[]{:S(2)}, u32[]{:S(2)}) collective-permute-start(f32[2,32,128]{2,1,0:T(8,128)S(1)} %pad_maximum_fusion.2), channel_id=1, source_target_pairs={{0,8},{8,0},{16,24},{24,16},{1,9},{9,1},{17,25},{25,17},{2,10},{10... | collective-permute-start | bytes 98312 | tf_op jit(solution)/shard_map/ppermute | solution.py:221
  10.5 0.8 %constant_dynamic-update-slice_fusion.4 = (f32[16,32,128]{2,1,0:T(8,128)S(1)}, f32[32,32,128]{2,1,0:T(8,128)S(1)}) fusion(f32[32]{0:T(128)S(1)} %pad.16.clone, f32[3,128]{1,0:T(4,128)} %param.6, f32[24,128]{1,0:T(8,128)} %param.7), kind=kLoop, calls=%fused_computation.7 | loop fusion | flops 8190 | bytes 46720
  11.3 1.5 %collective-permute-done.1 = f32[2,32,128]{2,1,0:T(8,128)S(1)} collective-permute-done((f32[2,32,128]{2,1,0:T(8,128)S(1)}, f32[2,32,128]{2,1,0:T(8,128)S(1)}, u32[]{:S(2)}, u32[]{:S(2)}) %collective-permute-start.1) | collective-permute-done | bytes 32800 | tf_op jit(solution)/shard_map/ppermute | solution.py:221
  12.8 1.5 %collective-permute-start.2 = (f32[4,32,128]{2,1,0:T(8,128)S(1)}, f32[4,32,128]{2,1,0:T(8,128)S(1)}, u32[]{:S(2)}, u32[]{:S(2)}) collective-permute-start(f32[4,32,128]{2,1,0:T(8,128)S(1)} %pad_maximum_fusion.1), channel_id=1, source_target_pairs={{0,1},{1,0},{2,3},{3,2},{4,5},{5,4},{6,7},{7,6},{8,9},{9,8},{10,11... | collective-permute-start | bytes 196616 | tf_op jit(solution)/shard_map/ppermute | solution.py:221
  14.3 2.7 %collective-permute-done.2 = f32[4,32,128]{2,1,0:T(8,128)S(1)} collective-permute-done((f32[4,32,128]{2,1,0:T(8,128)S(1)}, f32[4,32,128]{2,1,0:T(8,128)S(1)}, u32[]{:S(2)}, u32[]{:S(2)}) %collective-permute-start.2) | collective-permute-done | bytes 65568 | tf_op jit(solution)/shard_map/ppermute | solution.py:221
  17.1 0.6 %collective-permute-start.3 = (f32[8,32,128]{2,1,0:T(8,128)S(1)}, f32[8,32,128]{2,1,0:T(8,128)S(1)}, u32[]{:S(2)}, u32[]{:S(2)}) collective-permute-start(f32[8,32,128]{2,1,0:T(8,128)S(1)} %pad_maximum_fusion), channel_id=1, source_target_pairs={{0,4},{2,6},{4,0},{6,2},{1,5},{3,7},{5,1},{7,3},{8,12},{10,14},{12... | collective-permute-start | bytes 393224 | tf_op jit(solution)/shard_map/ppermute | solution.py:221
  17.7 0.0 collective-permute-done.4.refs_1_
  17.7 0.0 copy-done
  17.7 0.0 copy-start.3
  17.7 0.7 %copy-done.3 = f32[40,8,128]{2,1,0:T(8,128)} copy-done((f32[40,8,128]{2,1,0:T(8,128)}, f32[40,8,128]{2,1,0:T(8,128)S(1)}, u32[]{:S(2)}) %copy-start.3) | copy-done | bytes 163864
  18.4 4.8 %cell_prep.1 = (bf16[2,40,128,48]{3,2,1,0:T(8,128)(2,1)}, f32[2,320,128]{2,1,0:T(8,128)}, s32[2,40,128]{2,1,0:T(8,128)}) custom-call(f32[40,8,128]{2,1,0:T(8,128)} %copy-done, f32[40,8,128]{2,1,0:T(8,128)} %copy-done.3), custom_call_target="tpu_custom_call" | custom-call | tf_op jit(solution)/shard_map/cell_prep/pallas_call | solution.py:204
  23.2 0.0 collective-permute-done.3
  23.2 0.1 collective-permute-start.5
  23.3 1.5 %collective-permute-done.5 = f32[16,32,128]{2,1,0:T(8,128)S(1)} collective-permute-done((f32[16,32,128]{2,1,0:T(8,128)S(1)}, f32[16,32,128]{2,1,0:T(8,128)S(1)}, u32[]{:S(2)}, u32[]{:S(2)}) %collective-permute-start.5) | collective-permute-done | bytes 262176 | tf_op jit(solution)/shard_map/ppermute | solution.py:221
  24.8 0.0 copy-start.1
  24.8 0.8 %copy-done.1 = f32[32,32,128]{2,1,0:T(8,128)} copy-done((f32[32,32,128]{2,1,0:T(8,128)}, f32[32,32,128]{2,1,0:T(8,128)S(1)}, u32[]{:S(2)}) %copy-start.1) | copy-done | bytes 524312
  25.6 16.6 %rbf_sums.1 = (f32[2,12,40,128]{3,2,1,0:T(8,128)}, f32[2,12,40,128]{3,2,1,0:T(8,128)}) custom-call(s32[2,40,128]{2,1,0:T(8,128)} %get-tuple-element.16.list_ref, f32[4,12,24]{2,1,0:T(8,128)} %constant.3.clone.mix_ref, f32[32,32,128]{2,1,0:T(8,128)} %copy-done.1, bf16[2,40,128,48]{3,2,1,0:T(8,128)(2,1)} %get-tuple-element.18.feature_ref, ...), custom_call_target="tpu_custom_call" | custom-call | tf_op jit(solution)/shard_map/rbf_sums/pallas_call | solution.py:233
  42.2 0.1 collective-permute-start.6
  42.4 1.9 %collective-permute-done.6.peer_ref = f32[2,12,40,128]{3,2,1,0:T(8,128)S(1)} collective-permute-done((f32[2,12,40,128]{3,2,1,0:T(8,128)}, f32[2,12,40,128]{3,2,1,0:T(8,128)S(1)}, u32[]{:S(2)}, u32[]{:S(2)}) %collective-permute-start.6) | collective-permute-done | bytes 491552 | tf_op jit(solution)/shard_map/ppermute | solution.py:250
  44.3 0.0 copy-start.2
  44.3 0.8 %copy-done.2 = f32[2,12,40,128]{3,2,1,0:T(8,128)} copy-done((f32[2,12,40,128]{3,2,1,0:T(8,128)}, f32[2,12,40,128]{3,2,1,0:T(8,128)S(1)}, u32[]{:S(2)}) %copy-start.2) | copy-done | bytes 491544
  45.1 2.2 %merge.1 = (f32[6,40,512]{2,1,0:T(8,128)}, f32[6,40,512]{2,1,0:T(8,128)}) custom-call(f32[2,12,40,128]{3,2,1,0:T(8,128)} %get-tuple-element.20.own_ref, f32[2,12,40,128]{3,2,1,0:T(8,128)} %copy-done.2), custom_call_target="tpu_custom_call" | custom-call | tf_op jit(solution)/shard_map/merge/pallas_call | solution.py:252
  (12 shorter events, 0.1 us)
Async XLA Ops:
  1.5 7.4 %collective-permute-start = (f32[1,32,128]{2,1,0:T(8,128)S(1)}, f32[1,32,128]{2,1,0:T(8,128)S(1)}, u32[]{:S(2)}, u32[]{:S(2)}) collective-permute-start(f32[1,32,128]{2,1,0:T(8,128)S(1)} %maximum_bitcast_fusion), channel_id=1, source_target_pairs={{0,16},{8,24},{16,0},{24,8},{1,17},{9,25},{17,1},{25,9},{2,18},{10... | collective-permute-start | bytes 49160 | tf_op jit(solution)/shard_map/ppermute | solution.py:221
  7.3 10.4 %copy-start = (f32[40,8,128]{2,1,0:T(8,128)}, f32[40,8,128]{2,1,0:T(8,128)S(1)}, u32[]{:S(2)}) copy-start(f32[40,8,128]{2,1,0:T(8,128)S(1)} %stack.11.refs_0_) | copy-start | bytes 491524
  7.3 10.4 %collective-permute-start.4 = (f32[40,8,128]{2,1,0:T(8,128)S(1)}, f32[40,8,128]{2,1,0:T(8,128)S(1)}, u32[]{:S(2)}, u32[]{:S(2)}) collective-permute-start(f32[40,8,128]{2,1,0:T(8,128)S(1)} %stack.11.refs_0_), channel_id=1, source_target_pairs={{0,4},{2,6},{4,0},{6,2},{1,5},{3,7},{5,1},{7,3},{8,12},{10,14},{12... | collective-permute-start | bytes 491528 | tf_op jit(solution)/shard_map/ppermute | solution.py:197
  8.9 3.9 %collective-permute-start.1 = (f32[2,32,128]{2,1,0:T(8,128)S(1)}, f32[2,32,128]{2,1,0:T(8,128)S(1)}, u32[]{:S(2)}, u32[]{:S(2)}) collective-permute-start(f32[2,32,128]{2,1,0:T(8,128)S(1)} %pad_maximum_fusion.2), channel_id=1, source_target_pairs={{0,8},{8,0},{16,24},{24,16},{1,9},{9,1},{17,25},{25,17},{2,10},{10... | collective-permute-start | bytes 98312 | tf_op jit(solution)/shard_map/ppermute | solution.py:221
  12.8 4.3 %collective-permute-start.2 = (f32[4,32,128]{2,1,0:T(8,128)S(1)}, f32[4,32,128]{2,1,0:T(8,128)S(1)}, u32[]{:S(2)}, u32[]{:S(2)}) collective-permute-start(f32[4,32,128]{2,1,0:T(8,128)S(1)} %pad_maximum_fusion.1), channel_id=1, source_target_pairs={{0,1},{1,0},{2,3},{3,2},{4,5},{5,4},{6,7},{7,6},{8,9},{9,8},{10,11... | collective-permute-start | bytes 196616 | tf_op jit(solution)/shard_map/ppermute | solution.py:221
  17.1 6.1 %collective-permute-start.3 = (f32[8,32,128]{2,1,0:T(8,128)S(1)}, f32[8,32,128]{2,1,0:T(8,128)S(1)}, u32[]{:S(2)}, u32[]{:S(2)}) collective-permute-start(f32[8,32,128]{2,1,0:T(8,128)S(1)} %pad_maximum_fusion), channel_id=1, source_target_pairs={{0,4},{2,6},{4,0},{6,2},{1,5},{3,7},{5,1},{7,3},{8,12},{10,14},{12... | collective-permute-start | bytes 393224 | tf_op jit(solution)/shard_map/ppermute | solution.py:221
  17.7 0.7 %copy-start.3 = (f32[40,8,128]{2,1,0:T(8,128)}, f32[40,8,128]{2,1,0:T(8,128)S(1)}, u32[]{:S(2)}) copy-start(f32[40,8,128]{2,1,0:T(8,128)S(1)} %collective-permute-done.4.refs_1_) | copy-start | bytes 491524
  23.2 1.6 %collective-permute-start.5 = (f32[16,32,128]{2,1,0:T(8,128)S(1)}, f32[16,32,128]{2,1,0:T(8,128)S(1)}, u32[]{:S(2)}, u32[]{:S(2)}) collective-permute-start(f32[16,32,128]{2,1,0:T(8,128)S(1)} %get-tuple-element.24), channel_id=1, source_target_pairs={{0,2},{2,0},{4,6},{6,4},{1,3},{3,1},{5,7},{7,5},{8,10},{10,8},{12,... | collective-permute-start | bytes 786440 | tf_op jit(solution)/shard_map/ppermute | solution.py:221
  24.8 0.8 %copy-start.1 = (f32[32,32,128]{2,1,0:T(8,128)}, f32[32,32,128]{2,1,0:T(8,128)S(1)}, u32[]{:S(2)}) copy-start(f32[32,32,128]{2,1,0:T(8,128)S(1)} %constant_dynamic-update-slice_fusion.5.block_ref) | copy-start | bytes 1572868
  42.2 2.1 %collective-permute-start.6 = (f32[2,12,40,128]{3,2,1,0:T(8,128)}, f32[2,12,40,128]{3,2,1,0:T(8,128)S(1)}, u32[]{:S(2)}, u32[]{:S(2)}) collective-permute-start(f32[2,12,40,128]{3,2,1,0:T(8,128)} %get-tuple-element.21), channel_id=1, source_target_pairs={{0,2},{2,0},{4,6},{6,4},{1,3},{3,1},{5,7},{7,5},{8,10},{10,8},{12,... | collective-permute-start | bytes 1474568 | tf_op jit(solution)/shard_map/ppermute | solution.py:250
  44.3 0.8 %copy-start.2 = (f32[2,12,40,128]{3,2,1,0:T(8,128)}, f32[2,12,40,128]{3,2,1,0:T(8,128)S(1)}, u32[]{:S(2)}) copy-start(f32[2,12,40,128]{3,2,1,0:T(8,128)S(1)} %collective-permute-done.6.peer_ref) | copy-start | bytes 1474564

commit v3 on v2

--- a/solution.py
+++ b/solution.py
@@ -14,6 +14,7 @@
 EDGE = 4.0**0.2
 SCALE = (EDGE / RADIUS) ** 2
 FEATURES = 48
+VMEM_LIMIT = 16 * 1024 * 1024
 BOTH_MINOR = (((1,), (1,)), ((), ()))
 F32 = jnp.float32
 BF16 = jnp.bfloat16
@@ -174,6 +175,10 @@
             velocity_ref[:, :, pl.ds(lane, TILE)] = source[slot, shifts:]
 
 
+def in_vmem(value):
+    return pltpu.with_memory_space_constraint(value, pltpu.VMEM)
+
+
 def vmem():
     return pl.BlockSpec(memory_space=pltpu.VMEM)
 
@@ -207,14 +212,15 @@
             masks=masks if width == TILE else None,
         ),
         out_shape=(
-            jax.ShapeDtypeStruct((slots, rows, TILE, FEATURES), BF16),
-            jax.ShapeDtypeStruct((slots, 8 * rows, TILE), F32),
+            pltpu.VMEM((slots, rows, TILE, FEATURES), BF16),
+            pltpu.VMEM((slots, 8 * rows, TILE), F32),
             jax.ShapeDtypeStruct((slots, rows, TILE), jnp.int32),
         ),
         in_specs=[vmem()] * slots,
         out_specs=(vmem(),) * 3,
+        compiler_params=pltpu.CompilerParams(vmem_limit_bytes=VMEM_LIMIT),
         name="cell_prep",
-    )(cell_rows, *others)
+    )(in_vmem(cell_rows), *map(in_vmem, others))
 
     blocks = block[None]
     for index, (axis, size, bit, _) in enumerate(phases):
@@ -232,7 +238,7 @@
 
     own, peer = pl.pallas_call(
         functools.partial(sums_kernel, rows=rows, slots=slots, terms=terms, half=half),
-        out_shape=(jax.ShapeDtypeStruct((slots, half, rows, TILE), F32),) * 2,
+        out_shape=(pltpu.VMEM((slots, half, rows, TILE), F32),) * 2,
         in_specs=[smem(), vmem(), vmem(), vmem(), vmem()],
         out_specs=(vmem(), vmem()),
         scratch_shapes=[
@@ -244,8 +250,9 @@
             pltpu.VMEM((terms // 2, 2 * TILE, 2 * TILE), BF16),
             pltpu.VMEM((terms // 2, 2 * TILE, 2 * TILE), BF16),
         ],
+        compiler_params=pltpu.CompilerParams(vmem_limit_bytes=VMEM_LIMIT),
         name="rbf_sums",
-    )(places, jnp.asarray(spectral_rows(NT, n_inst)), blocks, features, coords)
+    )(places, jnp.asarray(spectral_rows(NT, n_inst)), in_vmem(blocks), in_vmem(features), in_vmem(coords))
 
     received = lax.ppermute(peer, "inst", flip(n_inst, 1))
     out = jax.ShapeDtypeStruct((half // 2, rows, n_inst * TILE), F32)
@@ -254,8 +261,9 @@
         out_shape=(out, out),
         in_specs=[vmem(), vmem()],
         out_specs=(vmem(), vmem()),
+        compiler_params=pltpu.CompilerParams(vmem_limit_bytes=VMEM_LIMIT),
         name="merge",
-    )(own, received)
+    )(in_vmem(own), in_vmem(received))
     shape = (NT // n_inst, 3, rows, n_inst * TILE)
     return (moved.reshape(shape), velocity.reshape(shape))
 

time: 47.7 us -> 42 us (0.88)
  Pallas kernels: 23.6 us -> 18.3 us
  local copies, waits for them, and re-layouts: 4.08 us -> 1.85 us
  waiting for transfers between devices: 7.75 us -> 9.63 us
    pallas_call x1, Pallas kernels: 4.78 us -> 2.3 us  [on_device(): pl.pallas_call(functools.partial(cell_prep_kernel, rows=rows, slots=slots...]
    unnamed x12 -> x6, local copies, waits for them, and re-layouts: 3.02 us -> 0.79 us
    ppermute x5, waiting for transfers between devices: 5.81 us -> 7.9 us  [on_device(): arrived = lax.ppermute(blocks, axis, flip(size, bit))]
    pallas_call x1, Pallas kernels: 16.6 us -> 14.9 us  [on_device(): pl.pallas_call(functools.partial(sums_kernel, rows=rows, slots=slots, ter...]
    pallas_call x1, Pallas kernels: 2.24 us -> 1.07 us  [on_device(): pl.pallas_call(functools.partial(merge_kernel, slots=slots, half=half), o...]
  transfers between devices with their start and end apart: 7 -> 7, of which waited for: 4 -> 5; matrix products, arithmetic and copies ran while one was open for 5% -> 6% of each run, Pallas kernels for 10% -> 6%
where the time goes in v3:
time: 42 us; the launch traced here: 41.7 us
  Pallas kernels  18.3 us (44%)
  waiting for transfers between devices  9.63 us (23%)
  starting transfers between devices  9.59 us (23%)
  local copies, waits for them, and re-layouts  1.85 us (4%)
  other arithmetic  1.61 us (4%)
  between operations  0.73 us (2%)
    pallas_call x1, Pallas kernels, on_device(): pl.pallas_call(functools.partial(sums_kernel, rows=rows, slots=slots, ter...  14.9 us
    ppermute x5, waiting for transfers between devices, on_device(): arrived = lax.ppermute(blocks, axis, flip(size, bit))  7.9 us
    ppermute x5, starting transfers between devices, on_device(): arrived = lax.ppermute(blocks, axis, flip(size, bit))  7.83 us
    pallas_call x1, Pallas kernels, on_device(): pl.pallas_call(functools.partial(cell_prep_kernel, rows=rows, slots=slots...  2.3 us
    ppermute x1, waiting for transfers between devices, on_device(): received = lax.ppermute(peer, 'inst', flip(n_inst, 1))  1.72 us
    ppermute x1, starting transfers between devices, on_device(): lax.ppermute(cell_rows, 'inst', flip(n_inst, 2 * s))  1.56 us
    pallas_call x1, Pallas kernels, on_device(): pl.pallas_call(functools.partial(merge_kernel, slots=slots, half=half), o...  1.07 us
  transfers between devices with their start and end apart: 7, of which 5 were waited for; matrix products, arithmetic and copies ran while one was open for 6% of the time, Pallas kernels for 6%

profile of v3, /device:TPU:0, one launch (start us, length us, event | category | flops | bytes accessed | tf_op | source)
XLA Modules:
  0.0 41.7 jit_solution(10447583562712883896)
XLA Ops:
  0.6 0.0 copy-start
  0.7 0.1 pad.16.clone
  0.7 0.8 %maximum_bitcast_fusion = f32[1,32,128]{2,1,0:T(8,128)S(1)} fusion(f32[3,128]{1,0:T(4,128)} %param.6, f32[24,128]{1,0:T(8,128)} %param.7, f32[32]{0:T(128)S(1)} %pad.16.clone), kind=kLoop, calls=%fused_computation.15 | loop fusion | flops 8192 | bytes 30336 | tf_op jit(solution)/shard_map/broadcast_in_dim | solution.py:225
  1.5 4.1 %collective-permute-start = (f32[1,32,128]{2,1,0:T(8,128)S(1)}, f32[1,32,128]{2,1,0:T(8,128)S(1)}, u32[]{:S(2)}, u32[]{:S(2)}) collective-permute-start(f32[1,32,128]{2,1,0:T(8,128)S(1)} %maximum_bitcast_fusion), channel_id=1, source_target_pairs={{0,16},{8,24},{16,0},{24,8},{1,17},{9,25},{17,1},{25,9},{2,18},{10... | collective-permute-start | bytes 49160 | tf_op jit(solution)/shard_map/ppermute | solution.py:227
  5.6 0.8 %copy.7 = s32[40,1,4]{2,0,1:T(8,128)S(1)} copy(s32[40,1,4]{0,2,1:T(4,128)} %param.8) | data formatting | bytes 1280 | tf_op args[3]
  6.4 0.8 %fusion = (f32[1,40,128]{2,1,0:T(8,128)S(1)}, f32[1,40,128]{2,1,0:T(8,128)S(1)}, f32[1,40,128]{2,1,0:T(8,128)S(1)}) fusion(f32[3,40,128]{2,1,0:T(8,128)} %param.5), kind=kLoop, calls=%fused_computation.16 | loop fusion | bytes 122880 | tf_op jit(solution)/shard_map/slice | solution.py:200
  7.2 0.2 stack.11.refs_0_
  7.3 1.6 %collective-permute-start.4 = (f32[40,8,128]{2,1,0:T(8,128)S(1)}, f32[40,8,128]{2,1,0:T(8,128)S(1)}, u32[]{:S(2)}, u32[]{:S(2)}) collective-permute-start(f32[40,8,128]{2,1,0:T(8,128)S(1)} %stack.11.refs_0_), channel_id=1, source_target_pairs={{0,4},{2,6},{4,0},{6,2},{1,5},{3,7},{5,1},{7,3},{8,12},{10,14},{12... | collective-permute-start | bytes 491528 | tf_op jit(solution)/shard_map/ppermute | solution.py:202
  8.9 0.0 collective-permute-done
  8.9 1.6 %collective-permute-start.1 = (f32[2,32,128]{2,1,0:T(8,128)S(1)}, f32[2,32,128]{2,1,0:T(8,128)S(1)}, u32[]{:S(2)}, u32[]{:S(2)}) collective-permute-start(f32[2,32,128]{2,1,0:T(8,128)S(1)} %pad_maximum_fusion.2), channel_id=1, source_target_pairs={{0,8},{8,0},{16,24},{24,16},{1,9},{9,1},{17,25},{25,17},{2,10},{10... | collective-permute-start | bytes 98312 | tf_op jit(solution)/shard_map/ppermute | solution.py:227
  10.5 0.8 %constant_dynamic-update-slice_fusion.4 = (f32[16,32,128]{2,1,0:T(8,128)S(1)}, f32[32,32,128]{2,1,0:T(8,128)S(1)}) fusion(f32[32]{0:T(128)S(1)} %pad.16.clone, f32[3,128]{1,0:T(4,128)} %param.6, f32[24,128]{1,0:T(8,128)} %param.7), kind=kLoop, calls=%fused_computation.7 | loop fusion | flops 8190 | bytes 46720
  11.3 1.5 %collective-permute-done.1 = f32[2,32,128]{2,1,0:T(8,128)S(1)} collective-permute-done((f32[2,32,128]{2,1,0:T(8,128)S(1)}, f32[2,32,128]{2,1,0:T(8,128)S(1)}, u32[]{:S(2)}, u32[]{:S(2)}) %collective-permute-start.1) | collective-permute-done | bytes 32800 | tf_op jit(solution)/shard_map/ppermute | solution.py:227
  12.8 1.5 %collective-permute-start.2 = (f32[4,32,128]{2,1,0:T(8,128)S(1)}, f32[4,32,128]{2,1,0:T(8,128)S(1)}, u32[]{:S(2)}, u32[]{:S(2)}) collective-permute-start(f32[4,32,128]{2,1,0:T(8,128)S(1)} %pad_maximum_fusion.1), channel_id=1, source_target_pairs={{0,1},{1,0},{2,3},{3,2},{4,5},{5,4},{6,7},{7,6},{8,9},{9,8},{10,11... | collective-permute-start | bytes 196616 | tf_op jit(solution)/shard_map/ppermute | solution.py:227
  14.3 2.7 %collective-permute-done.2 = f32[4,32,128]{2,1,0:T(8,128)S(1)} collective-permute-done((f32[4,32,128]{2,1,0:T(8,128)S(1)}, f32[4,32,128]{2,1,0:T(8,128)S(1)}, u32[]{:S(2)}, u32[]{:S(2)}) %collective-permute-start.2) | collective-permute-done | bytes 65568 | tf_op jit(solution)/shard_map/ppermute | solution.py:227
  17.1 0.6 %collective-permute-start.3 = (f32[8,32,128]{2,1,0:T(8,128)S(1)}, f32[8,32,128]{2,1,0:T(8,128)S(1)}, u32[]{:S(2)}, u32[]{:S(2)}) collective-permute-start(f32[8,32,128]{2,1,0:T(8,128)S(1)} %pad_maximum_fusion), channel_id=1, source_target_pairs={{0,4},{2,6},{4,0},{6,2},{1,5},{3,7},{5,1},{7,3},{8,12},{10,14},{12... | collective-permute-start | bytes 393224 | tf_op jit(solution)/shard_map/ppermute | solution.py:227
  17.7 0.0 collective-permute-done.4.refs_1_
  17.7 2.3 %cell_prep.1 = (bf16[2,40,128,48]{3,2,1,0:T(8,128)(2,1)S(1)}, f32[2,320,128]{2,1,0:T(8,128)S(1)}, s32[2,40,128]{2,1,0:T(8,128)S(1)}) custom-call(f32[40,8,128]{2,1,0:T(8,128)S(1)} %stack.11.refs_0_, f32[40,8,128]{2,1,0:T(8,128)S(1)} %collective-permute-done.4.refs_1_), custom_call_target="tpu_custom_call" | custom-call | tf_op jit(solution)/shard_map/cell_prep/pallas_call | solution.py:209
  20.0 2.1 %collective-permute-done.3 = f32[8,32,128]{2,1,0:T(8,128)S(1)} collective-permute-done((f32[8,32,128]{2,1,0:T(8,128)S(1)}, f32[8,32,128]{2,1,0:T(8,128)S(1)}, u32[]{:S(2)}, u32[]{:S(2)}) %collective-permute-start.3) | collective-permute-done | bytes 131104 | tf_op jit(solution)/shard_map/ppermute | solution.py:227
  22.2 0.1 collective-permute-start.5
  22.2 1.5 %collective-permute-done.5 = f32[16,32,128]{2,1,0:T(8,128)S(1)} collective-permute-done((f32[16,32,128]{2,1,0:T(8,128)S(1)}, f32[16,32,128]{2,1,0:T(8,128)S(1)}, u32[]{:S(2)}, u32[]{:S(2)}) %collective-permute-start.5) | collective-permute-done | bytes 262176 | tf_op jit(solution)/shard_map/ppermute | solution.py:227
  23.8 0.0 copy-done
  23.8 14.9 %rbf_sums.1 = (f32[2,12,40,128]{3,2,1,0:T(8,128)S(1)}, f32[2,12,40,128]{3,2,1,0:T(8,128)S(1)}) custom-call(s32[2,40,128]{2,1,0:T(8,128)S(1)} %get-tuple-element.16.list_ref, f32[4,12,24]{2,1,0:T(8,128)S(1)} %copy-done, f32[32,32,128]{2,1,0:T(8,128)S(1)} %constant_dynamic-update-slice_fusion.5.block_ref, ...), custom_call_target="tpu_custom_call" | custom-call | tf_op jit(solution)/shard_map/rbf_sums/pallas_call | solution.py:239
  38.7 0.2 collective-permute-start.6
  38.9 1.7 %collective-permute-done.6.peer_ref = f32[2,12,40,128]{3,2,1,0:T(8,128)S(1)} collective-permute-done((f32[2,12,40,128]{3,2,1,0:T(8,128)S(1)}, f32[2,12,40,128]{3,2,1,0:T(8,128)S(1)}, u32[]{:S(2)}, u32[]{:S(2)}) %collective-permute-start.6) | collective-permute-done | bytes 491552 | tf_op jit(solution)/shard_map/ppermute | solution.py:257
  40.6 1.1 %merge.1 = (f32[6,40,512]{2,1,0:T(8,128)}, f32[6,40,512]{2,1,0:T(8,128)}) custom-call(f32[2,12,40,128]{3,2,1,0:T(8,128)S(1)} %get-tuple-element.20.own_ref, f32[2,12,40,128]{3,2,1,0:T(8,128)S(1)} %collective-permute-done.6.peer_ref), custom_call_target="tpu_custom_call" | custom-call | tf_op jit(solution)/shard_map/merge/pallas_call | solution.py:259
  (12 shorter events, 0.1 us)
Async XLA Ops:
  0.6 23.1 %copy-start = (f32[4,12,24]{2,1,0:T(8,128)S(1)}, f32[4,12,24]{2,1,0:T(8,128)}, u32[]{:S(2)}) copy-start(f32[4,12,24]{2,1,0:T(8,128)} %constant.3.clone.mix_ref) | copy-start | bytes 13828
  1.5 7.4 %collective-permute-start = (f32[1,32,128]{2,1,0:T(8,128)S(1)}, f32[1,32,128]{2,1,0:T(8,128)S(1)}, u32[]{:S(2)}, u32[]{:S(2)}) collective-permute-start(f32[1,32,128]{2,1,0:T(8,128)S(1)} %maximum_bitcast_fusion), channel_id=1, source_target_pairs={{0,16},{8,24},{16,0},{24,8},{1,17},{9,25},{17,1},{25,9},{2,18},{10... | collective-permute-start | bytes 49160 | tf_op jit(solution)/shard_map/ppermute | solution.py:227
  7.3 10.4 %collective-permute-start.4 = (f32[40,8,128]{2,1,0:T(8,128)S(1)}, f32[40,8,128]{2,1,0:T(8,128)S(1)}, u32[]{:S(2)}, u32[]{:S(2)}) collective-permute-start(f32[40,8,128]{2,1,0:T(8,128)S(1)} %stack.11.refs_0_), channel_id=1, source_target_pairs={{0,4},{2,6},{4,0},{6,2},{1,5},{3,7},{5,1},{7,3},{8,12},{10,14},{12... | collective-permute-start | bytes 491528 | tf_op jit(solution)/shard_map/ppermute | solution.py:202
  8.9 3.9 %collective-permute-start.1 = (f32[2,32,128]{2,1,0:T(8,128)S(1)}, f32[2,32,128]{2,1,0:T(8,128)S(1)}, u32[]{:S(2)}, u32[]{:S(2)}) collective-permute-start(f32[2,32,128]{2,1,0:T(8,128)S(1)} %pad_maximum_fusion.2), channel_id=1, source_target_pairs={{0,8},{8,0},{16,24},{24,16},{1,9},{9,1},{17,25},{25,17},{2,10},{10... | collective-permute-start | bytes 98312 | tf_op jit(solution)/shard_map/ppermute | solution.py:227
  12.8 4.3 %collective-permute-start.2 = (f32[4,32,128]{2,1,0:T(8,128)S(1)}, f32[4,32,128]{2,1,0:T(8,128)S(1)}, u32[]{:S(2)}, u32[]{:S(2)}) collective-permute-start(f32[4,32,128]{2,1,0:T(8,128)S(1)} %pad_maximum_fusion.1), channel_id=1, source_target_pairs={{0,1},{1,0},{2,3},{3,2},{4,5},{5,4},{6,7},{7,6},{8,9},{9,8},{10,11... | collective-permute-start | bytes 196616 | tf_op jit(solution)/shard_map/ppermute | solution.py:227
  17.1 5.0 %collective-permute-start.3 = (f32[8,32,128]{2,1,0:T(8,128)S(1)}, f32[8,32,128]{2,1,0:T(8,128)S(1)}, u32[]{:S(2)}, u32[]{:S(2)}) collective-permute-start(f32[8,32,128]{2,1,0:T(8,128)S(1)} %pad_maximum_fusion), channel_id=1, source_target_pairs={{0,4},{2,6},{4,0},{6,2},{1,5},{3,7},{5,1},{7,3},{8,12},{10,14},{12... | collective-permute-start | bytes 393224 | tf_op jit(solution)/shard_map/ppermute | solution.py:227
  22.2 1.6 %collective-permute-start.5 = (f32[16,32,128]{2,1,0:T(8,128)S(1)}, f32[16,32,128]{2,1,0:T(8,128)S(1)}, u32[]{:S(2)}, u32[]{:S(2)}) collective-permute-start(f32[16,32,128]{2,1,0:T(8,128)S(1)} %get-tuple-element.24), channel_id=1, source_target_pairs={{0,2},{2,0},{4,6},{6,4},{1,3},{3,1},{5,7},{7,5},{8,10},{10,8},{12,... | collective-permute-start | bytes 786440 | tf_op jit(solution)/shard_map/ppermute | solution.py:227
  38.7 1.9 %collective-permute-start.6 = (f32[2,12,40,128]{3,2,1,0:T(8,128)S(1)}, f32[2,12,40,128]{3,2,1,0:T(8,128)S(1)}, u32[]{:S(2)}, u32[]{:S(2)}) collective-permute-start(f32[2,12,40,128]{3,2,1,0:T(8,128)S(1)} %get-tuple-element.21), channel_id=1, source_target_pairs={{0,2},{2,0},{4,6},{6,4},{1,3},{3,1},{5,7},{7,5},{8,10},{10,8},{12,... | collective-permute-start | bytes 1474568 | tf_op jit(solution)/shard_map/ppermute | solution.py:257

commit v4 on v3

v4 whole, which is shorter than its diff:
```python
import functools

import jax
import jax.numpy as jnp
import numpy as np
from jax import lax
from jax.experimental import pallas as pl
from jax.experimental.pallas import tpu as pltpu
from jax.sharding import PartitionSpec as P

NT = 8
TILE = 128
RADIUS = 0.4
EDGE = 4.0**0.2
SCALE = (EDGE / RADIUS) ** 2
FEATURES = 48
UNROLL = 4
VMEM_LIMIT = 16 * 1024 * 1024
BOTH_MINOR = (((1,), (1,)), ((), ()))
F32 = jnp.float32
BF16 = jnp.bfloat16


def spectral_rows(instances, groups):
    later = np.arange(instances)[:, None]
    earlier = np.arange(instances)[None, :]
    distance = (later - earlier).astype(np.float64)
    guarded = np.where(distance == 0, 0.5, np.pi * distance / instances)
    parity = np.where((later - earlier) % 2 == 0, 1.0, -1.0)
    matrix = np.where(distance == 0, 0.0, 0.5 * parity * np.cos(guarded) / np.sin(guarded))
    per = instances // groups
    rows = []
    for group in range(groups):
        own = slice(group * per, (group + 1) * per)
        rows.append(np.concatenate([np.eye(instances)[own], matrix[own]], axis=0))
    return np.stack([np.kron(block, np.eye(3)) for block in rows]).astype(np.float32)


def split3(value):
    high = value.astype(BF16).astype(F32)
    rest = value - high
    middle = rest.astype(BF16).astype(F32)
    return high, middle, rest - middle


def flip(size, bit):
    return [(i, i ^ bit) for i in range(size)]


def bits_of(size):
    return [1 << b for b in range(size.bit_length() - 1)]


def cell_prep_kernel(source, feature_ref, coord_ref, place_ref, *, rows, plane, sizes, masks):
    n_inst, n_cell = sizes["inst"], sizes["cell"]
    device = (lax.axis_index("blade") * n_inst + lax.axis_index("inst")) * n_cell + lax.axis_index("cell")
    row_id = lax.broadcasted_iota(jnp.int32, (8, TILE), 0)
    diagonal = lax.broadcasted_iota(jnp.int32, (TILE, TILE), 0) == lax.broadcasted_iota(jnp.int32, (TILE, TILE), 1)
    identity = jnp.where(diagonal, 1.0, 0.0).astype(BF16)

    def one_row(r, carry):
        value = source[r]
        coord_ref[pl.ds(r, 8, stride=rows), :] = value
        centred = jnp.where(row_id < 3, value - 0.5, 0.0)
        length = SCALE * jnp.sum(centred * centred, axis=0, keepdims=True)
        value = jnp.where(row_id == 3, 1.0, jnp.where(row_id == 4, length, centred))
        high, middle, low = split3(value)
        stacked = jnp.concatenate([high, middle, low, high, middle, high], axis=0).astype(BF16)
        turned = lax.dot_general(identity, stacked, BOTH_MINOR, preferred_element_type=F32)
        feature_ref[r] = turned.astype(BF16)
        return carry

    lax.fori_loop(0, rows, one_row, 0, unroll=8)
    tile = coord_ref[3 * rows : 4 * rows, :].T[:8].astype(jnp.int32)
    if masks is not None:
        tile = tile ^ device
        places = [(lax.shift_right_logical(tile, m) & 1) << k for k, m in enumerate(masks)]
        tile = functools.reduce(lambda x, y: x | y, places)
    else:
        tile = tile & (plane - 1)
    place_ref[:, :rows] = tile


def sums_kernel(*refs, rows, start, count, slots, half, first, prepare, last):
    list_refs, mix_ref, feature_refs = refs[:slots], refs[slots], refs[slots + 1 : 2 * slots + 1]
    refs = refs[2 * slots + 1 :]
    dist0, dist1, weight0, weight1 = refs[-5 if last else -4 :][:4]
    refs = list(refs[: -5 if last else -4]) + list(refs[-1:] if last else [])
    if last:
        coord_refs, before_ref = refs[:slots], refs[slots]
        refs = refs[slots + 1 :]
    block_refs = refs[:prepare]
    refs = refs[prepare:]
    if prepare and last:
        own_ref, peer_ref, centre_ref, coef_ref, total_ref = refs
    elif prepare:
        total_ref, centre_ref, coef_ref = refs
    elif last:
        centre_ref, coef_ref, own_ref, peer_ref, total_ref = refs
    else:
        centre_ref, coef_ref, total_ref = refs
    combos = 2 * half
    plane = centre_ref.shape[0] // 2
    row_id = lax.broadcasted_iota(jnp.int32, (8, TILE), 0)
    inst = lax.axis_index("inst")
    blade = lax.axis_index("blade")
    terms = [blade ^ first, blade ^ (first + 1)]
    mix = jnp.concatenate([mix_ref[inst], mix_ref[inst ^ 1]], axis=0)

    base = 0
    for block_ref in block_refs:

        def one_tile(p, carry, block_ref=block_ref, base=base):
            value = block_ref[p, 3 * NT : 3 * NT + 8, :]
            centred = jnp.where(row_id < 3, value - 0.5, 0.0)
            length = SCALE * jnp.sum(centred * centred, axis=0, keepdims=True)
            value = jnp.where(row_id == 3, length, jnp.where(row_id == 4, 1.0, (-2.0 * SCALE) * centred))
            high, middle, low = split3(value)
            stacked = jnp.concatenate([high, high, high, middle, middle, low], axis=0)
            centre_ref[base + p] = stacked.astype(BF16)
            mixed = jnp.dot(
                mix, block_ref[p, : 3 * NT, :],
                preferred_element_type=F32, precision=lax.Precision.HIGHEST,
            )
            mixed_high = mixed.astype(BF16).astype(F32)
            coef_ref[base + p] = jnp.concatenate([mixed_high, mixed - mixed_high], axis=0).astype(BF16)
            return carry

        lax.fori_loop(0, block_ref.shape[0], one_tile, 0, unroll=4)
        base += block_ref.shape[0]

    def tile_pair(r, slot):
        lists = list_refs[slot]
        return lists[terms[0], start + r], lists[terms[1], start + r] + plane

    def distances(i, slot, out):
        for k in range(2):
            a, b = tile_pair(2 * i + k, slot)
            out[k] = jnp.dot(
                feature_refs[slot][start + 2 * i + k], jnp.concatenate([centre_ref[a], centre_ref[b]], axis=1),
                preferred_element_type=F32,
            )

    def weights(source, out):
        for k in range(2):
            squared = jnp.maximum(source[k], 1e-12)
            margin = jnp.maximum(EDGE - squared * lax.rsqrt(squared), 0.0)
            margin_sq = margin * margin
            weight = (margin_sq * margin_sq) * (1.25 * EDGE - margin)
            high = weight.astype(BF16)
            out[k, :TILE] = high
            out[k, TILE:] = (weight - high.astype(F32)).astype(BF16)

    def contract(i, slot, source):
        for k in range(2):
            r = 2 * i + k
            a, b = tile_pair(r, slot)
            total = lax.dot_general(
                jnp.concatenate([coef_ref[a], coef_ref[b]], axis=1), source[k], BOTH_MINOR,
                preferred_element_type=F32,
            )
            total = total[:combos, :TILE] + total[combos:, :TILE] + total[:combos, TILE:]
            for group in range(combos // 8):
                total_ref[slot, pl.ds(r + group * 8 * count, 8, stride=count), :] = total[group * 8 : group * 8 + 8]

    distances(0, 0, dist0)
    pairs = count // 2

    def one_pair(i, carry):
        contract(jnp.maximum(i - 1, 0), 1, weight1)
        distances(i, 1, dist1)
        weights(dist0, weight0)
        contract(i, 0, weight0)
        distances(jnp.minimum(i + 1, pairs - 1), 0, dist0)
        weights(dist1, weight1)
        return carry

    lax.fori_loop(0, pairs, one_pair, 0, unroll=UNROLL)
    contract(pairs - 1, 1, weight1)
    if not last:
        return

    shifts = half // 2
    for slot in range(slots):
        for out, first_row in ((own_ref, 0), (peer_ref, half)):
            for c in range(half):
                span = slice((first_row + c) * count, (first_row + c + 1) * count)
                value = total_ref[slot, span, :] + before_ref[slot, span, :]
                if c < shifts:
                    begin = (c % 3) * rows + start
                    value = value + coord_refs[slot][begin : begin + count, :]
                out[slot, c] = value


def merge_kernel(*refs, slots, half, spans):
    shifts = half // 2
    moved_ref, velocity_ref = refs[-2:]
    inst = lax.axis_index("inst")
    for index, source in enumerate(refs[:-2]):
        start, count = spans[index // 2]
        for slot in range(slots):
            lane = pl.multiple_of((inst ^ (index % 2) ^ (2 * slot)) * TILE, TILE)
            moved_ref[:, start : start + count, pl.ds(lane, TILE)] = source[slot, :shifts]
            velocity_ref[:, start : start + count, pl.ds(lane, TILE)] = source[slot, shifts:]


def in_vmem(value):
    return pltpu.with_memory_space_constraint(value, pltpu.VMEM)


def vmem():
    return pl.BlockSpec(memory_space=pltpu.VMEM)


def smem():
    return pl.BlockSpec(memory_space=pltpu.SMEM)


def on_device(cell_coords, centre_points, coefficients, tile_lists, *, sizes):
    n_blade, n_inst, n_cell = sizes["blade"], sizes["inst"], sizes["cell"]
    rows = cell_coords.shape[1]
    terms = tile_lists.shape[2]
    width = centre_points.shape[1]
    slots = n_inst // 2
    half = 2 * 3 * (NT // n_inst)
    block = jnp.concatenate([coefficients, centre_points, jnp.zeros((5, width), F32)], axis=0)
    list_row = jnp.pad(tile_lists[:, 0, :].astype(F32), ((0, 0), (0, TILE - terms)))
    blank = jnp.zeros_like(list_row)
    cell_rows = jnp.stack([cell_coords[0], cell_coords[1], cell_coords[2], list_row] + [blank] * 4, axis=1)

    core = 1
    inner = [("cell", n_cell, b, b) for b in bits_of(n_cell)]
    inner += [("inst", n_inst, b, b * n_cell) for b in bits_of(n_inst) if b != core]
    masks = [mask.bit_length() - 1 for _, _, _, mask in inner] + [(core * n_cell).bit_length() - 1]

    half_plane = block[None]
    for index, (axis, size, bit, _) in enumerate(inner):
        arrived = lax.ppermute(half_plane, axis, flip(size, bit))
        if index == 0:
            arrived, cell_rows = lax.optimization_barrier((arrived, cell_rows))
        half_plane = jnp.concatenate([half_plane, arrived], axis=0)
    others = [lax.ppermute(cell_rows, "inst", flip(n_inst, 2 * s)) for s in range(1, slots)]
    halves = [half_plane]
    for m in range(1, n_blade):
        halves.append(lax.ppermute(half_plane, "blade", flip(n_blade, m)))

    swapped = []
    for m in range(2):
        swapped.append(lax.ppermute(halves[m], "inst", flip(n_inst, core)))
    late = lax.ppermute(jnp.concatenate(halves[2:], axis=0), "inst", flip(n_inst, core))
    swapped += jnp.split(late, n_blade - 2, axis=0)

    if width < TILE:
        device = lax.axis_index("inst") * n_cell + lax.axis_index("cell")
        relative = jnp.arange(n_inst * n_cell) ^ device
        order = sum(((relative >> m) & 1) << k for k, m in enumerate(masks))

        def whole_plane(mine, theirs):
            blocks = jnp.take(jnp.concatenate([mine, theirs], axis=0), order, axis=0)
            blocks = blocks.reshape(-1, TILE // width, 3 * NT + 8, width)
            return [jnp.moveaxis(blocks, 1, 2).reshape(-1, 3 * NT + 8, TILE)]

        plane = n_inst * n_cell * width // TILE
    else:
        def whole_plane(mine, theirs):
            return [mine, theirs]

        plane = n_inst * n_cell
    planes = [whole_plane(*pair) for pair in zip(halves, swapped)]

    def cell_prep(cells):
        return pl.pallas_call(
            functools.partial(
                cell_prep_kernel, rows=rows, plane=plane, sizes=sizes,
                masks=masks if width == TILE else None,
            ),
            out_shape=(
                pltpu.VMEM((rows, TILE, FEATURES), BF16),
                pltpu.VMEM((8 * rows, TILE), F32),
                jax.ShapeDtypeStruct((8, TILE), jnp.int32),
            ),
            in_specs=[vmem()],
            out_specs=(vmem(),) * 3,
            compiler_params=pltpu.CompilerParams(vmem_limit_bytes=VMEM_LIMIT),
            name="cell_prep",
        )(in_vmem(cells))

    prepared = [cell_prep(cell_rows)]
    prepared += [cell_prep(cells) for cells in others]
    features, coords, places = map(list, zip(*prepared))

    mix = jnp.asarray(spectral_rows(NT, n_inst))
    tables = (pltpu.VMEM((2 * plane, FEATURES, TILE), BF16), pltpu.VMEM((2 * plane, 4 * half, TILE), BF16))
    spans = [(0, rows)]

    def sums(first, span, given, extra):
        start, count = spans[span]
        last = len(extra) > 0
        blocks = [] if given else planes[first] + planes[first + 1]
        total = pltpu.VMEM((slots, 2 * half * count, TILE), F32)
        out = (pltpu.VMEM((slots, half, count, TILE), F32),) * 2 if last else (total,)
        out = out + (() if given else tables)
        operands = [*features, *extra, *blocks, *given]
        return pl.pallas_call(
            functools.partial(
                sums_kernel, rows=rows, start=start, count=count, slots=slots, half=half, first=first,
                prepare=len(blocks), last=last,
            ),
            out_shape=out,
            in_specs=[smem()] * slots + [vmem()] * (1 + len(operands)),
            out_specs=(vmem(),) * len(out),
            scratch_shapes=[pltpu.VMEM((2, TILE, 2 * TILE), F32)] * 2
            + [pltpu.VMEM((2, 2 * TILE, 2 * TILE), BF16)] * 2
            + ([total] if last else []),
            compiler_params=pltpu.CompilerParams(vmem_limit_bytes=VMEM_LIMIT),
        )(*places, in_vmem(mix), *map(in_vmem, operands))

    before, near = [], []
    for span in range(len(spans)):
        part, *tables_made = sums(0, span, near, [])
        before, near = before + [part], near or tables_made
    results, far = [], []
    for span in range(len(spans)):
        own, peer, *tables_made = sums(2, span, far, [*coords, before[span]])
        far = far or tables_made
        results += [own, lax.ppermute(peer, "inst", flip(n_inst, core))]
    out = jax.ShapeDtypeStruct((half // 2, rows, n_inst * TILE), F32)
    moved, velocity = pl.pallas_call(
        functools.partial(merge_kernel, slots=slots, half=half, spans=spans),
        out_shape=(out, out),
        in_specs=[vmem()] * len(results),
        out_specs=(vmem(), vmem()),
        compiler_params=pltpu.CompilerParams(vmem_limit_bytes=VMEM_LIMIT),
        name="merge",
    )(*map(in_vmem, results))
    shape = (NT // n_inst, 3, rows, n_inst * TILE)
    return (moved.reshape(shape), velocity.reshape(shape))


def solution(mesh):
    sizes = dict(mesh.shape)
    in_specs = (
        P(None, ("blade", "cell"), "inst"),
        P(None, ("blade", "inst", "cell")),
        P(None, ("blade", "inst", "cell")),
        P(("blade", "cell"), "inst", None),
    )
    out_specs = (P("inst", None, ("blade", "cell"), None), P("inst", None, ("blade", "cell"), None))
    return jax.shard_map(
        functools.partial(on_device, sizes=sizes),
        mesh=mesh, in_specs=in_specs, out_specs=out_specs, check_vma=False,
    )
```

time: 42 us -> 43.4 us (1.033)
  waiting for transfers between devices: 9.63 us -> 6.64 us
  starting transfers between devices: 9.59 us -> 12.3 us
  Pallas kernels: 18.3 us -> 20.9 us
  other arithmetic: 1.61 us -> 0.82 us
    ppermute x6 -> x9, waiting for transfers between devices: 9.62 us -> 6.64 us  [the longest x3 3.11 us: on_device(): halves.append(lax.ppermute(half_plane, 'blade', flip(n_blade, m)))]
    ppermute x6 -> x9, starting transfers between devices: 8.04 us -> 10.8 us  [the longest x2 4.94 us: on_device(): arrived = lax.ppermute(half_plane, axis, flip(size, bit))]
    pallas_call x3 -> x5, Pallas kernels: 18.3 us -> 20.9 us  [the longest x2 17.4 us: sums(): pl.pallas_call(functools.partial(sums_kernel, rows=rows, start=start, cou...]
    unnamed x1 -> x0, other arithmetic: 0.8 us -> none
  transfers between devices with their start and end apart: 7 -> 10, of which waited for: 5 -> 5; matrix products, arithmetic and copies ran while one was open for 6% -> 4% of each run, Pallas kernels for 6% -> 26%
where the time goes in v4:
time: 43.4 us; the launch traced here: 43.2 us
  Pallas kernels  20.9 us (48%)
  starting transfers between devices  12.3 us (28%)
  waiting for transfers between devices  6.64 us (15%)
  local copies, waits for them, and re-layouts  1.81 us (4%)
  other arithmetic  0.82 us (2%)
  between operations  0.73 us (2%)
    pallas_call x2, Pallas kernels, sums(): pl.pallas_call(functools.partial(sums_kernel, rows=rows, start=start, cou...  17.4 us
    ppermute x2, starting transfers between devices, on_device(): arrived = lax.ppermute(half_plane, axis, flip(size, bit))  4.94 us
    ppermute x3, starting transfers between devices, on_device(): halves.append(lax.ppermute(half_plane, 'blade', flip(n_blade, m)))  4.78 us
    ppermute x3, waiting for transfers between devices, on_device(): halves.append(lax.ppermute(half_plane, 'blade', flip(n_blade, m)))  3.11 us
    pallas_call x2, Pallas kernels, cell_prep(): pl.pallas_call(functools.partial(cell_prep_kernel, rows=rows, plane=plane...  2.42 us
    ppermute x2, waiting for transfers between devices, on_device(): arrived = lax.ppermute(half_plane, axis, flip(size, bit))  2.04 us
    ppermute x1, starting transfers between devices, on_device(): lax.ppermute(cell_rows, 'inst', flip(n_inst, 2 * s))  1.49 us
    ppermute x1, waiting for transfers between devices, on_device(): results += [own, lax.ppermute(peer, 'inst', flip(n_inst, core))]  1.49 us
  transfers between devices with their start and end apart: 10, of which 5 were waited for; matrix products, arithmetic and copies ran while one was open for 4% of the time, Pallas kernels for 26%

profile of v4, /device:TPU:0, one launch (start us, length us, event | category | flops | bytes accessed | tf_op | source)
XLA Modules:
  0.0 43.2 jit_solution(18077635160791748813)
XLA Ops:
  0.6 0.0 copy-start
  0.7 0.1 pad.14.clone
  0.7 0.8 %maximum_bitcast_fusion = f32[1,32,128]{2,1,0:T(8,128)S(1)} fusion(f32[3,128]{1,0:T(4,128)} %param.6, f32[24,128]{1,0:T(8,128)} %param.7, f32[32]{0:T(128)S(1)} %pad.14.clone), kind=kLoop, calls=%fused_computation.4 | loop fusion | flops 8192 | bytes 30336 | tf_op jit(solution)/shard_map/broadcast_in_dim | solution.py:236
  1.5 3.0 %collective-permute-start = (f32[1,32,128]{2,1,0:T(8,128)S(1)}, f32[1,32,128]{2,1,0:T(8,128)S(1)}, u32[]{:S(2)}, u32[]{:S(2)}) collective-permute-start(f32[1,32,128]{2,1,0:T(8,128)S(1)} %maximum_bitcast_fusion), channel_id=1, source_target_pairs={{0,1},{1,0},{2,3},{3,2},{4,5},{5,4},{6,7},{7,6},{8,9},{9,8},{10,11... | collective-permute-start | bytes 49160 | tf_op jit(solution)/shard_map/ppermute | solution.py:238
  4.5 0.8 %copy.7 = s32[40,1,4]{2,0,1:T(8,128)S(1)} copy(s32[40,1,4]{0,2,1:T(4,128)} %param.8) | data formatting | bytes 1280 | tf_op args[3]
  5.3 0.8 %fusion.1 = (f32[1,40,128]{2,1,0:T(8,128)S(1)}, f32[1,40,128]{2,1,0:T(8,128)S(1)}, f32[1,40,128]{2,1,0:T(8,128)S(1)}) fusion(f32[3,40,128]{2,1,0:T(8,128)} %param.5), kind=kLoop, calls=%fused_computation.6 | loop fusion | bytes 122880 | tf_op jit(solution)/shard_map/slice | solution.py:229
  6.1 0.2 stack.11.source
  6.3 0.0 collective-permute-done
  6.3 1.9 %collective-permute-start.2 = (f32[2,32,128]{2,1,0:T(8,128)S(1)}, f32[2,32,128]{2,1,0:T(8,128)S(1)}, u32[]{:S(2)}, u32[]{:S(2)}) collective-permute-start(f32[2,32,128]{2,1,0:T(8,128)S(1)} %pad_maximum_fusion.2), channel_id=1, source_target_pairs={{0,4},{2,6},{4,0},{6,2},{1,5},{3,7},{5,1},{7,3},{8,12},{10,14},{12... | collective-permute-start | bytes 98312 | tf_op jit(solution)/shard_map/ppermute | solution.py:238
  8.2 2.0 %collective-permute-done.2 = f32[2,32,128]{2,1,0:T(8,128)S(1)} collective-permute-done((f32[2,32,128]{2,1,0:T(8,128)S(1)}, f32[2,32,128]{2,1,0:T(8,128)S(1)}, u32[]{:S(2)}, u32[]{:S(2)}) %collective-permute-start.2) | collective-permute-done | bytes 32800 | tf_op jit(solution)/shard_map/ppermute | solution.py:238
  10.3 4.0 %collective-permute-start.7 = (f32[4,32,128]{2,1,0:T(8,128)S(1)}, f32[4,32,128]{2,1,0:T(8,128)S(1)}, u32[]{:S(2)}, u32[]{:S(2)}) collective-permute-start(f32[4,32,128]{2,1,0:T(8,128)S(1)} %pad_maximum_fusion.1.refs_5_), channel_id=1, source_target_pairs={{0,24},{8,16},{16,8},{24,0},{1,25},{9,17},{17,9},{25,1},{2,26},{10... | collective-permute-start | bytes 196616 | tf_op jit(solution)/shard_map/ppermute | solution.py:245
  14.3 0.0 collective-permute-start.6
  14.3 1.5 %collective-permute-start.1 = (f32[40,8,128]{2,1,0:T(8,128)S(1)}, f32[40,8,128]{2,1,0:T(8,128)S(1)}, u32[]{:S(2)}, u32[]{:S(2)}) collective-permute-start(f32[40,8,128]{2,1,0:T(8,128)S(1)} %stack.11.source), channel_id=1, source_target_pairs={{0,4},{2,6},{4,0},{6,2},{1,5},{3,7},{5,1},{7,3},{8,12},{10,14},{12... | collective-permute-start | bytes 491528 | tf_op jit(solution)/shard_map/ppermute | solution.py:242
  15.8 0.8 %collective-permute-start.4 = (f32[4,32,128]{2,1,0:T(8,128)S(1)}, f32[4,32,128]{2,1,0:T(8,128)S(1)}, u32[]{:S(2)}, u32[]{:S(2)}) collective-permute-start(f32[4,32,128]{2,1,0:T(8,128)S(1)} %pad_maximum_fusion.1.refs_5_), channel_id=1, source_target_pairs={{0,8},{8,0},{16,24},{24,16},{1,9},{9,1},{17,25},{25,17},{2,10},{10... | collective-permute-start | bytes 196616 | tf_op jit(solution)/shard_map/ppermute | solution.py:245
  16.5 0.1 collective-permute-done.7.refs_10_
  16.7 2.9 %collective-permute-done.6.refs_8_ = f32[4,32,128]{2,1,0:T(8,128)S(1)} collective-permute-done((f32[4,32,128]{2,1,0:T(8,128)S(1)}, f32[4,32,128]{2,1,0:T(8,128)S(1)}, u32[]{:S(2)}, u32[]{:S(2)}) %collective-permute-start.6) | collective-permute-done | bytes 65568 | tf_op jit(solution)/shard_map/ppermute | solution.py:245
  19.6 0.1 collective-permute-start.8
  19.7 0.5 %collective-permute-start.3 = (f32[4,32,128]{2,1,0:T(8,128)S(1)}, f32[4,32,128]{2,1,0:T(8,128)S(1)}, u32[]{:S(2)}, u32[]{:S(2)}) collective-permute-start(f32[4,32,128]{2,1,0:T(8,128)S(1)} %pad_maximum_fusion.1.refs_5_), channel_id=1, source_target_pairs={{0,2},{2,0},{4,6},{6,4},{1,3},{3,1},{5,7},{7,5},{8,10},{10,8},{12,... | collective-permute-start | bytes 196616 | tf_op jit(solution)/shard_map/ppermute | solution.py:249
  20.2 0.1 collective-permute-done.4.refs_7_
  20.2 0.0 collective-permute-start.5
  20.2 1.2 %cell_prep.2 = (bf16[40,128,48]{2,1,0:T(8,128)(2,1)S(1)}, f32[320,128]{1,0:T(8,128)S(1)}, s32[8,128]{1,0:T(8,128)S(1)}) custom-call(f32[40,8,128]{2,1,0:T(8,128)S(1)} %stack.11.source), custom_call_target="tpu_custom_call" | custom-call | tf_op jit(solution)/shard_map/cell_prep/pallas_call | solution.py:272
  21.5 0.0 collective-permute-done.1.source
  21.5 1.2 %cell_prep.3 = (bf16[40,128,48]{2,1,0:T(8,128)(2,1)S(1)}, f32[320,128]{1,0:T(8,128)S(1)}, s32[8,128]{1,0:T(8,128)S(1)}) custom-call(f32[40,8,128]{2,1,0:T(8,128)S(1)} %collective-permute-done.1.source), custom_call_target="tpu_custom_call" | custom-call | tf_op jit(solution)/shard_map/cell_prep/pallas_call | solution.py:272
  22.7 0.0 collective-permute-done.3.refs_6_
  22.7 0.0 collective-permute-done.5.refs_8_
  22.7 0.0 copy-done
  22.7 8.6 %shard_map.68 = (f32[2,960,128]{2,1,0:T(8,128)S(1)}, bf16[16,48,128]{2,1,0:T(8,128)(2,1)}, bf16[16,48,128]{2,1,0:T(8,128)(2,1)}) custom-call(s32[8,128]{1,0:T(8,128)S(1)} %get-tuple-element.16.refs_0_, s32[8,128]{1,0:T(8,128)S(1)} %get-tuple-element.17.refs_1_, f32[4,12,24]{2,1,0:T(8,128)S(1)} %copy-done, ...), custom_call_target="tpu_custom_call" | custom-call | tf_op jit(solution)/shard_map/pallas_call | solution.py:304
  31.3 0.0 collective-permute-done.8
  31.3 8.8 %shard_map.69 = (f32[2,12,40,128]{3,2,1,0:T(8,128)S(1)}, f32[2,12,40,128]{3,2,1,0:T(8,128)S(1)}, bf16[16,48,128]{2,1,0:T(8,128)(2,1)}, bf16[16,48,128]{2,1,0:T(8,128)(2,1)}) custom-call(s32[8,128]{1,0:T(8,128)S(1)} %get-tuple-element.16.refs_0_, s32[8,128]{1,0:T(8,128)S(1)} %get-tuple-element.17.refs_1_, f32[4,12,24]{2,1,0:T(8,128)S(1)} %copy-done, ...), custom_call_target="tpu_custom_call" | custom-call | tf_op jit(solution)/shard_map/pallas_call | solution.py:304
  40.1 0.5 %collective-permute-start.9 = (f32[2,12,40,128]{3,2,1,0:T(8,128)S(1)}, f32[2,12,40,128]{3,2,1,0:T(8,128)S(1)}, u32[]{:S(2)}, u32[]{:S(2)}) collective-permute-start(f32[2,12,40,128]{3,2,1,0:T(8,128)S(1)} %get-tuple-element.25), channel_id=1, source_target_pairs={{0,2},{2,0},{4,6},{6,4},{1,3},{3,1},{5,7},{7,5},{8,10},{10,8},{12,... | collective-permute-start | bytes 1474568 | tf_op jit(solution)/shard_map/ppermute | solution.py:326
  40.6 1.5 %collective-permute-done.9.refs_1_ = f32[2,12,40,128]{3,2,1,0:T(8,128)S(1)} collective-permute-done((f32[2,12,40,128]{3,2,1,0:T(8,128)S(1)}, f32[2,12,40,128]{3,2,1,0:T(8,128)S(1)}, u32[]{:S(2)}, u32[]{:S(2)}) %collective-permute-start.9) | collective-permute-done | bytes 491552 | tf_op jit(solution)/shard_map/ppermute | solution.py:326
  42.1 1.1 %merge.1 = (f32[6,40,512]{2,1,0:T(8,128)}, f32[6,40,512]{2,1,0:T(8,128)}) custom-call(f32[2,12,40,128]{3,2,1,0:T(8,128)S(1)} %get-tuple-element.24.refs_0_, f32[2,12,40,128]{3,2,1,0:T(8,128)S(1)} %collective-permute-done.9.refs_1_), custom_call_target="tpu_custom_call" | custom-call | tf_op jit(solution)/shard_map/merge/pallas_call | solution.py:328
  (8 shorter events, 0.1 us)
Async XLA Ops:
  0.6 22.1 %copy-start = (f32[4,12,24]{2,1,0:T(8,128)S(1)}, f32[4,12,24]{2,1,0:T(8,128)}, u32[]{:S(2)}) copy-start(f32[4,12,24]{2,1,0:T(8,128)} %constant.3.clone.refs_2_) | copy-start | bytes 13828
  1.5 4.7 %collective-permute-start = (f32[1,32,128]{2,1,0:T(8,128)S(1)}, f32[1,32,128]{2,1,0:T(8,128)S(1)}, u32[]{:S(2)}, u32[]{:S(2)}) collective-permute-start(f32[1,32,128]{2,1,0:T(8,128)S(1)} %maximum_bitcast_fusion), channel_id=1, source_target_pairs={{0,1},{1,0},{2,3},{3,2},{4,5},{5,4},{6,7},{7,6},{8,9},{9,8},{10,11... | collective-permute-start | bytes 49160 | tf_op jit(solution)/shard_map/ppermute | solution.py:238
  6.3 4.0 %collective-permute-start.2 = (f32[2,32,128]{2,1,0:T(8,128)S(1)}, f32[2,32,128]{2,1,0:T(8,128)S(1)}, u32[]{:S(2)}, u32[]{:S(2)}) collective-permute-start(f32[2,32,128]{2,1,0:T(8,128)S(1)} %pad_maximum_fusion.2), channel_id=1, source_target_pairs={{0,4},{2,6},{4,0},{6,2},{1,5},{3,7},{5,1},{7,3},{8,12},{10,14},{12... | collective-permute-start | bytes 98312 | tf_op jit(solution)/shard_map/ppermute | solution.py:238
  10.3 6.4 %collective-permute-start.7 = (f32[4,32,128]{2,1,0:T(8,128)S(1)}, f32[4,32,128]{2,1,0:T(8,128)S(1)}, u32[]{:S(2)}, u32[]{:S(2)}) collective-permute-start(f32[4,32,128]{2,1,0:T(8,128)S(1)} %pad_maximum_fusion.1.refs_5_), channel_id=1, source_target_pairs={{0,24},{8,16},{16,8},{24,0},{1,25},{9,17},{17,9},{25,1},{2,26},{10... | collective-permute-start | bytes 196616 | tf_op jit(solution)/shard_map/ppermute | solution.py:245
  14.3 5.3 %collective-permute-start.6 = (f32[4,32,128]{2,1,0:T(8,128)S(1)}, f32[4,32,128]{2,1,0:T(8,128)S(1)}, u32[]{:S(2)}, u32[]{:S(2)}) collective-permute-start(f32[4,32,128]{2,1,0:T(8,128)S(1)} %pad_maximum_fusion.1.refs_5_), channel_id=1, source_target_pairs={{0,16},{8,24},{16,0},{24,8},{1,17},{9,25},{17,1},{25,9},{2,18},{10... | collective-permute-start | bytes 196616 | tf_op jit(solution)/shard_map/ppermute | solution.py:245
  14.3 7.2 %collective-permute-start.1 = (f32[40,8,128]{2,1,0:T(8,128)S(1)}, f32[40,8,128]{2,1,0:T(8,128)S(1)}, u32[]{:S(2)}, u32[]{:S(2)}) collective-permute-start(f32[40,8,128]{2,1,0:T(8,128)S(1)} %stack.11.source), channel_id=1, source_target_pairs={{0,4},{2,6},{4,0},{6,2},{1,5},{3,7},{5,1},{7,3},{8,12},{10,14},{12... | collective-permute-start | bytes 491528 | tf_op jit(solution)/shard_map/ppermute | solution.py:242
  15.8 4.5 %collective-permute-start.4 = (f32[4,32,128]{2,1,0:T(8,128)S(1)}, f32[4,32,128]{2,1,0:T(8,128)S(1)}, u32[]{:S(2)}, u32[]{:S(2)}) collective-permute-start(f32[4,32,128]{2,1,0:T(8,128)S(1)} %pad_maximum_fusion.1.refs_5_), channel_id=1, source_target_pairs={{0,8},{8,0},{16,24},{24,16},{1,9},{9,1},{17,25},{25,17},{2,10},{10... | collective-permute-start | bytes 196616 | tf_op jit(solution)/shard_map/ppermute | solution.py:245
  19.6 11.7 %collective-permute-start.8 = (f32[8,32,128]{2,1,0:T(8,128)S(1)}, f32[8,32,128]{2,1,0:T(8,128)S(1)}, u32[]{:S(2)}, u32[]{:S(2)}) collective-permute-start(f32[8,32,128]{2,1,0:T(8,128)S(1)} %pad_maximum_fusion), channel_id=1, source_target_pairs={{0,2},{2,0},{4,6},{6,4},{1,3},{3,1},{5,7},{7,5},{8,10},{10,8},{12,... | collective-permute-start | bytes 393224 | tf_op jit(solution)/shard_map/ppermute | solution.py:250
  19.7 3.0 %collective-permute-start.3 = (f32[4,32,128]{2,1,0:T(8,128)S(1)}, f32[4,32,128]{2,1,0:T(8,128)S(1)}, u32[]{:S(2)}, u32[]{:S(2)}) collective-permute-start(f32[4,32,128]{2,1,0:T(8,128)S(1)} %pad_maximum_fusion.1.refs_5_), channel_id=1, source_target_pairs={{0,2},{2,0},{4,6},{6,4},{1,3},{3,1},{5,7},{7,5},{8,10},{10,8},{12,... | collective-permute-start | bytes 196616 | tf_op jit(solution)/shard_map/ppermute | solution.py:249
  20.2 2.4 %collective-permute-start.5 = (f32[4,32,128]{2,1,0:T(8,128)S(1)}, f32[4,32,128]{2,1,0:T(8,128)S(1)}, u32[]{:S(2)}, u32[]{:S(2)}) collective-permute-start(f32[4,32,128]{2,1,0:T(8,128)S(1)} %collective-permute-done.4.refs_7_), channel_id=1, source_target_pairs={{0,2},{2,0},{4,6},{6,4},{1,3},{3,1},{5,7},{7,5},{8,10},{10,8},{12,... | collective-permute-start | bytes 196616 | tf_op jit(solution)/shard_map/ppermute | solution.py:249
  40.1 2.0 %collective-permute-start.9 = (f32[2,12,40,128]{3,2,1,0:T(8,128)S(1)}, f32[2,12,40,128]{3,2,1,0:T(8,128)S(1)}, u32[]{:S(2)}, u32[]{:S(2)}) collective-permute-start(f32[2,12,40,128]{3,2,1,0:T(8,128)S(1)} %get-tuple-element.25), channel_id=1, source_target_pairs={{0,2},{2,0},{4,6},{6,4},{1,3},{3,1},{5,7},{7,5},{8,10},{10,8},{12,... | collective-permute-start | bytes 1474568 | tf_op jit(solution)/shard_map/ppermute | solution.py:326

commit v5 on v4

v5 whole, which is shorter than its diff:
```python
import functools

import jax
import jax.numpy as jnp
import numpy as np
from jax import lax
from jax.experimental import pallas as pl
from jax.experimental.pallas import tpu as pltpu
from jax.sharding import PartitionSpec as P

NT = 8
TILE = 128
RADIUS = 0.4
EDGE = 4.0**0.2
SCALE = (EDGE / RADIUS) ** 2
FEATURES = 48
NEAR_ROWS = 0
VMEM_LIMIT = 16 * 1024 * 1024
BOTH_MINOR = (((1,), (1,)), ((), ()))
F32 = jnp.float32
BF16 = jnp.bfloat16


def spectral_rows(instances, groups):
    later = np.arange(instances)[:, None]
    earlier = np.arange(instances)[None, :]
    distance = (later - earlier).astype(np.float64)
    guarded = np.where(distance == 0, 0.5, np.pi * distance / instances)
    parity = np.where((later - earlier) % 2 == 0, 1.0, -1.0)
    matrix = np.where(distance == 0, 0.0, 0.5 * parity * np.cos(guarded) / np.sin(guarded))
    per = instances // groups
    rows = []
    for group in range(groups):
        own = slice(group * per, (group + 1) * per)
        rows.append(np.concatenate([np.eye(instances)[own], matrix[own]], axis=0))
    return np.stack([np.kron(block, np.eye(3)) for block in rows]).astype(np.float32)


def split3(value):
    high = value.astype(BF16).astype(F32)
    rest = value - high
    middle = rest.astype(BF16).astype(F32)
    return high, middle, rest - middle


def flip(size, bit):
    return [(i, i ^ bit) for i in range(size)]


def bits_of(size):
    return [1 << b for b in range(size.bit_length() - 1)]


def cell_prep_kernel(source, *refs, rows, plane, sizes, masks):
    feature_ref, coord_ref, place_ref = refs[-4:-1] if len(refs) == 5 else refs
    if len(refs) == 5:
        mix_ref, mixed_ref = refs[0], refs[-1]
        inst = lax.axis_index("inst")
        mixed_ref[...] = jnp.concatenate([mix_ref[inst], mix_ref[inst ^ 1]], axis=0)
    n_inst, n_cell = sizes["inst"], sizes["cell"]
    device = (lax.axis_index("blade") * n_inst + lax.axis_index("inst")) * n_cell + lax.axis_index("cell")
    row_id = lax.broadcasted_iota(jnp.int32, (8, TILE), 0)
    diagonal = lax.broadcasted_iota(jnp.int32, (TILE, TILE), 0) == lax.broadcasted_iota(jnp.int32, (TILE, TILE), 1)
    identity = jnp.where(diagonal, 1.0, 0.0).astype(BF16)

    def one_row(r, carry):
        value = source[r]
        coord_ref[pl.ds(r, 8, stride=rows), :] = value
        centred = jnp.where(row_id < 3, value - 0.5, 0.0)
        length = SCALE * jnp.sum(centred * centred, axis=0, keepdims=True)
        value = jnp.where(row_id == 3, 1.0, jnp.where(row_id == 4, length, centred))
        high, middle, low = split3(value)
        stacked = jnp.concatenate([high, middle, low, high, middle, high], axis=0).astype(BF16)
        turned = lax.dot_general(identity, stacked, BOTH_MINOR, preferred_element_type=F32)
        feature_ref[r] = turned.astype(BF16)
        return carry

    lax.fori_loop(0, rows, one_row, 0, unroll=8)
    tile = coord_ref[3 * rows : 4 * rows, :].T[:8].astype(jnp.int32)
    if masks is not None:
        tile = tile ^ device
        places = [(lax.shift_right_logical(tile, m) & 1) << k for k, m in enumerate(masks)]
        tile = functools.reduce(lambda x, y: x | y, places)
    else:
        tile = tile & (plane - 1)
    place_ref[:, :rows] = tile


def sums_kernel(*refs, rows, start, count, slots, half, first, prepare, before_spans, share):
    last = len(before_spans) > 0
    refs = list(refs)

    def take(n):
        taken = refs[:n]
        del refs[:n]
        return taken

    list_refs, (mix_ref,), feature_refs = take(slots), take(1), take(slots)
    coord_refs, before_refs = (take(slots), take(len(before_spans))) if last else ([], [])
    block_refs = take(prepare)
    tables = [] if prepare else take(2)
    own_ref, peer_ref = take(2) if last else (None, None)
    total_ref = None if last else take(1)[0]
    tables = tables or take(2)
    if last:
        (total_ref,) = take(1)
    centre_ref, coef_ref = tables
    dist_ref, weight_ref = refs
    combos = 2 * half
    plane = centre_ref.shape[0] // 2
    row_id = lax.broadcasted_iota(jnp.int32, (8, TILE), 0)
    blade = lax.axis_index("blade")
    terms = [blade ^ first, blade ^ (first + 1)]

    base = 0
    for block_ref in block_refs:

        def one_tile(p, carry, block_ref=block_ref, base=base):
            value = block_ref[p, 3 * NT : 3 * NT + 8, :]
            centred = jnp.where(row_id < 3, value - 0.5, 0.0)
            length = SCALE * jnp.sum(centred * centred, axis=0, keepdims=True)
            value = jnp.where(row_id == 3, length, jnp.where(row_id == 4, 1.0, (-2.0 * SCALE) * centred))
            high, middle, low = split3(value)
            stacked = jnp.concatenate([high, high, high, middle, middle, low], axis=0)
            centre_ref[base + p] = stacked.astype(BF16)
            mixed = jnp.dot(
                mix_ref[...], block_ref[p, : 3 * NT, :],
                preferred_element_type=F32, precision=lax.Precision.HIGHEST,
            )
            mixed_high = mixed.astype(BF16).astype(F32)
            coef_ref[base + p] = jnp.concatenate([mixed_high, mixed - mixed_high], axis=0).astype(BF16)
            return carry

        lax.fori_loop(0, block_ref.shape[0], one_tile, 0, unroll=4)
        base += block_ref.shape[0]

    units = [(slot, k) for slot in range(slots) for k in range(2)]
    n_units = len(units)
    groups = count // 2

    def unit_of(group, unit):
        slot, k = units[unit]
        r = 2 * group + k
        lists = list_refs[slot]
        return slot, r, lists[terms[0], start + r], lists[terms[1], start + r] + plane

    def distances(group, unit):
        slot, r, a, b = unit_of(group, unit)
        dist_ref[unit] = jnp.dot(
            feature_refs[slot][start + r], jnp.concatenate([centre_ref[a], centre_ref[b]], axis=1),
            preferred_element_type=F32,
        )

    def weights(unit):
        squared = jnp.maximum(dist_ref[unit], 1e-12)
        margin = jnp.maximum(EDGE - squared * lax.rsqrt(squared), 0.0)
        margin_sq = margin * margin
        weight = (margin_sq * margin_sq) * (1.25 * EDGE - margin)
        high = weight.astype(BF16)
        weight_ref[unit, :TILE] = high
        weight_ref[unit, TILE:] = (weight - high.astype(F32)).astype(BF16)

    def contract(group, unit):
        slot, r, a, b = unit_of(group, unit)
        total = lax.dot_general(
            jnp.concatenate([coef_ref[a], coef_ref[b]], axis=1), weight_ref[unit], BOTH_MINOR,
            preferred_element_type=F32,
        )
        total = total[:combos, :TILE] + total[combos:, :TILE] + total[:combos, TILE:]
        for part in range(combos // 8):
            total_ref[slot, pl.ds(r + part * 8 * count, 8, stride=count), :] = total[part * 8 : part * 8 + 8]

    for unit in range(n_units - 1):
        distances(0, unit)

    def one_group(group, carry):
        before = jnp.maximum(group - 1, 0)
        after = jnp.minimum(group + 1, groups - 1)
        for unit in range(n_units):
            if unit < 2:
                contract(before, unit + n_units - 2)
            else:
                contract(group, unit - 2)
            if unit == 0:
                distances(group, n_units - 1)
            else:
                distances(after, unit - 1)
            weights(unit)
        return carry

    lax.fori_loop(0, groups, one_group, 0, unroll=max(n for n in range(1, 11) if groups % n == 0))
    for unit in range(n_units - 2, n_units):
        contract(groups - 1, unit)
    if not last:
        return

    shifts = half // 2
    for slot in range(slots):
        for out, first_row in ((own_ref, 0), (peer_ref, half)):
            for c in range(half):
                for before_ref, (begin, size) in zip(before_refs, before_spans):
                    row = (first_row + c) * count + begin
                    value = total_ref[slot, row : row + size, :]
                    value = value + before_ref[slot, (first_row + c) * size : (first_row + c + 1) * size, :]
                    if c < shifts:
                        row = (c % 3) * rows + start + begin
                        value = value + coord_refs[slot][row : row + size, :]
                    out[slot, c, begin : begin + size] = value


def merge_kernel(own_ref, peer_ref, moved_ref, velocity_ref, *, slots, half):
    shifts = half // 2
    inst = lax.axis_index("inst")
    for which, source in enumerate((own_ref, peer_ref)):
        for slot in range(slots):
            lane = pl.multiple_of((inst ^ which ^ (2 * slot)) * TILE, TILE)
            moved_ref[:, :, pl.ds(lane, TILE)] = source[slot, :shifts]
            velocity_ref[:, :, pl.ds(lane, TILE)] = source[slot, shifts:]


def in_vmem(value):
    return pltpu.with_memory_space_constraint(value, pltpu.VMEM)


def vmem():
    return pl.BlockSpec(memory_space=pltpu.VMEM)


def smem():
    return pl.BlockSpec(memory_space=pltpu.SMEM)


def on_device(cell_coords, centre_points, coefficients, tile_lists, *, sizes):
    n_blade, n_inst, n_cell = sizes["blade"], sizes["inst"], sizes["cell"]
    rows = cell_coords.shape[1]
    terms = tile_lists.shape[2]
    width = centre_points.shape[1]
    slots = n_inst // 2
    half = 2 * 3 * (NT // n_inst)
    block = jnp.concatenate([coefficients, centre_points, jnp.zeros((5, width), F32)], axis=0)
    list_row = jnp.pad(tile_lists[:, 0, :].astype(F32), ((0, 0), (0, TILE - terms)))
    blank = jnp.zeros_like(list_row)
    cell_rows = jnp.stack([cell_coords[0], cell_coords[1], cell_coords[2], list_row] + [blank] * 4, axis=1)

    core = 1
    inner = [("cell", n_cell, b, b) for b in bits_of(n_cell)]
    inner += [("inst", n_inst, b, b * n_cell) for b in bits_of(n_inst) if b != core]
    masks = [mask.bit_length() - 1 for _, _, _, mask in inner] + [(core * n_cell).bit_length() - 1]

    half_plane = block[None]
    for index, (axis, size, bit, _) in enumerate(inner):
        arrived = lax.ppermute(half_plane, axis, flip(size, bit))
        if index == 0:
            arrived, cell_rows = lax.optimization_barrier((arrived, cell_rows))
        half_plane = jnp.concatenate([half_plane, arrived], axis=0)
    others = [lax.ppermute(cell_rows, "inst", flip(n_inst, 2 * s)) for s in range(1, slots)]
    halves = [half_plane]
    for m in range(1, n_blade):
        halves.append(lax.ppermute(half_plane, "blade", flip(n_blade, m)))

    swapped = []
    for m in range(2):
        swapped.append(lax.ppermute(halves[m], "inst", flip(n_inst, core)))
    late = lax.ppermute(jnp.concatenate(halves[2:], axis=0), "inst", flip(n_inst, core))
    swapped += jnp.split(late, n_blade - 2, axis=0)

    if width < TILE:
        device = lax.axis_index("inst") * n_cell + lax.axis_index("cell")
        relative = jnp.arange(n_inst * n_cell) ^ device
        order = sum(((relative >> m) & 1) << k for k, m in enumerate(masks))

        def whole_plane(mine, theirs):
            blocks = jnp.take(jnp.concatenate([mine, theirs], axis=0), order, axis=0)
            blocks = blocks.reshape(-1, TILE // width, 3 * NT + 8, width)
            return [jnp.moveaxis(blocks, 1, 2).reshape(-1, 3 * NT + 8, TILE)]

        plane = n_inst * n_cell * width // TILE
    else:
        def whole_plane(mine, theirs):
            return [mine, theirs]

        plane = n_inst * n_cell
    planes = [whole_plane(*pair) for pair in zip(halves, swapped)]

    params = pltpu.CompilerParams(vmem_limit_bytes=VMEM_LIMIT)

    def cell_prep(cells, *mix):
        out = (
            pltpu.VMEM((rows, TILE, FEATURES), BF16),
            pltpu.VMEM((8 * rows, TILE), F32),
            jax.ShapeDtypeStruct((8, TILE), jnp.int32),
        ) + ((pltpu.VMEM((2 * half, 3 * NT), F32),) if mix else ())
        return pl.pallas_call(
            functools.partial(
                cell_prep_kernel, rows=rows, plane=plane, sizes=sizes, masks=masks if width == TILE else None
            ),
            out_shape=out,
            in_specs=[vmem()] * (1 + len(mix)),
            out_specs=(vmem(),) * len(out),
            compiler_params=params,
            name="cell_prep",
        )(in_vmem(cells), *mix)

    *own_cells, mix = cell_prep(cell_rows, jnp.asarray(spectral_rows(NT, n_inst)))
    prepared = [own_cells]
    prepared += [cell_prep(cells) for cells in others]
    features, coords, places = map(list, zip(*prepared))

    def sums(first, start, count, before=(), before_spans=(), given=(), share=False):
        last = len(before) > 0
        blocks = [] if given else planes[first] + planes[first + 1]
        total = pltpu.VMEM((slots, 2 * half * count, TILE), F32)
        tables = [pltpu.VMEM((2 * plane, n, TILE), BF16) for n in (FEATURES, 4 * half)]
        out = [pltpu.VMEM((slots, half, count, TILE), F32)] * 2 if last else [total]
        scratch = [] if given or share else tables
        operands = [mix, *features, *(coords if last else []), *before, *blocks, *given]
        return pl.pallas_call(
            functools.partial(
                sums_kernel, rows=rows, start=start, count=count, slots=slots, half=half, first=first,
                prepare=len(blocks), before_spans=before_spans, share=share,
            ),
            out_shape=tuple(out + (tables if share else [])),
            in_specs=[smem()] * slots + [vmem()] * len(operands),
            out_specs=(vmem(),) * (len(out) + (2 if share else 0)),
            scratch_shapes=scratch
            + ([total] if last else [])
            + [pltpu.VMEM((2 * slots, TILE, 2 * TILE), F32), pltpu.VMEM((2 * slots, 2 * TILE, 2 * TILE), BF16)],
            compiler_params=params,
        )(*places, *map(in_vmem, operands))

    spans = [(0, rows)] if NEAR_ROWS == 0 else [(0, NEAR_ROWS), (NEAR_ROWS, rows - NEAR_ROWS)]
    before, tables = [], []
    for start, count in spans:
        part, *made = sums(0, start, count, given=tables, share=len(spans) > 1 and not tables)
        before, tables = before + [part], tables or made
    own, peer = sums(2, 0, rows, before=before, before_spans=spans)
    received = lax.ppermute(peer, "inst", flip(n_inst, core))
    out = jax.ShapeDtypeStruct((half // 2, rows, n_inst * TILE), F32)
    moved, velocity = pl.pallas_call(
        functools.partial(merge_kernel, slots=slots, half=half),
        out_shape=(out, out),
        in_specs=[vmem()] * 2,
        out_specs=(vmem(), vmem()),
        compiler_params=params,
        name="merge",
    )(in_vmem(own), in_vmem(received))
    shape = (NT // n_inst, 3, rows, n_inst * TILE)
    return (moved.reshape(shape), velocity.reshape(shape))


def solution(mesh):
    sizes = dict(mesh.shape)
    in_specs = (
        P(None, ("blade", "cell"), "inst"),
        P(None, ("blade", "inst", "cell")),
        P(None, ("blade", "inst", "cell")),
        P(("blade", "cell"), "inst", None),
    )
    out_specs = (P("inst", None, ("blade", "cell"), None), P("inst", None, ("blade", "cell"), None))
    return jax.shard_map(
        functools.partial(on_device, sizes=sizes),
        mesh=mesh, in_specs=in_specs, out_specs=out_specs, check_vma=False,
    )
```

time: 43.4 us -> 39.9 us (0.919)
  Pallas kernels: 20.9 us -> 16.4 us
  local copies, waits for them, and re-layouts: 1.81 us -> 2.56 us
    pallas_call x2, Pallas kernels: 17.4 us -> 12.9 us  [sums(): pl.pallas_call(functools.partial(sums_kernel, rows=rows, start=start, cou...]
    unnamed x3, local copies, waits for them, and re-layouts: 0.77 us -> 1.52 us
  transfers between devices with their start and end apart: 10 -> 10, of which waited for: 5 -> 5; matrix products, arithmetic and copies ran while one was open for 4% -> 4% of each run, Pallas kernels for 26% -> 22%
where the time goes in v5:
time: 39.9 us; the launch traced here: 39.6 us
  Pallas kernels  16.4 us (41%)
  starting transfers between devices  12.4 us (31%)
  waiting for transfers between devices  6.64 us (17%)
  local copies, waits for them, and re-layouts  2.56 us (6%)
  other arithmetic  0.82 us (2%)
  between operations  0.74 us (2%)
    pallas_call x2, Pallas kernels, sums(): pl.pallas_call(functools.partial(sums_kernel, rows=rows, start=start, cou...  12.9 us
    ppermute x2, starting transfers between devices, on_device(): arrived = lax.ppermute(half_plane, axis, flip(size, bit))  4.94 us
    ppermute x3, starting transfers between devices, on_device(): halves.append(lax.ppermute(half_plane, 'blade', flip(n_blade, m)))  4.78 us
    ppermute x3, waiting for transfers between devices, on_device(): halves.append(lax.ppermute(half_plane, 'blade', flip(n_blade, m)))  3.11 us
    pallas_call x2, Pallas kernels, cell_prep(): pl.pallas_call(functools.partial(cell_prep_kernel, rows=rows, plane=plane...  2.42 us
    ppermute x2, waiting for transfers between devices, on_device(): arrived = lax.ppermute(half_plane, axis, flip(size, bit))  2.04 us
    unnamed x3, local copies, waits for them, and re-layouts  1.52 us
    ppermute x1, starting transfers between devices, on_device(): lax.ppermute(cell_rows, 'inst', flip(n_inst, 2 * s))  1.49 us
  transfers between devices with their start and end apart: 10, of which 5 were waited for; matrix products, arithmetic and copies ran while one was open for 4% of the time, Pallas kernels for 22%

profile of v5, /device:TPU:0, one launch (start us, length us, event | category | flops | bytes accessed | tf_op | source)
XLA Modules:
  0.0 39.6 jit_solution(5457267797661627914)
XLA Ops:
  0.6 0.1 pad.14.clone
  0.7 0.8 %maximum_bitcast_fusion = f32[1,32,128]{2,1,0:T(8,128)S(1)} fusion(f32[3,128]{1,0:T(4,128)} %param.6, f32[24,128]{1,0:T(8,128)} %param.7, f32[32]{0:T(128)S(1)} %pad.14.clone), kind=kLoop, calls=%fused_computation.4 | loop fusion | flops 8192 | bytes 30336 | tf_op jit(solution)/shard_map/broadcast_in_dim | solution.py:250
  1.5 3.0 %collective-permute-start = (f32[1,32,128]{2,1,0:T(8,128)S(1)}, f32[1,32,128]{2,1,0:T(8,128)S(1)}, u32[]{:S(2)}, u32[]{:S(2)}) collective-permute-start(f32[1,32,128]{2,1,0:T(8,128)S(1)} %maximum_bitcast_fusion), channel_id=1, source_target_pairs={{0,1},{1,0},{2,3},{3,2},{4,5},{5,4},{6,7},{7,6},{8,9},{9,8},{10,11... | collective-permute-start | bytes 49160 | tf_op jit(solution)/shard_map/ppermute | solution.py:252
  4.5 0.8 %copy.7 = s32[40,1,4]{2,0,1:T(8,128)S(1)} copy(s32[40,1,4]{0,2,1:T(4,128)} %param.8) | data formatting | bytes 1280 | tf_op args[3]
  5.3 0.8 %fusion.1 = (f32[1,40,128]{2,1,0:T(8,128)S(1)}, f32[1,40,128]{2,1,0:T(8,128)S(1)}, f32[1,40,128]{2,1,0:T(8,128)S(1)}) fusion(f32[3,40,128]{2,1,0:T(8,128)} %param.5), kind=kLoop, calls=%fused_computation.6 | loop fusion | bytes 122880 | tf_op jit(solution)/shard_map/slice | solution.py:243
  6.1 0.2 stack.11.source
  6.2 0.0 collective-permute-done
  6.3 1.9 %collective-permute-start.2 = (f32[2,32,128]{2,1,0:T(8,128)S(1)}, f32[2,32,128]{2,1,0:T(8,128)S(1)}, u32[]{:S(2)}, u32[]{:S(2)}) collective-permute-start(f32[2,32,128]{2,1,0:T(8,128)S(1)} %pad_maximum_fusion.2), channel_id=1, source_target_pairs={{0,4},{2,6},{4,0},{6,2},{1,5},{3,7},{5,1},{7,3},{8,12},{10,14},{12... | collective-permute-start | bytes 98312 | tf_op jit(solution)/shard_map/ppermute | solution.py:252
  8.2 2.0 %collective-permute-done.2 = f32[2,32,128]{2,1,0:T(8,128)S(1)} collective-permute-done((f32[2,32,128]{2,1,0:T(8,128)S(1)}, f32[2,32,128]{2,1,0:T(8,128)S(1)}, u32[]{:S(2)}, u32[]{:S(2)}) %collective-permute-start.2) | collective-permute-done | bytes 32800 | tf_op jit(solution)/shard_map/ppermute | solution.py:252
  10.3 4.0 %collective-permute-start.7 = (f32[4,32,128]{2,1,0:T(8,128)S(1)}, f32[4,32,128]{2,1,0:T(8,128)S(1)}, u32[]{:S(2)}, u32[]{:S(2)}) collective-permute-start(f32[4,32,128]{2,1,0:T(8,128)S(1)} %pad_maximum_fusion.1.refs_5_), channel_id=1, source_target_pairs={{0,24},{8,16},{16,8},{24,0},{1,25},{9,17},{17,9},{25,1},{2,26},{10... | collective-permute-start | bytes 196616 | tf_op jit(solution)/shard_map/ppermute | solution.py:259
  14.3 0.0 collective-permute-start.6
  14.3 1.5 %collective-permute-start.1 = (f32[40,8,128]{2,1,0:T(8,128)S(1)}, f32[40,8,128]{2,1,0:T(8,128)S(1)}, u32[]{:S(2)}, u32[]{:S(2)}) collective-permute-start(f32[40,8,128]{2,1,0:T(8,128)S(1)} %stack.11.source), channel_id=1, source_target_pairs={{0,4},{2,6},{4,0},{6,2},{1,5},{3,7},{5,1},{7,3},{8,12},{10,14},{12... | collective-permute-start | bytes 491528 | tf_op jit(solution)/shard_map/ppermute | solution.py:256
  15.7 0.8 %collective-permute-start.4 = (f32[4,32,128]{2,1,0:T(8,128)S(1)}, f32[4,32,128]{2,1,0:T(8,128)S(1)}, u32[]{:S(2)}, u32[]{:S(2)}) collective-permute-start(f32[4,32,128]{2,1,0:T(8,128)S(1)} %pad_maximum_fusion.1.refs_5_), channel_id=1, source_target_pairs={{0,8},{8,0},{16,24},{24,16},{1,9},{9,1},{17,25},{25,17},{2,10},{10... | collective-permute-start | bytes 196616 | tf_op jit(solution)/shard_map/ppermute | solution.py:259
  16.5 0.1 collective-permute-done.7.refs_10_
  16.6 2.9 %collective-permute-done.6.refs_8_ = f32[4,32,128]{2,1,0:T(8,128)S(1)} collective-permute-done((f32[4,32,128]{2,1,0:T(8,128)S(1)}, f32[4,32,128]{2,1,0:T(8,128)S(1)}, u32[]{:S(2)}, u32[]{:S(2)}) %collective-permute-start.6) | collective-permute-done | bytes 65568 | tf_op jit(solution)/shard_map/ppermute | solution.py:259
  19.6 0.1 collective-permute-start.8
  19.6 0.5 %collective-permute-start.3 = (f32[4,32,128]{2,1,0:T(8,128)S(1)}, f32[4,32,128]{2,1,0:T(8,128)S(1)}, u32[]{:S(2)}, u32[]{:S(2)}) collective-permute-start(f32[4,32,128]{2,1,0:T(8,128)S(1)} %pad_maximum_fusion.1.refs_5_), channel_id=1, source_target_pairs={{0,2},{2,0},{4,6},{6,4},{1,3},{3,1},{5,7},{7,5},{8,10},{10,8},{12,... | collective-permute-start | bytes 196616 | tf_op jit(solution)/shard_map/ppermute | solution.py:263
  20.1 0.1 collective-permute-done.4.refs_7_
  20.2 0.0 collective-permute-start.5
  20.2 0.0 copy-start
  20.2 0.8 %copy-done = f32[4,12,24]{2,1,0:T(8,128)S(1)} copy-done((f32[4,12,24]{2,1,0:T(8,128)S(1)}, f32[4,12,24]{2,1,0:T(8,128)}, u32[]{:S(2)}) %copy-start) | copy-done | bytes 4632
  21.0 1.2 %cell_prep.2 = (bf16[40,128,48]{2,1,0:T(8,128)(2,1)S(1)}, f32[320,128]{1,0:T(8,128)S(1)}, s32[8,128]{1,0:T(8,128)S(1)}, f32[24,24]{1,0:T(8,128)S(1)}) custom-call(f32[40,8,128]{2,1,0:T(8,128)S(1)} %stack.11.source, f32[4,12,24]{2,1,0:T(8,128)S(1)} %copy-done), custom_call_target="tpu_custom_call" | custom-call | tf_op jit(solution)/shard_map/cell_prep/pallas_call | solution.py:293
  22.2 0.0 collective-permute-done.1.source
  22.2 1.2 %cell_prep.3 = (bf16[40,128,48]{2,1,0:T(8,128)(2,1)S(1)}, f32[320,128]{1,0:T(8,128)S(1)}, s32[8,128]{1,0:T(8,128)S(1)}) custom-call(f32[40,8,128]{2,1,0:T(8,128)S(1)} %collective-permute-done.1.source), custom_call_target="tpu_custom_call" | custom-call | tf_op jit(solution)/shard_map/cell_prep/pallas_call | solution.py:293
  23.4 0.0 collective-permute-done.3.refs_6_
  23.4 0.0 collective-permute-done.5.refs_8_
  23.4 6.5 %shard_map.68.refs_7_ = f32[2,960,128]{2,1,0:T(8,128)S(1)} custom-call(s32[8,128]{1,0:T(8,128)S(1)} %get-tuple-element.16.refs_0_, s32[8,128]{1,0:T(8,128)S(1)} %get-tuple-element.17.refs_1_, f32[24,24]{1,0:T(8,128)S(1)} %get-tuple-element.18.refs_2_, bf16[40,128,48]{2,1,0:T(8,128)(2,1)S(1)} %get-tuple-element.19.refs_3_, ...), custom_call_target="tpu_custom_call" | custom-call | tf_op jit(solution)/shard_map/pallas_call | solution.py:317
  29.9 0.0 collective-permute-done.8
  29.9 6.5 %shard_map.69 = (f32[2,12,40,128]{3,2,1,0:T(8,128)S(1)}, f32[2,12,40,128]{3,2,1,0:T(8,128)S(1)}) custom-call(s32[8,128]{1,0:T(8,128)S(1)} %get-tuple-element.16.refs_0_, s32[8,128]{1,0:T(8,128)S(1)} %get-tuple-element.17.refs_1_, f32[24,24]{1,0:T(8,128)S(1)} %get-tuple-element.18.refs_2_, bf16[40,128,48]{2,1,0:T(8,128)(2,1)S(1)} %get-tuple-element.19.refs_3_, ...), custom_call_target="tpu_custom_call" | custom-call | tf_op jit(solution)/shard_map/pallas_call | solution.py:317
  36.4 0.6 %collective-permute-start.9 = (f32[2,12,40,128]{3,2,1,0:T(8,128)S(1)}, f32[2,12,40,128]{3,2,1,0:T(8,128)S(1)}, u32[]{:S(2)}, u32[]{:S(2)}) collective-permute-start(f32[2,12,40,128]{3,2,1,0:T(8,128)S(1)} %get-tuple-element.25), channel_id=1, source_target_pairs={{0,2},{2,0},{4,6},{6,4},{1,3},{3,1},{5,7},{7,5},{8,10},{10,8},{12,... | collective-permute-start | bytes 1474568 | tf_op jit(solution)/shard_map/ppermute | solution.py:337
  37.0 1.5 %collective-permute-done.9.peer_ref = f32[2,12,40,128]{3,2,1,0:T(8,128)S(1)} collective-permute-done((f32[2,12,40,128]{3,2,1,0:T(8,128)S(1)}, f32[2,12,40,128]{3,2,1,0:T(8,128)S(1)}, u32[]{:S(2)}, u32[]{:S(2)}) %collective-permute-start.9) | collective-permute-done | bytes 491552 | tf_op jit(solution)/shard_map/ppermute | solution.py:337
  38.5 1.1 %merge.1 = (f32[6,40,512]{2,1,0:T(8,128)}, f32[6,40,512]{2,1,0:T(8,128)}) custom-call(f32[2,12,40,128]{3,2,1,0:T(8,128)S(1)} %get-tuple-element.24.own_ref, f32[2,12,40,128]{3,2,1,0:T(8,128)S(1)} %collective-permute-done.9.peer_ref), custom_call_target="tpu_custom_call" | custom-call | tf_op jit(solution)/shard_map/merge/pallas_call | solution.py:339
  (8 shorter events, 0.1 us)
Async XLA Ops:
  1.5 4.7 %collective-permute-start = (f32[1,32,128]{2,1,0:T(8,128)S(1)}, f32[1,32,128]{2,1,0:T(8,128)S(1)}, u32[]{:S(2)}, u32[]{:S(2)}) collective-permute-start(f32[1,32,128]{2,1,0:T(8,128)S(1)} %maximum_bitcast_fusion), channel_id=1, source_target_pairs={{0,1},{1,0},{2,3},{3,2},{4,5},{5,4},{6,7},{7,6},{8,9},{9,8},{10,11... | collective-permute-start | bytes 49160 | tf_op jit(solution)/shard_map/ppermute | solution.py:252
  6.3 4.0 %collective-permute-start.2 = (f32[2,32,128]{2,1,0:T(8,128)S(1)}, f32[2,32,128]{2,1,0:T(8,128)S(1)}, u32[]{:S(2)}, u32[]{:S(2)}) collective-permute-start(f32[2,32,128]{2,1,0:T(8,128)S(1)} %pad_maximum_fusion.2), channel_id=1, source_target_pairs={{0,4},{2,6},{4,0},{6,2},{1,5},{3,7},{5,1},{7,3},{8,12},{10,14},{12... | collective-permute-start | bytes 98312 | tf_op jit(solution)/shard_map/ppermute | solution.py:252
  10.3 6.4 %collective-permute-start.7 = (f32[4,32,128]{2,1,0:T(8,128)S(1)}, f32[4,32,128]{2,1,0:T(8,128)S(1)}, u32[]{:S(2)}, u32[]{:S(2)}) collective-permute-start(f32[4,32,128]{2,1,0:T(8,128)S(1)} %pad_maximum_fusion.1.refs_5_), channel_id=1, source_target_pairs={{0,24},{8,16},{16,8},{24,0},{1,25},{9,17},{17,9},{25,1},{2,26},{10... | collective-permute-start | bytes 196616 | tf_op jit(solution)/shard_map/ppermute | solution.py:259
  14.3 5.3 %collective-permute-start.6 = (f32[4,32,128]{2,1,0:T(8,128)S(1)}, f32[4,32,128]{2,1,0:T(8,128)S(1)}, u32[]{:S(2)}, u32[]{:S(2)}) collective-permute-start(f32[4,32,128]{2,1,0:T(8,128)S(1)} %pad_maximum_fusion.1.refs_5_), channel_id=1, source_target_pairs={{0,16},{8,24},{16,0},{24,8},{1,17},{9,25},{17,1},{25,9},{2,18},{10... | collective-permute-start | bytes 196616 | tf_op jit(solution)/shard_map/ppermute | solution.py:259
  14.3 7.9 %collective-permute-start.1 = (f32[40,8,128]{2,1,0:T(8,128)S(1)}, f32[40,8,128]{2,1,0:T(8,128)S(1)}, u32[]{:S(2)}, u32[]{:S(2)}) collective-permute-start(f32[40,8,128]{2,1,0:T(8,128)S(1)} %stack.11.source), channel_id=1, source_target_pairs={{0,4},{2,6},{4,0},{6,2},{1,5},{3,7},{5,1},{7,3},{8,12},{10,14},{12... | collective-permute-start | bytes 491528 | tf_op jit(solution)/shard_map/ppermute | solution.py:256
  15.7 4.5 %collective-permute-start.4 = (f32[4,32,128]{2,1,0:T(8,128)S(1)}, f32[4,32,128]{2,1,0:T(8,128)S(1)}, u32[]{:S(2)}, u32[]{:S(2)}) collective-permute-start(f32[4,32,128]{2,1,0:T(8,128)S(1)} %pad_maximum_fusion.1.refs_5_), channel_id=1, source_target_pairs={{0,8},{8,0},{16,24},{24,16},{1,9},{9,1},{17,25},{25,17},{2,10},{10... | collective-permute-start | bytes 196616 | tf_op jit(solution)/shard_map/ppermute | solution.py:259
  19.6 10.3 %collective-permute-start.8 = (f32[8,32,128]{2,1,0:T(8,128)S(1)}, f32[8,32,128]{2,1,0:T(8,128)S(1)}, u32[]{:S(2)}, u32[]{:S(2)}) collective-permute-start(f32[8,32,128]{2,1,0:T(8,128)S(1)} %pad_maximum_fusion), channel_id=1, source_target_pairs={{0,2},{2,0},{4,6},{6,4},{1,3},{3,1},{5,7},{7,5},{8,10},{10,8},{12,... | collective-permute-start | bytes 393224 | tf_op jit(solution)/shard_map/ppermute | solution.py:264
  19.6 3.8 %collective-permute-start.3 = (f32[4,32,128]{2,1,0:T(8,128)S(1)}, f32[4,32,128]{2,1,0:T(8,128)S(1)}, u32[]{:S(2)}, u32[]{:S(2)}) collective-permute-start(f32[4,32,128]{2,1,0:T(8,128)S(1)} %pad_maximum_fusion.1.refs_5_), channel_id=1, source_target_pairs={{0,2},{2,0},{4,6},{6,4},{1,3},{3,1},{5,7},{7,5},{8,10},{10,8},{12,... | collective-permute-start | bytes 196616 | tf_op jit(solution)/shard_map/ppermute | solution.py:263
  20.2 3.2 %collective-permute-start.5 = (f32[4,32,128]{2,1,0:T(8,128)S(1)}, f32[4,32,128]{2,1,0:T(8,128)S(1)}, u32[]{:S(2)}, u32[]{:S(2)}) collective-permute-start(f32[4,32,128]{2,1,0:T(8,128)S(1)} %collective-permute-done.4.refs_7_), channel_id=1, source_target_pairs={{0,2},{2,0},{4,6},{6,4},{1,3},{3,1},{5,7},{7,5},{8,10},{10,8},{12,... | collective-permute-start | bytes 196616 | tf_op jit(solution)/shard_map/ppermute | solution.py:263
  20.2 0.8 %copy-start = (f32[4,12,24]{2,1,0:T(8,128)S(1)}, f32[4,12,24]{2,1,0:T(8,128)}, u32[]{:S(2)}) copy-start(f32[4,12,24]{2,1,0:T(8,128)} %constant.3.clone.refs_0_) | copy-start | bytes 13828
  36.4 2.1 %collective-permute-start.9 = (f32[2,12,40,128]{3,2,1,0:T(8,128)S(1)}, f32[2,12,40,128]{3,2,1,0:T(8,128)S(1)}, u32[]{:S(2)}, u32[]{:S(2)}) collective-permute-start(f32[2,12,40,128]{3,2,1,0:T(8,128)S(1)} %get-tuple-element.25), channel_id=1, source_target_pairs={{0,2},{2,0},{4,6},{6,4},{1,3},{3,1},{5,7},{7,5},{8,10},{10,8},{12,... | collective-permute-start | bytes 1474568 | tf_op jit(solution)/shard_map/ppermute | solution.py:337

commit v6 on v5

--- a/solution.py
+++ b/solution.py
@@ -14,7 +14,7 @@
 EDGE = 4.0**0.2
 SCALE = (EDGE / RADIUS) ** 2
 FEATURES = 48
-NEAR_ROWS = 0
+NEAR_ROWS = 24
 VMEM_LIMIT = 16 * 1024 * 1024
 BOTH_MINOR = (((1,), (1,)), ((), ()))
 F32 = jnp.float32
@@ -52,6 +52,7 @@
 
 
 def cell_prep_kernel(source, *refs, rows, plane, sizes, masks):
+    *refs, staged_ref, sem = refs
     feature_ref, coord_ref, place_ref = refs[-4:-1] if len(refs) == 5 else refs
     if len(refs) == 5:
         mix_ref, mixed_ref = refs[0], refs[-1]
@@ -62,6 +63,17 @@
     row_id = lax.broadcasted_iota(jnp.int32, (8, TILE), 0)
     diagonal = lax.broadcasted_iota(jnp.int32, (TILE, TILE), 0) == lax.broadcasted_iota(jnp.int32, (TILE, TILE), 1)
     identity = jnp.where(diagonal, 1.0, 0.0).astype(BF16)
+
+    tile = source[:, 3, :].T[:8].astype(jnp.int32)
+    if masks is not None:
+        tile = tile ^ device
+        places = [(lax.shift_right_logical(tile, m) & 1) << k for k, m in enumerate(masks)]
+        tile = functools.reduce(lambda x, y: x | y, places)
+    else:
+        tile = tile & (plane - 1)
+    staged_ref[:, :rows] = tile
+    staged = pltpu.make_async_copy(staged_ref, place_ref, sem)
+    staged.start()
 
     def one_row(r, carry):
         value = source[r]
@@ -76,14 +88,7 @@
         return carry
 
     lax.fori_loop(0, rows, one_row, 0, unroll=8)
-    tile = coord_ref[3 * rows : 4 * rows, :].T[:8].astype(jnp.int32)
-    if masks is not None:
-        tile = tile ^ device
-        places = [(lax.shift_right_logical(tile, m) & 1) << k for k, m in enumerate(masks)]
-        tile = functools.reduce(lambda x, y: x | y, places)
-    else:
-        tile = tile & (plane - 1)
-    place_ref[:, :rows] = tile
+    staged.wait()
 
 
 def sums_kernel(*refs, rows, start, count, slots, half, first, prepare, before_spans, share):
@@ -222,6 +227,10 @@
     return pltpu.with_memory_space_constraint(value, pltpu.VMEM)
 
 
+def in_smem(value):
+    return pltpu.with_memory_space_constraint(value, pltpu.SMEM)
+
+
 def vmem():
     return pl.BlockSpec(memory_space=pltpu.VMEM)
 
@@ -288,7 +297,7 @@
         out = (
             pltpu.VMEM((rows, TILE, FEATURES), BF16),
             pltpu.VMEM((8 * rows, TILE), F32),
-            jax.ShapeDtypeStruct((8, TILE), jnp.int32),
+            pltpu.SMEM((8, TILE), jnp.int32),
         ) + ((pltpu.VMEM((2 * half, 3 * NT), F32),) if mix else ())
         return pl.pallas_call(
             functools.partial(
@@ -296,7 +305,8 @@
             ),
             out_shape=out,
             in_specs=[vmem()] * (1 + len(mix)),
-            out_specs=(vmem(),) * len(out),
+            out_specs=(vmem(), vmem(), smem()) + (vmem(),) * len(mix),
+            scratch_shapes=[pltpu.VMEM((8, TILE), jnp.int32), pltpu.SemaphoreType.DMA],
             compiler_params=params,
             name="cell_prep",
         )(in_vmem(cells), *mix)
@@ -326,7 +336,7 @@
             + ([total] if last else [])
             + [pltpu.VMEM((2 * slots, TILE, 2 * TILE), F32), pltpu.VMEM((2 * slots, 2 * TILE, 2 * TILE), BF16)],
             compiler_params=params,
-        )(*places, *map(in_vmem, operands))
+        )(*map(in_smem, places), *map(in_vmem, operands))
 
     spans = [(0, rows)] if NEAR_ROWS == 0 else [(0, NEAR_ROWS), (NEAR_ROWS, rows - NEAR_ROWS)]
     before, tables = [], []

time: 39.9 us -> 39.1 us (0.980)
  Pallas kernels: 16.4 us -> 15.7 us
    pallas_call x2 -> x3, Pallas kernels: 12.9 us -> 12.1 us  [sums(): pl.pallas_call(functools.partial(sums_kernel, rows=rows, start=start, cou...]
  transfers between devices with their start and end apart: 10 -> 10, of which waited for: 5 -> 5; matrix products, arithmetic and copies ran while one was open for 4% -> 4% of each run, Pallas kernels for 22% -> 23%
where the time goes in v6:
time: 39.1 us; the launch traced here: 38.8 us
  Pallas kernels  15.7 us (40%)
  starting transfers between devices  12.4 us (32%)
  waiting for transfers between devices  6.64 us (17%)
  local copies, waits for them, and re-layouts  2.56 us (7%)
  other arithmetic  0.82 us (2%)
  between operations  0.77 us (2%)
    pallas_call x3, Pallas kernels, sums(): pl.pallas_call(functools.partial(sums_kernel, rows=rows, start=start, cou...  12.1 us
    ppermute x2, starting transfers between devices, on_device(): arrived = lax.ppermute(half_plane, axis, flip(size, bit))  4.94 us
    ppermute x3, starting transfers between devices, on_device(): halves.append(lax.ppermute(half_plane, 'blade', flip(n_blade, m)))  4.78 us
    ppermute x3, waiting for transfers between devices, on_device(): halves.append(lax.ppermute(half_plane, 'blade', flip(n_blade, m)))  3.11 us
    pallas_call x2, Pallas kernels, cell_prep(): pl.pallas_call(functools.partial(cell_prep_kernel, rows=rows, plane=plane...  2.47 us
    ppermute x2, waiting for transfers between devices, on_device(): arrived = lax.ppermute(half_plane, axis, flip(size, bit))  2.04 us
    unnamed x3, local copies, waits for them, and re-layouts  1.52 us
    ppermute x1, starting transfers between devices, on_device(): lax.ppermute(cell_rows, 'inst', flip(n_inst, 2 * s))  1.49 us
  transfers between devices with their start and end apart: 10, of which 5 were waited for; matrix products, arithmetic and copies ran while one was open for 4% of the time, Pallas kernels for 23%

profile of v6, /device:TPU:0, one launch (start us, length us, event | category | flops | bytes accessed | tf_op | source)
XLA Modules:
  0.0 38.8 jit_solution(1146755755265378392)
XLA Ops:
  0.6 0.1 pad.14.clone
  0.7 0.8 %maximum_bitcast_fusion = f32[1,32,128]{2,1,0:T(8,128)S(1)} fusion(f32[3,128]{1,0:T(4,128)} %param.6, f32[24,128]{1,0:T(8,128)} %param.7, f32[32]{0:T(128)S(1)} %pad.14.clone), kind=kLoop, calls=%fused_computation.4 | loop fusion | flops 8192 | bytes 30336 | tf_op jit(solution)/shard_map/broadcast_in_dim | solution.py:259
  1.5 3.0 %collective-permute-start = (f32[1,32,128]{2,1,0:T(8,128)S(1)}, f32[1,32,128]{2,1,0:T(8,128)S(1)}, u32[]{:S(2)}, u32[]{:S(2)}) collective-permute-start(f32[1,32,128]{2,1,0:T(8,128)S(1)} %maximum_bitcast_fusion), channel_id=1, source_target_pairs={{0,1},{1,0},{2,3},{3,2},{4,5},{5,4},{6,7},{7,6},{8,9},{9,8},{10,11... | collective-permute-start | bytes 49160 | tf_op jit(solution)/shard_map/ppermute | solution.py:261
  4.5 0.8 %copy.7 = s32[40,1,4]{2,0,1:T(8,128)S(1)} copy(s32[40,1,4]{0,2,1:T(4,128)} %param.8) | data formatting | bytes 1280 | tf_op args[3]
  5.3 0.8 %fusion.1 = (f32[1,40,128]{2,1,0:T(8,128)S(1)}, f32[1,40,128]{2,1,0:T(8,128)S(1)}, f32[1,40,128]{2,1,0:T(8,128)S(1)}) fusion(f32[3,40,128]{2,1,0:T(8,128)} %param.5), kind=kLoop, calls=%fused_computation.6 | loop fusion | bytes 122880 | tf_op jit(solution)/shard_map/slice | solution.py:252
  6.1 0.2 stack.11.source
  6.2 0.0 collective-permute-done
  6.3 1.9 %collective-permute-start.2 = (f32[2,32,128]{2,1,0:T(8,128)S(1)}, f32[2,32,128]{2,1,0:T(8,128)S(1)}, u32[]{:S(2)}, u32[]{:S(2)}) collective-permute-start(f32[2,32,128]{2,1,0:T(8,128)S(1)} %pad_maximum_fusion.2), channel_id=1, source_target_pairs={{0,4},{2,6},{4,0},{6,2},{1,5},{3,7},{5,1},{7,3},{8,12},{10,14},{12... | collective-permute-start | bytes 98312 | tf_op jit(solution)/shard_map/ppermute | solution.py:261
  8.2 2.0 %collective-permute-done.2 = f32[2,32,128]{2,1,0:T(8,128)S(1)} collective-permute-done((f32[2,32,128]{2,1,0:T(8,128)S(1)}, f32[2,32,128]{2,1,0:T(8,128)S(1)}, u32[]{:S(2)}, u32[]{:S(2)}) %collective-permute-start.2) | collective-permute-done | bytes 32800 | tf_op jit(solution)/shard_map/ppermute | solution.py:261
  10.3 4.0 %collective-permute-start.7 = (f32[4,32,128]{2,1,0:T(8,128)S(1)}, f32[4,32,128]{2,1,0:T(8,128)S(1)}, u32[]{:S(2)}, u32[]{:S(2)}) collective-permute-start(f32[4,32,128]{2,1,0:T(8,128)S(1)} %pad_maximum_fusion.1.refs_5_), channel_id=1, source_target_pairs={{0,24},{8,16},{16,8},{24,0},{1,25},{9,17},{17,9},{25,1},{2,26},{10... | collective-permute-start | bytes 196616 | tf_op jit(solution)/shard_map/ppermute | solution.py:268
  14.3 0.0 collective-permute-start.6
  14.3 1.5 %collective-permute-start.1 = (f32[40,8,128]{2,1,0:T(8,128)S(1)}, f32[40,8,128]{2,1,0:T(8,128)S(1)}, u32[]{:S(2)}, u32[]{:S(2)}) collective-permute-start(f32[40,8,128]{2,1,0:T(8,128)S(1)} %stack.11.source), channel_id=1, source_target_pairs={{0,4},{2,6},{4,0},{6,2},{1,5},{3,7},{5,1},{7,3},{8,12},{10,14},{12... | collective-permute-start | bytes 491528 | tf_op jit(solution)/shard_map/ppermute | solution.py:265
  15.7 0.8 %collective-permute-start.4 = (f32[4,32,128]{2,1,0:T(8,128)S(1)}, f32[4,32,128]{2,1,0:T(8,128)S(1)}, u32[]{:S(2)}, u32[]{:S(2)}) collective-permute-start(f32[4,32,128]{2,1,0:T(8,128)S(1)} %pad_maximum_fusion.1.refs_5_), channel_id=1, source_target_pairs={{0,8},{8,0},{16,24},{24,16},{1,9},{9,1},{17,25},{25,17},{2,10},{10... | collective-permute-start | bytes 196616 | tf_op jit(solution)/shard_map/ppermute | solution.py:268
  16.5 0.1 collective-permute-done.7.refs_11_
  16.6 2.9 %collective-permute-done.6.refs_9_ = f32[4,32,128]{2,1,0:T(8,128)S(1)} collective-permute-done((f32[4,32,128]{2,1,0:T(8,128)S(1)}, f32[4,32,128]{2,1,0:T(8,128)S(1)}, u32[]{:S(2)}, u32[]{:S(2)}) %collective-permute-start.6) | collective-permute-done | bytes 65568 | tf_op jit(solution)/shard_map/ppermute | solution.py:268
  19.6 0.1 collective-permute-start.8
  19.6 0.5 %collective-permute-start.3 = (f32[4,32,128]{2,1,0:T(8,128)S(1)}, f32[4,32,128]{2,1,0:T(8,128)S(1)}, u32[]{:S(2)}, u32[]{:S(2)}) collective-permute-start(f32[4,32,128]{2,1,0:T(8,128)S(1)} %pad_maximum_fusion.1.refs_5_), channel_id=1, source_target_pairs={{0,2},{2,0},{4,6},{6,4},{1,3},{3,1},{5,7},{7,5},{8,10},{10,8},{12,... | collective-permute-start | bytes 196616 | tf_op jit(solution)/shard_map/ppermute | solution.py:272
  20.1 0.1 collective-permute-done.4.refs_7_
  20.2 0.0 collective-permute-start.5
  20.2 0.0 copy-start
  20.2 0.8 %copy-done = f32[4,12,24]{2,1,0:T(8,128)S(1)} copy-done((f32[4,12,24]{2,1,0:T(8,128)S(1)}, f32[4,12,24]{2,1,0:T(8,128)}, u32[]{:S(2)}) %copy-start) | copy-done | bytes 4632
  21.0 1.2 %cell_prep.2 = (bf16[40,128,48]{2,1,0:T(8,128)(2,1)S(1)}, f32[320,128]{1,0:T(8,128)S(1)}, s32[8,128]{1,0:T(8,128)S(4)}, f32[24,24]{1,0:T(8,128)S(1)}) custom-call(f32[40,8,128]{2,1,0:T(8,128)S(1)} %stack.11.source, f32[4,12,24]{2,1,0:T(8,128)S(1)} %copy-done), custom_call_target="tpu_custom_call" | custom-call | tf_op jit(solution)/shard_map/cell_prep/pallas_call | solution.py:302
  22.2 0.0 collective-permute-done.1.source
  22.2 1.2 %cell_prep.3 = (bf16[40,128,48]{2,1,0:T(8,128)(2,1)S(1)}, f32[320,128]{1,0:T(8,128)S(1)}, s32[8,128]{1,0:T(8,128)S(4)}) custom-call(f32[40,8,128]{2,1,0:T(8,128)S(1)} %collective-permute-done.1.source), custom_call_target="tpu_custom_call" | custom-call | tf_op jit(solution)/shard_map/cell_prep/pallas_call | solution.py:302
  23.5 0.0 collective-permute-done.3.refs_6_
  23.5 0.0 collective-permute-done.5.refs_8_
  23.5 3.8 %shard_map.68 = (f32[2,576,128]{2,1,0:T(8,128)S(1)}, bf16[16,48,128]{2,1,0:T(8,128)(2,1)S(1)}, bf16[16,48,128]{2,1,0:T(8,128)(2,1)S(1)}) custom-call(s32[8,128]{1,0:T(8,128)S(4)} %get-tuple-element.19.refs_0_, s32[8,128]{1,0:T(8,128)S(4)} %get-tuple-element.20.refs_1_, f32[24,24]{1,0:T(8,128)S(1)} %get-tuple-element.21.refs_2_, ...), custom_call_target="tpu_custom_call" | custom-call | tf_op jit(solution)/shard_map/pallas_call | solution.py:327
  27.3 2.5 %shard_map.69.refs_8_ = f32[2,384,128]{2,1,0:T(8,128)S(1)} custom-call(s32[8,128]{1,0:T(8,128)S(4)} %get-tuple-element.19.refs_0_, s32[8,128]{1,0:T(8,128)S(4)} %get-tuple-element.20.refs_1_, f32[24,24]{1,0:T(8,128)S(1)} %get-tuple-element.21.refs_2_, bf16[40,128,48]{2,1,0:T(8,128)(2,1)S(1)} %get-tuple-element.22.refs_3_, ...), custom_call_target="tpu_custom_call" | custom-call | tf_op jit(solution)/shard_map/pallas_call | solution.py:327
  29.8 0.0 collective-permute-done.8
  29.9 5.8 %shard_map.70 = (f32[2,12,40,128]{3,2,1,0:T(8,128)S(1)}, f32[2,12,40,128]{3,2,1,0:T(8,128)S(1)}) custom-call(s32[8,128]{1,0:T(8,128)S(4)} %get-tuple-element.19.refs_0_, s32[8,128]{1,0:T(8,128)S(4)} %get-tuple-element.20.refs_1_, f32[24,24]{1,0:T(8,128)S(1)} %get-tuple-element.21.refs_2_, bf16[40,128,48]{2,1,0:T(8,128)(2,1)S(1)} %get-tuple-element.22.refs_3_, ...), custom_call_target="tpu_custom_call" | custom-call | tf_op jit(solution)/shard_map/pallas_call | solution.py:327
  35.7 0.6 %collective-permute-start.9 = (f32[2,12,40,128]{3,2,1,0:T(8,128)S(1)}, f32[2,12,40,128]{3,2,1,0:T(8,128)S(1)}, u32[]{:S(2)}, u32[]{:S(2)}) collective-permute-start(f32[2,12,40,128]{3,2,1,0:T(8,128)S(1)} %get-tuple-element.31), channel_id=1, source_target_pairs={{0,2},{2,0},{4,6},{6,4},{1,3},{3,1},{5,7},{7,5},{8,10},{10,8},{12,... | collective-permute-start | bytes 1474568 | tf_op jit(solution)/shard_map/ppermute | solution.py:347
  36.3 1.5 %collective-permute-done.9.peer_ref = f32[2,12,40,128]{3,2,1,0:T(8,128)S(1)} collective-permute-done((f32[2,12,40,128]{3,2,1,0:T(8,128)S(1)}, f32[2,12,40,128]{3,2,1,0:T(8,128)S(1)}, u32[]{:S(2)}, u32[]{:S(2)}) %collective-permute-start.9) | collective-permute-done | bytes 491552 | tf_op jit(solution)/shard_map/ppermute | solution.py:347
  37.8 1.1 %merge.1 = (f32[6,40,512]{2,1,0:T(8,128)}, f32[6,40,512]{2,1,0:T(8,128)}) custom-call(f32[2,12,40,128]{3,2,1,0:T(8,128)S(1)} %get-tuple-element.30.own_ref, f32[2,12,40,128]{3,2,1,0:T(8,128)S(1)} %collective-permute-done.9.peer_ref), custom_call_target="tpu_custom_call" | custom-call | tf_op jit(solution)/shard_map/merge/pallas_call | solution.py:349
  (8 shorter events, 0.1 us)
Async XLA Ops:
  1.5 4.7 %collective-permute-start = (f32[1,32,128]{2,1,0:T(8,128)S(1)}, f32[1,32,128]{2,1,0:T(8,128)S(1)}, u32[]{:S(2)}, u32[]{:S(2)}) collective-permute-start(f32[1,32,128]{2,1,0:T(8,128)S(1)} %maximum_bitcast_fusion), channel_id=1, source_target_pairs={{0,1},{1,0},{2,3},{3,2},{4,5},{5,4},{6,7},{7,6},{8,9},{9,8},{10,11... | collective-permute-start | bytes 49160 | tf_op jit(solution)/shard_map/ppermute | solution.py:261
  6.3 4.0 %collective-permute-start.2 = (f32[2,32,128]{2,1,0:T(8,128)S(1)}, f32[2,32,128]{2,1,0:T(8,128)S(1)}, u32[]{:S(2)}, u32[]{:S(2)}) collective-permute-start(f32[2,32,128]{2,1,0:T(8,128)S(1)} %pad_maximum_fusion.2), channel_id=1, source_target_pairs={{0,4},{2,6},{4,0},{6,2},{1,5},{3,7},{5,1},{7,3},{8,12},{10,14},{12... | collective-permute-start | bytes 98312 | tf_op jit(solution)/shard_map/ppermute | solution.py:261
  10.3 6.4 %collective-permute-start.7 = (f32[4,32,128]{2,1,0:T(8,128)S(1)}, f32[4,32,128]{2,1,0:T(8,128)S(1)}, u32[]{:S(2)}, u32[]{:S(2)}) collective-permute-start(f32[4,32,128]{2,1,0:T(8,128)S(1)} %pad_maximum_fusion.1.refs_5_), channel_id=1, source_target_pairs={{0,24},{8,16},{16,8},{24,0},{1,25},{9,17},{17,9},{25,1},{2,26},{10... | collective-permute-start | bytes 196616 | tf_op jit(solution)/shard_map/ppermute | solution.py:268
  14.3 5.3 %collective-permute-start.6 = (f32[4,32,128]{2,1,0:T(8,128)S(1)}, f32[4,32,128]{2,1,0:T(8,128)S(1)}, u32[]{:S(2)}, u32[]{:S(2)}) collective-permute-start(f32[4,32,128]{2,1,0:T(8,128)S(1)} %pad_maximum_fusion.1.refs_5_), channel_id=1, source_target_pairs={{0,16},{8,24},{16,0},{24,8},{1,17},{9,25},{17,1},{25,9},{2,18},{10... | collective-permute-start | bytes 196616 | tf_op jit(solution)/shard_map/ppermute | solution.py:268
  14.3 8.0 %collective-permute-start.1 = (f32[40,8,128]{2,1,0:T(8,128)S(1)}, f32[40,8,128]{2,1,0:T(8,128)S(1)}, u32[]{:S(2)}, u32[]{:S(2)}) collective-permute-start(f32[40,8,128]{2,1,0:T(8,128)S(1)} %stack.11.source), channel_id=1, source_target_pairs={{0,4},{2,6},{4,0},{6,2},{1,5},{3,7},{5,1},{7,3},{8,12},{10,14},{12... | collective-permute-start | bytes 491528 | tf_op jit(solution)/shard_map/ppermute | solution.py:265
  15.7 4.5 %collective-permute-start.4 = (f32[4,32,128]{2,1,0:T(8,128)S(1)}, f32[4,32,128]{2,1,0:T(8,128)S(1)}, u32[]{:S(2)}, u32[]{:S(2)}) collective-permute-start(f32[4,32,128]{2,1,0:T(8,128)S(1)} %pad_maximum_fusion.1.refs_5_), channel_id=1, source_target_pairs={{0,8},{8,0},{16,24},{24,16},{1,9},{9,1},{17,25},{25,17},{2,10},{10... | collective-permute-start | bytes 196616 | tf_op jit(solution)/shard_map/ppermute | solution.py:268
  19.6 10.3 %collective-permute-start.8 = (f32[8,32,128]{2,1,0:T(8,128)S(1)}, f32[8,32,128]{2,1,0:T(8,128)S(1)}, u32[]{:S(2)}, u32[]{:S(2)}) collective-permute-start(f32[8,32,128]{2,1,0:T(8,128)S(1)} %pad_maximum_fusion), channel_id=1, source_target_pairs={{0,2},{2,0},{4,6},{6,4},{1,3},{3,1},{5,7},{7,5},{8,10},{10,8},{12,... | collective-permute-start | bytes 393224 | tf_op jit(solution)/shard_map/ppermute | solution.py:273
  19.6 3.8 %collective-permute-start.3 = (f32[4,32,128]{2,1,0:T(8,128)S(1)}, f32[4,32,128]{2,1,0:T(8,128)S(1)}, u32[]{:S(2)}, u32[]{:S(2)}) collective-permute-start(f32[4,32,128]{2,1,0:T(8,128)S(1)} %pad_maximum_fusion.1.refs_5_), channel_id=1, source_target_pairs={{0,2},{2,0},{4,6},{6,4},{1,3},{3,1},{5,7},{7,5},{8,10},{10,8},{12,... | collective-permute-start | bytes 196616 | tf_op jit(solution)/shard_map/ppermute | solution.py:272
  20.2 3.3 %collective-permute-start.5 = (f32[4,32,128]{2,1,0:T(8,128)S(1)}, f32[4,32,128]{2,1,0:T(8,128)S(1)}, u32[]{:S(2)}, u32[]{:S(2)}) collective-permute-start(f32[4,32,128]{2,1,0:T(8,128)S(1)} %collective-permute-done.4.refs_7_), channel_id=1, source_target_pairs={{0,2},{2,0},{4,6},{6,4},{1,3},{3,1},{5,7},{7,5},{8,10},{10,8},{12,... | collective-permute-start | bytes 196616 | tf_op jit(solution)/shard_map/ppermute | solution.py:272
  20.2 0.8 %copy-start = (f32[4,12,24]{2,1,0:T(8,128)S(1)}, f32[4,12,24]{2,1,0:T(8,128)}, u32[]{:S(2)}) copy-start(f32[4,12,24]{2,1,0:T(8,128)} %constant.3.clone.refs_0_) | copy-start | bytes 13828
  35.7 2.1 %collective-permute-start.9 = (f32[2,12,40,128]{3,2,1,0:T(8,128)S(1)}, f32[2,12,40,128]{3,2,1,0:T(8,128)S(1)}, u32[]{:S(2)}, u32[]{:S(2)}) collective-permute-start(f32[2,12,40,128]{3,2,1,0:T(8,128)S(1)} %get-tuple-element.31), channel_id=1, source_target_pairs={{0,2},{2,0},{4,6},{6,4},{1,3},{3,1},{5,7},{7,5},{8,10},{10,8},{12,... | collective-permute-start | bytes 1474568 | tf_op jit(solution)/shard_map/ppermute | solution.py:347

commit v7 on v6

--- a/solution.py
+++ b/solution.py
@@ -15,6 +15,7 @@
 SCALE = (EDGE / RADIUS) ** 2
 FEATURES = 48
 NEAR_ROWS = 24
+FAR_ROWS = 0
 VMEM_LIMIT = 16 * 1024 * 1024
 BOTH_MINOR = (((1,), (1,)), ((), ()))
 F32 = jnp.float32
@@ -33,7 +34,13 @@
     for group in range(groups):
         own = slice(group * per, (group + 1) * per)
         rows.append(np.concatenate([np.eye(instances)[own], matrix[own]], axis=0))
-    return np.stack([np.kron(block, np.eye(3)) for block in rows]).astype(np.float32)
+    mix = np.stack([np.kron(block, np.eye(3)) for block in rows]).astype(np.float32)
+    parts = []
+    for _ in range(3):
+        parts.append(mix.astype(jnp.bfloat16).astype(np.float32))
+        mix = mix - parts[-1]
+    high, middle, low = parts
+    return np.concatenate([high, middle, low, high, middle, high], axis=2)
 
 
 def split3(value):
@@ -51,33 +58,40 @@
     return [1 << b for b in range(size.bit_length() - 1)]
 
 
-def cell_prep_kernel(source, *refs, rows, plane, sizes, masks):
-    *refs, staged_ref, sem = refs
-    feature_ref, coord_ref, place_ref = refs[-4:-1] if len(refs) == 5 else refs
-    if len(refs) == 5:
-        mix_ref, mixed_ref = refs[0], refs[-1]
-        inst = lax.axis_index("inst")
-        mixed_ref[...] = jnp.concatenate([mix_ref[inst], mix_ref[inst ^ 1]], axis=0)
+def pack_kernel(coef_ref, point_ref, coord_ref, list_ref, mix_ref, block_ref, cell_ref, mixed_ref):
+    count = coef_ref.shape[0]
+    width = coef_ref.shape[1]
+    block_ref[:count] = coef_ref[...]
+    block_ref[count:] = jnp.concatenate([point_ref[...], jnp.zeros((5, width), F32)], axis=0)
+    size = coord_ref.shape[0]
+    cell_ref[:size] = coord_ref[...]
+    cell_ref[size:] = jnp.zeros((8, TILE), F32)
+    terms, rows = list_ref.shape
+    cell_ref[size : size + terms, :rows] = list_ref[...].astype(F32)
+    inst = lax.axis_index("inst")
+    mixed_ref[...] = jnp.concatenate([mix_ref[inst], mix_ref[inst ^ 1]], axis=0).astype(BF16)
+
+
+def cell_prep_kernel(cell_ref, feature_ref, place_ref, staged_ref, sem, *, rows, plane, sizes, masks):
     n_inst, n_cell = sizes["inst"], sizes["cell"]
     device = (lax.axis_index("blade") * n_inst + lax.axis_index("inst")) * n_cell + lax.axis_index("cell")
     row_id = lax.broadcasted_iota(jnp.int32, (8, TILE), 0)
     diagonal = lax.broadcasted_iota(jnp.int32, (TILE, TILE), 0) == lax.broadcasted_iota(jnp.int32, (TILE, TILE), 1)
     identity = jnp.where(diagonal, 1.0, 0.0).astype(BF16)
 
-    tile = source[:, 3, :].T[:8].astype(jnp.int32)
+    tile = cell_ref[3 * rows :, :].astype(jnp.int32)
     if masks is not None:
         tile = tile ^ device
         places = [(lax.shift_right_logical(tile, m) & 1) << k for k, m in enumerate(masks)]
         tile = functools.reduce(lambda x, y: x | y, places)
     else:
         tile = tile & (plane - 1)
-    staged_ref[:, :rows] = tile
+    staged_ref[...] = tile
     staged = pltpu.make_async_copy(staged_ref, place_ref, sem)
     staged.start()
 
     def one_row(r, carry):
-        value = source[r]
-        coord_ref[pl.ds(r, 8, stride=rows), :] = value
+        value = jnp.concatenate([cell_ref[pl.ds(r, 3, stride=rows), :], jnp.zeros((5, TILE), F32)], axis=0)
         centred = jnp.where(row_id < 3, value - 0.5, 0.0)
         length = SCALE * jnp.sum(centred * centred, axis=0, keepdims=True)
         value = jnp.where(row_id == 3, 1.0, jnp.where(row_id == 4, length, centred))
@@ -128,10 +142,9 @@
             high, middle, low = split3(value)
             stacked = jnp.concatenate([high, high, high, middle, middle, low], axis=0)
             centre_ref[base + p] = stacked.astype(BF16)
-            mixed = jnp.dot(
-                mix_ref[...], block_ref[p, : 3 * NT, :],
-                preferred_element_type=F32, precision=lax.Precision.HIGHEST,
-            )
+            high, middle, low = split3(block_ref[p, : 3 * NT, :])
+            stacked = jnp.concatenate([high, high, high, middle, middle, low], axis=0).astype(BF16)
+            mixed = jnp.dot(mix_ref[...], stacked, preferred_element_type=F32)
             mixed_high = mixed.astype(BF16).astype(F32)
             coef_ref[base + p] = jnp.concatenate([mixed_high, mixed - mixed_high], axis=0).astype(BF16)
             return carry
@@ -157,8 +170,8 @@
         )
 
     def weights(unit):
-        squared = jnp.maximum(dist_ref[unit], 1e-12)
-        margin = jnp.maximum(EDGE - squared * lax.rsqrt(squared), 0.0)
+        squared = jnp.clip(dist_ref[unit], 1e-12, EDGE * EDGE)
+        margin = EDGE - squared * lax.rsqrt(squared)
         margin_sq = margin * margin
         weight = (margin_sq * margin_sq) * (1.25 * EDGE - margin)
         high = weight.astype(BF16)
@@ -213,14 +226,22 @@
                     out[slot, c, begin : begin + size] = value
 
 
-def merge_kernel(own_ref, peer_ref, moved_ref, velocity_ref, *, slots, half):
+def merge_kernel(own_ref, peer_ref, *refs, slots, half, start, count):
     shifts = half // 2
+    moved_ref, velocity_ref, stage_ref, sems = refs[-4:]
     inst = lax.axis_index("inst")
-    for which, source in enumerate((own_ref, peer_ref)):
-        for slot in range(slots):
-            lane = pl.multiple_of((inst ^ which ^ (2 * slot)) * TILE, TILE)
-            moved_ref[:, :, pl.ds(lane, TILE)] = source[slot, :shifts]
-            velocity_ref[:, :, pl.ds(lane, TILE)] = source[slot, shifts:]
+    copies = []
+    for c in range(half):
+        for which, source in enumerate((own_ref, peer_ref)):
+            for slot in range(slots):
+                lane = pl.multiple_of((inst ^ which ^ (2 * slot)) * TILE, TILE)
+                stage_ref[c, :, pl.ds(lane, TILE)] = source[slot, c]
+        out = moved_ref if c < shifts else velocity_ref
+        copy = pltpu.make_async_copy(stage_ref.at[c], out.at[c % shifts, pl.ds(start, count)], sems.at[c])
+        copy.start()
+        copies.append(copy)
+    for copy in copies:
+        copy.wait()
 
 
 def in_vmem(value):
@@ -231,8 +252,16 @@
     return pltpu.with_memory_space_constraint(value, pltpu.SMEM)
 
 
+def in_hbm(value):
+    return pltpu.with_memory_space_constraint(value, pltpu.HBM)
+
+
 def vmem():
     return pl.BlockSpec(memory_space=pltpu.VMEM)
+
+
+def hbm():
+    return pl.BlockSpec(memory_space=pl.ANY)
 
 
 def smem():
@@ -242,27 +271,57 @@
 def on_device(cell_coords, centre_points, coefficients, tile_lists, *, sizes):
     n_blade, n_inst, n_cell = sizes["blade"], sizes["inst"], sizes["cell"]
     rows = cell_coords.shape[1]
-    terms = tile_lists.shape[2]
     width = centre_points.shape[1]
     slots = n_inst // 2
     half = 2 * 3 * (NT // n_inst)
-    block = jnp.concatenate([coefficients, centre_points, jnp.zeros((5, width), F32)], axis=0)
-    list_row = jnp.pad(tile_lists[:, 0, :].astype(F32), ((0, 0), (0, TILE - terms)))
-    blank = jnp.zeros_like(list_row)
-    cell_rows = jnp.stack([cell_coords[0], cell_coords[1], cell_coords[2], list_row] + [blank] * 4, axis=1)
-
+    params = pltpu.CompilerParams(vmem_limit_bytes=VMEM_LIMIT)
+    given = (
+        coefficients, centre_points, cell_coords.reshape(3 * rows, TILE), tile_lists[:, 0, :].T,
+        jnp.asarray(spectral_rows(NT, n_inst)),
+    )
+    block, cells, mix = pl.pallas_call(
+        pack_kernel,
+        out_shape=(
+            pltpu.VMEM((3 * NT + 8, width), F32),
+            pltpu.VMEM((3 * rows + 8, TILE), F32),
+            pltpu.VMEM((2 * half, 18 * NT), BF16),
+        ),
+        in_specs=[vmem()] * len(given),
+        out_specs=(vmem(),) * 3,
+        compiler_params=params,
+        name="pack",
+    )(*map(in_hbm, given))
     core = 1
     inner = [("cell", n_cell, b, b) for b in bits_of(n_cell)]
     inner += [("inst", n_inst, b, b * n_cell) for b in bits_of(n_inst) if b != core]
     masks = [mask.bit_length() - 1 for _, _, _, mask in inner] + [(core * n_cell).bit_length() - 1]
 
+    plane = n_inst * n_cell * width // TILE
+
+    def cell_prep(cells):
+        return pl.pallas_call(
+            functools.partial(
+                cell_prep_kernel, rows=rows, plane=plane, sizes=sizes, masks=masks if width == TILE else None
+            ),
+            out_shape=(pltpu.VMEM((rows, TILE, FEATURES), BF16), pltpu.SMEM((8, TILE), jnp.int32)),
+            in_specs=[vmem()],
+            out_specs=(vmem(), smem()),
+            scratch_shapes=[pltpu.VMEM((8, TILE), jnp.int32), pltpu.SemaphoreType.DMA],
+            compiler_params=params,
+            name="cell_prep",
+        )(in_vmem(cells))
+
     half_plane = block[None]
-    for index, (axis, size, bit, _) in enumerate(inner):
-        arrived = lax.ppermute(half_plane, axis, flip(size, bit))
-        if index == 0:
-            arrived, cell_rows = lax.optimization_barrier((arrived, cell_rows))
-        half_plane = jnp.concatenate([half_plane, arrived], axis=0)
-    others = [lax.ppermute(cell_rows, "inst", flip(n_inst, 2 * s)) for s in range(1, slots)]
+    joint = inner[-2:]
+    for axis, size, bit, _ in inner[:-2]:
+        half_plane = jnp.concatenate([half_plane, lax.ppermute(half_plane, axis, flip(size, bit))], axis=0)
+    pieces = [half_plane]
+    for combination in range(1, 1 << len(joint)):
+        mask = sum(joint[k][3] for k in range(len(joint)) if combination >> k & 1)
+        pieces.append(lax.ppermute(half_plane, ("inst", "cell"), flip(n_inst * n_cell, mask)))
+    half_plane = jnp.concatenate(pieces, axis=0)
+    others = [lax.ppermute(cells, "inst", flip(n_inst, 2 * k)) for k in range(1, slots)]
+    prepared = [cell_prep(cells)]
     halves = [half_plane]
     for m in range(1, n_blade):
         halves.append(lax.ppermute(half_plane, "blade", flip(n_blade, m)))
@@ -283,38 +342,15 @@
             blocks = blocks.reshape(-1, TILE // width, 3 * NT + 8, width)
             return [jnp.moveaxis(blocks, 1, 2).reshape(-1, 3 * NT + 8, TILE)]
 
-        plane = n_inst * n_cell * width // TILE
     else:
         def whole_plane(mine, theirs):
             return [mine, theirs]
 
-        plane = n_inst * n_cell
     planes = [whole_plane(*pair) for pair in zip(halves, swapped)]
 
-    params = pltpu.CompilerParams(vmem_limit_bytes=VMEM_LIMIT)
-
-    def cell_prep(cells, *mix):
-        out = (
-            pltpu.VMEM((rows, TILE, FEATURES), BF16),
-            pltpu.VMEM((8 * rows, TILE), F32),
-            pltpu.SMEM((8, TILE), jnp.int32),
-        ) + ((pltpu.VMEM((2 * half, 3 * NT), F32),) if mix else ())
-        return pl.pallas_call(
-            functools.partial(
-                cell_prep_kernel, rows=rows, plane=plane, sizes=sizes, masks=masks if width == TILE else None
-            ),
-            out_shape=out,
-            in_specs=[vmem()] * (1 + len(mix)),
-            out_specs=(vmem(), vmem(), smem()) + (vmem(),) * len(mix),
-            scratch_shapes=[pltpu.VMEM((8, TILE), jnp.int32), pltpu.SemaphoreType.DMA],
-            compiler_params=params,
-            name="cell_prep",
-        )(in_vmem(cells), *mix)
-
-    *own_cells, mix = cell_prep(cell_rows, jnp.asarray(spectral_rows(NT, n_inst)))
-    prepared = [own_cells]
-    prepared += [cell_prep(cells) for cells in others]
-    features, coords, places = map(list, zip(*prepared))
+    prepared += [cell_prep(other) for other in others]
+    features, places = map(list, zip(*prepared))
+    coords = [cells] + others
 
     def sums(first, start, count, before=(), before_spans=(), given=(), share=False):
         last = len(before) > 0
@@ -338,22 +374,42 @@
             compiler_params=params,
         )(*map(in_smem, places), *map(in_vmem, operands))
 
-    spans = [(0, rows)] if NEAR_ROWS == 0 else [(0, NEAR_ROWS), (NEAR_ROWS, rows - NEAR_ROWS)]
+    def spans_of(lead):
+        return [(0, lead), (lead, rows - lead)] if lead else [(0, rows)]
+
+    spans = spans_of(NEAR_ROWS)
     before, tables = [], []
     for start, count in spans:
         part, *made = sums(0, start, count, given=tables, share=len(spans) > 1 and not tables)
         before, tables = before + [part], tables or made
-    own, peer = sums(2, 0, rows, before=before, before_spans=spans)
-    received = lax.ppermute(peer, "inst", flip(n_inst, core))
+    pieces, tables = [], []
+    if FAR_ROWS:
+        spans = spans_of(FAR_ROWS)
+        parts = [([part], [(0, count)]) for part, (_, count) in zip(before, spans)]
+    else:
+        parts, spans = [(before, spans)], [(0, rows)]
+    for (part, part_spans), (start, count) in zip(parts, spans):
+        own, peer, *made = sums(
+            2, start, count, before=part, before_spans=part_spans,
+            given=tables, share=len(spans) > 1 and not tables,
+        )
+        tables = tables or made
+        pieces.append((own, lax.ppermute(peer, "inst", flip(n_inst, core))))
     out = jax.ShapeDtypeStruct((half // 2, rows, n_inst * TILE), F32)
-    moved, velocity = pl.pallas_call(
-        functools.partial(merge_kernel, slots=slots, half=half),
-        out_shape=(out, out),
-        in_specs=[vmem()] * 2,
-        out_specs=(vmem(), vmem()),
-        compiler_params=params,
-        name="merge",
-    )(in_vmem(own), in_vmem(received))
+    outputs = ()
+    for (start, count), piece in zip(spans, pieces):
+        outputs = pl.pallas_call(
+            functools.partial(merge_kernel, slots=slots, half=half, start=start, count=count),
+            out_shape=(out, out),
+            in_specs=[vmem()] * 2 + [hbm()] * len(outputs),
+            out_specs=(hbm(), hbm()),
+            input_output_aliases={2 + i: i for i in range(len(outputs))},
+            scratch_shapes=[
+                pltpu.VMEM((half, count, n_inst * TILE), F32), pltpu.SemaphoreType.DMA((half,)),
+            ],
+            compiler_params=params,
+        )(*map(in_vmem, piece), *outputs)
+    moved, velocity = outputs
     shape = (NT // n_inst, 3, rows, n_inst * TILE)
     return (moved.reshape(shape), velocity.reshape(shape))
 

time: 39.1 us -> 38.8 us (level)
  waiting for transfers between devices: 6.64 us -> 11.1 us
  local copies, waits for them, and re-layouts: 2.56 us -> 0.01 us
  starting transfers between devices: 12.4 us -> 11.2 us
  other arithmetic: 0.82 us -> 0.02 us
    ppermute x4 -> x5, waiting for transfers between devices: 3.53 us -> 6.75 us  [the longest x3 3.63 us: on_device(): lax.ppermute(half_plane, ('inst', 'cell'), flip(n_inst * n_cell, mask))]
    unnamed x3 -> x0, local copies, waits for them, and re-layouts: 1.52 us -> none
    ppermute x3, waiting for transfers between devices: 3.11 us -> 4.38 us  [on_device(): halves.append(lax.ppermute(half_plane, 'blade', flip(n_blade, m)))]
    pallas_call x1 -> x2, Pallas kernels: 1.07 us -> 1.99 us  [the longest x1 1.06 us: on_device(): pl.pallas_call(functools.partial(merge_kernel, slots=slots, half=half, st...]
    pallas_call x3, Pallas kernels: 12.1 us -> 11.3 us  [sums(): pl.pallas_call(functools.partial(sums_kernel, rows=rows, start=start, cou...]
    broadcast_in_dim x1 -> x0, other arithmetic: 0.8 us -> none  [on_device(): half_plane = block[None]]
    slice x1 -> x0, local copies, waits for them, and re-layouts: 0.77 us -> none  [on_device(): cell_coords[2]]
    ppermute x4 -> x5, starting transfers between devices: 7.01 us -> 6.26 us  [the longest x3 4.63 us: on_device(): lax.ppermute(half_plane, ('inst', 'cell'), flip(n_inst * n_cell, mask))]
  transfers between devices with their start and end apart: 10 -> 11, of which waited for: 5 -> 7; matrix products, arithmetic and copies ran while one was open for 4% -> 0% of each run, Pallas kernels for 23% -> 21%
where the time goes in v7:
time: 38.8 us; the launch traced here: 38.7 us
  Pallas kernels  15.6 us (40%)
  starting transfers between devices  11.2 us (29%)
  waiting for transfers between devices  11.1 us (29%)
  between operations  0.73 us (2%)
    pallas_call x3, Pallas kernels, sums(): pl.pallas_call(functools.partial(sums_kernel, rows=rows, start=start, cou...  11.3 us
    ppermute x3, starting transfers between devices, on_device(): lax.ppermute(half_plane, ('inst', 'cell'), flip(n_inst * n_cell, mask))  4.63 us
    ppermute x3, starting transfers between devices, on_device(): halves.append(lax.ppermute(half_plane, 'blade', flip(n_blade, m)))  4.39 us
    ppermute x3, waiting for transfers between devices, on_device(): halves.append(lax.ppermute(half_plane, 'blade', flip(n_blade, m)))  4.38 us
    ppermute x3, waiting for transfers between devices, on_device(): lax.ppermute(half_plane, ('inst', 'cell'), flip(n_inst * n_cell, mask))  3.63 us
    pallas_call x2, Pallas kernels, cell_prep(): pl.pallas_call(functools.partial(cell_prep_kernel, rows=rows, plane=plane...  2.3 us
    ppermute x1, waiting for transfers between devices, on_device(): pieces.append((own, lax.ppermute(peer, 'inst', flip(n_inst, core))))  1.85 us
    ppermute x1, starting transfers between devices, on_device(): lax.ppermute(cells, 'inst', flip(n_inst, 2 * k))  1.56 us
  transfers between devices with their start and end apart: 11, of which 7 were waited for; matrix products, arithmetic and copies ran while one was open for 0% of the time, Pallas kernels for 21%

profile of v7, /device:TPU:0, one launch (start us, length us, event | category | flops | bytes accessed | tf_op | source)
XLA Modules:
  0.0 38.7 jit_solution(11578898467397907591)
XLA Ops:
  0.6 0.9 %pack.1 = (f32[32,128]{1,0:T(8,128)S(1)}, f32[128,128]{1,0:T(8,128)S(1)}, bf16[24,144]{1,0:T(8,128)(2,1)S(1)}) custom-call(f32[24,128]{1,0:T(8,128)} %coef_ref.1, f32[3,128]{1,0:T(4,128)} %point_ref.1, f32[120,128]{1,0:T(8,128)} %bitcast.11, s32[4,40]{1,0:T(4,128)} %bitcast.12, f32[4,12,144]{2,1,0:T(8,128)} %constant.2.clone.mix_ref), custom_call_target="tpu_custom_call" | custom-call | tf_op jit(solution)/shard_map/pack/pallas_call | solution.py:282
  1.6 4.0 %collective-permute-start.3 = (f32[1,32,128]{2,1,0:T(8,128)S(1)}, f32[1,32,128]{2,1,0:T(8,128)S(1)}, u32[]{:S(2)}, u32[]{:S(2)}) collective-permute-start(f32[1,32,128]{2,1,0:T(8,128)S(1)} %bitcast.7), channel_id=1, source_target_pairs={{0,5},{1,4},{2,7},{3,6},{4,1},{5,0},{6,3},{7,2},{8,13},{9,12},{10,... | collective-permute-start | bytes 49160 | tf_op jit(solution)/shard_map/ppermute | solution.py:321
  5.6 0.5 %collective-permute-start.2 = (f32[1,32,128]{2,1,0:T(8,128)S(1)}, f32[1,32,128]{2,1,0:T(8,128)S(1)}, u32[]{:S(2)}, u32[]{:S(2)}) collective-permute-start(f32[1,32,128]{2,1,0:T(8,128)S(1)} %bitcast.8), channel_id=1, source_target_pairs={{0,4},{1,5},{2,6},{3,7},{4,0},{5,1},{6,2},{7,3},{8,12},{9,13},{10,... | collective-permute-start | bytes 49160 | tf_op jit(solution)/shard_map/ppermute | solution.py:321
  6.1 0.1 collective-permute-start.1
  6.2 1.1 %collective-permute-done.3 = f32[1,32,128]{2,1,0:T(8,128)S(1)} collective-permute-done((f32[1,32,128]{2,1,0:T(8,128)S(1)}, f32[1,32,128]{2,1,0:T(8,128)S(1)}, u32[]{:S(2)}, u32[]{:S(2)}) %collective-permute-start.3) | collective-permute-done | bytes 16416 | tf_op jit(solution)/shard_map/ppermute | solution.py:321
  7.3 2.0 %collective-permute-done.2 = f32[1,32,128]{2,1,0:T(8,128)S(1)} collective-permute-done((f32[1,32,128]{2,1,0:T(8,128)S(1)}, f32[1,32,128]{2,1,0:T(8,128)S(1)}, u32[]{:S(2)}, u32[]{:S(2)}) %collective-permute-start.2) | collective-permute-done | bytes 16416 | tf_op jit(solution)/shard_map/ppermute | solution.py:321
  9.3 0.5 %collective-permute-done.1 = f32[1,32,128]{2,1,0:T(8,128)S(1)} collective-permute-done((f32[1,32,128]{2,1,0:T(8,128)S(1)}, f32[1,32,128]{2,1,0:T(8,128)S(1)}, u32[]{:S(2)}, u32[]{:S(2)}) %collective-permute-start.1) | collective-permute-done | bytes 16416 | tf_op jit(solution)/shard_map/ppermute | solution.py:321
  9.8 3.6 %collective-permute-start.8 = (f32[4,32,128]{2,1,0:T(8,128)S(1)}, f32[4,32,128]{2,1,0:T(8,128)S(1)}, u32[]{:S(2)}, u32[]{:S(2)}) collective-permute-start(f32[4,32,128]{2,1,0:T(8,128)S(1)} %pad_maximum_fusion.1.refs_5_), channel_id=1, source_target_pairs={{0,24},{8,16},{16,8},{24,0},{1,25},{9,17},{17,9},{25,1},{2,26},{10... | collective-permute-start | bytes 196616 | tf_op jit(solution)/shard_map/ppermute | solution.py:327
  13.4 0.0 collective-permute-start.7
  13.4 0.8 %collective-permute-start.5 = (f32[4,32,128]{2,1,0:T(8,128)S(1)}, f32[4,32,128]{2,1,0:T(8,128)S(1)}, u32[]{:S(2)}, u32[]{:S(2)}) collective-permute-start(f32[4,32,128]{2,1,0:T(8,128)S(1)} %pad_maximum_fusion.1.refs_5_), channel_id=1, source_target_pairs={{0,8},{8,0},{16,24},{24,16},{1,9},{9,1},{17,25},{25,17},{2,10},{10... | collective-permute-start | bytes 196616 | tf_op jit(solution)/shard_map/ppermute | solution.py:327
  14.2 1.8 %collective-permute-done.8.refs_11_ = f32[4,32,128]{2,1,0:T(8,128)S(1)} collective-permute-done((f32[4,32,128]{2,1,0:T(8,128)S(1)}, f32[4,32,128]{2,1,0:T(8,128)S(1)}, u32[]{:S(2)}, u32[]{:S(2)}) %collective-permute-start.8) | collective-permute-done | bytes 65568 | tf_op jit(solution)/shard_map/ppermute | solution.py:327
  16.0 2.6 %collective-permute-done.7.refs_9_ = f32[4,32,128]{2,1,0:T(8,128)S(1)} collective-permute-done((f32[4,32,128]{2,1,0:T(8,128)S(1)}, f32[4,32,128]{2,1,0:T(8,128)S(1)}, u32[]{:S(2)}, u32[]{:S(2)}) %collective-permute-start.7) | collective-permute-done | bytes 65568 | tf_op jit(solution)/shard_map/ppermute | solution.py:327
  18.6 0.1 collective-permute-start.9
  18.7 1.6 %collective-permute-start = (f32[128,128]{1,0:T(8,128)S(1)}, f32[128,128]{1,0:T(8,128)S(1)}, u32[]{:S(2)}, u32[]{:S(2)}) collective-permute-start(f32[128,128]{1,0:T(8,128)S(1)} %get-tuple-element.16.cell_ref.refs_5_), channel_id=1, source_target_pairs={{0,4},{2,6},{4,0},{6,2},{1,5},{3,7},{5,1},{7,3},{8,12},{10,14},{12... | collective-permute-start | bytes 196616 | tf_op jit(solution)/shard_map/ppermute | solution.py:323
  20.3 0.2 collective-permute-start.4
  20.4 0.0 collective-permute-done.5.refs_7_
  20.4 0.4 collective-permute-start.6
  20.8 1.2 %cell_prep.2 = (bf16[40,128,48]{2,1,0:T(8,128)(2,1)S(1)}, s32[8,128]{1,0:T(8,128)S(4)}) custom-call(f32[128,128]{1,0:T(8,128)S(1)} %get-tuple-element.16.cell_ref.refs_5_), custom_call_target="tpu_custom_call" | custom-call | tf_op jit(solution)/shard_map/cell_prep/pallas_call | solution.py:302
  21.9 1.3 %collective-permute-done.cell_ref.refs_6_ = f32[128,128]{1,0:T(8,128)S(1)} collective-permute-done((f32[128,128]{1,0:T(8,128)S(1)}, f32[128,128]{1,0:T(8,128)S(1)}, u32[]{:S(2)}, u32[]{:S(2)}) %collective-permute-start) | collective-permute-done | bytes 65568 | tf_op jit(solution)/shard_map/ppermute | solution.py:323
  23.2 1.1 %cell_prep.3 = (bf16[40,128,48]{2,1,0:T(8,128)(2,1)S(1)}, s32[8,128]{1,0:T(8,128)S(4)}) custom-call(f32[128,128]{1,0:T(8,128)S(1)} %collective-permute-done.cell_ref.refs_6_), custom_call_target="tpu_custom_call" | custom-call | tf_op jit(solution)/shard_map/cell_prep/pallas_call | solution.py:302
  24.3 0.0 collective-permute-done.4.refs_6_
  24.4 0.0 collective-permute-done.6.refs_8_
  24.4 3.5 %shard_map.68 = (f32[2,576,128]{2,1,0:T(8,128)S(1)}, bf16[16,48,128]{2,1,0:T(8,128)(2,1)S(1)}, bf16[16,48,128]{2,1,0:T(8,128)(2,1)S(1)}) custom-call(s32[8,128]{1,0:T(8,128)S(4)} %get-tuple-element.17.refs_0_, s32[8,128]{1,0:T(8,128)S(4)} %get-tuple-element.18.refs_1_, bf16[24,144]{1,0:T(8,128)(2,1)S(1)} %get-tuple-element.19.refs_2_, ...), custom_call_target="tpu_custom_call" | custom-call | tf_op jit(solution)/shard_map/pallas_call | solution.py:363
  27.9 2.3 %shard_map.69.refs_8_ = f32[2,384,128]{2,1,0:T(8,128)S(1)} custom-call(s32[8,128]{1,0:T(8,128)S(4)} %get-tuple-element.17.refs_0_, s32[8,128]{1,0:T(8,128)S(4)} %get-tuple-element.18.refs_1_, bf16[24,144]{1,0:T(8,128)(2,1)S(1)} %get-tuple-element.19.refs_2_, bf16[40,128,48]{2,1,0:T(8,128)(2,1)S(1)} %get-tuple-element.20.refs_3_, ...), custom_call_target="tpu_custom_call" | custom-call | tf_op jit(solution)/shard_map/pallas_call | solution.py:363
  30.2 0.0 collective-permute-done.9
  30.2 5.4 %shard_map.70 = (f32[2,12,40,128]{3,2,1,0:T(8,128)S(1)}, f32[2,12,40,128]{3,2,1,0:T(8,128)S(1)}) custom-call(s32[8,128]{1,0:T(8,128)S(4)} %get-tuple-element.17.refs_0_, s32[8,128]{1,0:T(8,128)S(4)} %get-tuple-element.18.refs_1_, bf16[24,144]{1,0:T(8,128)(2,1)S(1)} %get-tuple-element.19.refs_2_, bf16[40,128,48]{2,1,0:T(8,128)(2,1)S(1)} %get-tuple-element.20.refs_3_, ...), custom_call_target="tpu_custom_call" | custom-call | tf_op jit(solution)/shard_map/pallas_call | solution.py:363
  35.7 0.1 collective-permute-start.10
  35.8 1.9 %collective-permute-done.10.peer_ref = f32[2,12,40,128]{3,2,1,0:T(8,128)S(1)} collective-permute-done((f32[2,12,40,128]{3,2,1,0:T(8,128)S(1)}, f32[2,12,40,128]{3,2,1,0:T(8,128)S(1)}, u32[]{:S(2)}, u32[]{:S(2)}) %collective-permute-start.10) | collective-permute-done | bytes 491552 | tf_op jit(solution)/shard_map/ppermute | solution.py:397
  37.6 1.1 %shard_map.71 = (f32[6,40,512]{2,1,0:T(8,128)}, f32[6,40,512]{2,1,0:T(8,128)}) custom-call(f32[2,12,40,128]{3,2,1,0:T(8,128)S(1)} %get-tuple-element.26.own_ref, f32[2,12,40,128]{3,2,1,0:T(8,128)S(1)} %collective-permute-done.10.peer_ref), custom_call_target="tpu_custom_call" | custom-call | tf_op jit(solution)/shard_map/pallas_call | solution.py:401
  (3 shorter events, 0.0 us)
Async XLA Ops:
  1.6 5.7 %collective-permute-start.3 = (f32[1,32,128]{2,1,0:T(8,128)S(1)}, f32[1,32,128]{2,1,0:T(8,128)S(1)}, u32[]{:S(2)}, u32[]{:S(2)}) collective-permute-start(f32[1,32,128]{2,1,0:T(8,128)S(1)} %bitcast.7), channel_id=1, source_target_pairs={{0,5},{1,4},{2,7},{3,6},{4,1},{5,0},{6,3},{7,2},{8,13},{9,12},{10,... | collective-permute-start | bytes 49160 | tf_op jit(solution)/shard_map/ppermute | solution.py:321
  5.6 3.7 %collective-permute-start.2 = (f32[1,32,128]{2,1,0:T(8,128)S(1)}, f32[1,32,128]{2,1,0:T(8,128)S(1)}, u32[]{:S(2)}, u32[]{:S(2)}) collective-permute-start(f32[1,32,128]{2,1,0:T(8,128)S(1)} %bitcast.8), channel_id=1, source_target_pairs={{0,4},{1,5},{2,6},{3,7},{4,0},{5,1},{6,2},{7,3},{8,12},{9,13},{10,... | collective-permute-start | bytes 49160 | tf_op jit(solution)/shard_map/ppermute | solution.py:321
  6.1 3.7 %collective-permute-start.1 = (f32[1,32,128]{2,1,0:T(8,128)S(1)}, f32[1,32,128]{2,1,0:T(8,128)S(1)}, u32[]{:S(2)}, u32[]{:S(2)}) collective-permute-start(f32[1,32,128]{2,1,0:T(8,128)S(1)} %bitcast.9), channel_id=1, source_target_pairs={{0,1},{1,0},{2,3},{3,2},{4,5},{5,4},{6,7},{7,6},{8,9},{9,8},{10,11... | collective-permute-start | bytes 49160 | tf_op jit(solution)/shard_map/ppermute | solution.py:321
  9.8 6.2 %collective-permute-start.8 = (f32[4,32,128]{2,1,0:T(8,128)S(1)}, f32[4,32,128]{2,1,0:T(8,128)S(1)}, u32[]{:S(2)}, u32[]{:S(2)}) collective-permute-start(f32[4,32,128]{2,1,0:T(8,128)S(1)} %pad_maximum_fusion.1.refs_5_), channel_id=1, source_target_pairs={{0,24},{8,16},{16,8},{24,0},{1,25},{9,17},{17,9},{25,1},{2,26},{10... | collective-permute-start | bytes 196616 | tf_op jit(solution)/shard_map/ppermute | solution.py:327
  13.4 5.2 %collective-permute-start.7 = (f32[4,32,128]{2,1,0:T(8,128)S(1)}, f32[4,32,128]{2,1,0:T(8,128)S(1)}, u32[]{:S(2)}, u32[]{:S(2)}) collective-permute-start(f32[4,32,128]{2,1,0:T(8,128)S(1)} %pad_maximum_fusion.1.refs_5_), channel_id=1, source_target_pairs={{0,16},{8,24},{16,0},{24,8},{1,17},{9,25},{17,1},{25,9},{2,18},{10... | collective-permute-start | bytes 196616 | tf_op jit(solution)/shard_map/ppermute | solution.py:327
  13.4 7.0 %collective-permute-start.5 = (f32[4,32,128]{2,1,0:T(8,128)S(1)}, f32[4,32,128]{2,1,0:T(8,128)S(1)}, u32[]{:S(2)}, u32[]{:S(2)}) collective-permute-start(f32[4,32,128]{2,1,0:T(8,128)S(1)} %pad_maximum_fusion.1.refs_5_), channel_id=1, source_target_pairs={{0,8},{8,0},{16,24},{24,16},{1,9},{9,1},{17,25},{25,17},{2,10},{10... | collective-permute-start | bytes 196616 | tf_op jit(solution)/shard_map/ppermute | solution.py:327
  18.6 11.6 %collective-permute-start.9 = (f32[8,32,128]{2,1,0:T(8,128)S(1)}, f32[8,32,128]{2,1,0:T(8,128)S(1)}, u32[]{:S(2)}, u32[]{:S(2)}) collective-permute-start(f32[8,32,128]{2,1,0:T(8,128)S(1)} %pad_maximum_fusion), channel_id=1, source_target_pairs={{0,2},{2,0},{4,6},{6,4},{1,3},{3,1},{5,7},{7,5},{8,10},{10,8},{12,... | collective-permute-start | bytes 393224 | tf_op jit(solution)/shard_map/ppermute | solution.py:332
  18.7 4.5 %collective-permute-start = (f32[128,128]{1,0:T(8,128)S(1)}, f32[128,128]{1,0:T(8,128)S(1)}, u32[]{:S(2)}, u32[]{:S(2)}) collective-permute-start(f32[128,128]{1,0:T(8,128)S(1)} %get-tuple-element.16.cell_ref.refs_5_), channel_id=1, source_target_pairs={{0,4},{2,6},{4,0},{6,2},{1,5},{3,7},{5,1},{7,3},{8,12},{10,14},{12... | collective-permute-start | bytes 196616 | tf_op jit(solution)/shard_map/ppermute | solution.py:323
  20.3 4.1 %collective-permute-start.4 = (f32[4,32,128]{2,1,0:T(8,128)S(1)}, f32[4,32,128]{2,1,0:T(8,128)S(1)}, u32[]{:S(2)}, u32[]{:S(2)}) collective-permute-start(f32[4,32,128]{2,1,0:T(8,128)S(1)} %pad_maximum_fusion.1.refs_5_), channel_id=1, source_target_pairs={{0,2},{2,0},{4,6},{6,4},{1,3},{3,1},{5,7},{7,5},{8,10},{10,8},{12,... | collective-permute-start | bytes 196616 | tf_op jit(solution)/shard_map/ppermute | solution.py:331
  20.4 4.0 %collective-permute-start.6 = (f32[4,32,128]{2,1,0:T(8,128)S(1)}, f32[4,32,128]{2,1,0:T(8,128)S(1)}, u32[]{:S(2)}, u32[]{:S(2)}) collective-permute-start(f32[4,32,128]{2,1,0:T(8,128)S(1)} %collective-permute-done.5.refs_7_), channel_id=1, source_target_pairs={{0,2},{2,0},{4,6},{6,4},{1,3},{3,1},{5,7},{7,5},{8,10},{10,8},{12,... | collective-permute-start | bytes 196616 | tf_op jit(solution)/shard_map/ppermute | solution.py:331
  35.7 1.9 %collective-permute-start.10 = (f32[2,12,40,128]{3,2,1,0:T(8,128)S(1)}, f32[2,12,40,128]{3,2,1,0:T(8,128)S(1)}, u32[]{:S(2)}, u32[]{:S(2)}) collective-permute-start(f32[2,12,40,128]{3,2,1,0:T(8,128)S(1)} %get-tuple-element.27), channel_id=1, source_target_pairs={{0,2},{2,0},{4,6},{6,4},{1,3},{3,1},{5,7},{7,5},{8,10},{10,8},{12,... | collective-permute-start | bytes 1474568 | tf_op jit(solution)/shard_map/ppermute | solution.py:397

commit v8 on v7

--- a/solution.py
+++ b/solution.py
@@ -14,8 +14,6 @@
 EDGE = 4.0**0.2
 SCALE = (EDGE / RADIUS) ** 2
 FEATURES = 48
-NEAR_ROWS = 24
-FAR_ROWS = 0
 VMEM_LIMIT = 16 * 1024 * 1024
 BOTH_MINOR = (((1,), (1,)), ((), ()))
 F32 = jnp.float32
@@ -101,7 +99,7 @@
         feature_ref[r] = turned.astype(BF16)
         return carry
 
-    lax.fori_loop(0, rows, one_row, 0, unroll=8)
+    lax.fori_loop(0, rows, one_row, 0, unroll=20)
     staged.wait()
 
 
@@ -226,20 +224,20 @@
                     out[slot, c, begin : begin + size] = value
 
 
-def merge_kernel(own_ref, peer_ref, *refs, slots, half, start, count):
+def place_kernel(source_ref, *refs, slots, half, which):
+    moved_ref, velocity_ref, sems = refs[-3:]
     shifts = half // 2
-    moved_ref, velocity_ref, stage_ref, sems = refs[-4:]
     inst = lax.axis_index("inst")
     copies = []
-    for c in range(half):
-        for which, source in enumerate((own_ref, peer_ref)):
-            for slot in range(slots):
-                lane = pl.multiple_of((inst ^ which ^ (2 * slot)) * TILE, TILE)
-                stage_ref[c, :, pl.ds(lane, TILE)] = source[slot, c]
-        out = moved_ref if c < shifts else velocity_ref
-        copy = pltpu.make_async_copy(stage_ref.at[c], out.at[c % shifts, pl.ds(start, count)], sems.at[c])
-        copy.start()
-        copies.append(copy)
+    for slot in range(slots):
+        lane = pl.multiple_of((inst ^ which ^ (2 * slot)) * TILE, TILE)
+        for part, out in enumerate((moved_ref, velocity_ref)):
+            copy = pltpu.make_async_copy(
+                source_ref.at[slot, pl.ds(part * shifts, shifts)], out.at[:, :, pl.ds(lane, TILE)],
+                sems.at[2 * slot + part],
+            )
+            copy.start()
+            copies.append(copy)
     for copy in copies:
         copy.wait()
 
@@ -374,41 +372,26 @@
             compiler_params=params,
         )(*map(in_smem, places), *map(in_vmem, operands))
 
-    def spans_of(lead):
-        return [(0, lead), (lead, rows - lead)] if lead else [(0, rows)]
-
-    spans = spans_of(NEAR_ROWS)
+    lead = rows * 3 // 5 // 8 * 8
+    spans = [(0, lead), (lead, rows - lead)] if lead else [(0, rows)]
     before, tables = [], []
     for start, count in spans:
         part, *made = sums(0, start, count, given=tables, share=len(spans) > 1 and not tables)
         before, tables = before + [part], tables or made
-    pieces, tables = [], []
-    if FAR_ROWS:
-        spans = spans_of(FAR_ROWS)
-        parts = [([part], [(0, count)]) for part, (_, count) in zip(before, spans)]
-    else:
-        parts, spans = [(before, spans)], [(0, rows)]
-    for (part, part_spans), (start, count) in zip(parts, spans):
-        own, peer, *made = sums(
-            2, start, count, before=part, before_spans=part_spans,
-            given=tables, share=len(spans) > 1 and not tables,
-        )
-        tables = tables or made
-        pieces.append((own, lax.ppermute(peer, "inst", flip(n_inst, core))))
+    own, peer = sums(2, 0, rows, before=before, before_spans=spans)
+    received = lax.ppermute(peer, "inst", flip(n_inst, core))
     out = jax.ShapeDtypeStruct((half // 2, rows, n_inst * TILE), F32)
     outputs = ()
-    for (start, count), piece in zip(spans, pieces):
+    for index, source in enumerate((own, received)):
         outputs = pl.pallas_call(
-            functools.partial(merge_kernel, slots=slots, half=half, start=start, count=count),
+            functools.partial(place_kernel, slots=slots, half=half, which=index),
             out_shape=(out, out),
-            in_specs=[vmem()] * 2 + [hbm()] * len(outputs),
+            in_specs=[vmem()] + [hbm()] * len(outputs),
             out_specs=(hbm(), hbm()),
-            input_output_aliases={2 + i: i for i in range(len(outputs))},
-            scratch_shapes=[
-                pltpu.VMEM((half, count, n_inst * TILE), F32), pltpu.SemaphoreType.DMA((half,)),
-            ],
+            input_output_aliases={1 + i: i for i in range(len(outputs))},
+            scratch_shapes=[pltpu.SemaphoreType.DMA((2 * slots,))],
             compiler_params=params,
-        )(*map(in_vmem, piece), *outputs)
+        )(in_vmem(source), *outputs)
     moved, velocity = outputs
     shape = (NT // n_inst, 3, rows, n_inst * TILE)
     return (moved.reshape(shape), velocity.reshape(shape))

time: 38.8 us -> 38.1 us (0.982)
  Pallas kernels: 15.6 us -> 15.2 us
    pallas_call x2, Pallas kernels: 2.3 us -> 1.38 us  [cell_prep(): pl.pallas_call(functools.partial(cell_prep_kernel, rows=rows, plane=plane...]
    ppermute x1, waiting for transfers between devices: 1.85 us -> 1.03 us  [on_device(): received = lax.ppermute(peer, 'inst', flip(n_inst, core))]
    pallas_call x1 -> x2, Pallas kernels: 1.06 us -> 1.62 us  [on_device(): pl.pallas_call(functools.partial(place_kernel, slots=slots, half=half, wh...]
    ppermute x1, waiting for transfers between devices: 1.26 us -> 1.72 us  [on_device(): lax.ppermute(cells, 'inst', flip(n_inst, 2 * k))]
where the time goes in v8:
time: 38.1 us; the launch traced here: 38 us
  Pallas kernels  15.2 us (40%)
  starting transfers between devices  11.2 us (29%)
  waiting for transfers between devices  10.8 us (28%)
  between operations  0.74 us (2%)
    pallas_call x3, Pallas kernels, sums(): pl.pallas_call(functools.partial(sums_kernel, rows=rows, start=start, cou...  11.3 us
    ppermute x3, starting transfers between devices, on_device(): lax.ppermute(half_plane, ('inst', 'cell'), flip(n_inst * n_cell, mask))  4.63 us
    ppermute x3, starting transfers between devices, on_device(): halves.append(lax.ppermute(half_plane, 'blade', flip(n_blade, m)))  4.39 us
    ppermute x3, waiting for transfers between devices, on_device(): halves.append(lax.ppermute(half_plane, 'blade', flip(n_blade, m)))  4.38 us
    ppermute x3, waiting for transfers between devices, on_device(): lax.ppermute(half_plane, ('inst', 'cell'), flip(n_inst * n_cell, mask))  3.63 us
    ppermute x1, waiting for transfers between devices, on_device(): lax.ppermute(cells, 'inst', flip(n_inst, 2 * k))  1.72 us
    pallas_call x2, Pallas kernels, on_device(): pl.pallas_call(functools.partial(place_kernel, slots=slots, half=half, wh...  1.62 us
    ppermute x1, starting transfers between devices, on_device(): lax.ppermute(cells, 'inst', flip(n_inst, 2 * k))  1.56 us
  transfers between devices with their start and end apart: 11, of which 7 were waited for; matrix products, arithmetic and copies ran while one was open for 0% of the time, Pallas kernels for 21%

profile of v8, /device:TPU:0, one launch (start us, length us, event | category | flops | bytes accessed | tf_op | source)
XLA Modules:
  0.0 38.0 jit_solution(9144557586953117235)
XLA Ops:
  0.6 0.9 %pack.1 = (f32[32,128]{1,0:T(8,128)S(1)}, f32[128,128]{1,0:T(8,128)S(1)}, bf16[24,144]{1,0:T(8,128)(2,1)S(1)}) custom-call(f32[24,128]{1,0:T(8,128)} %coef_ref.1, f32[3,128]{1,0:T(4,128)} %point_ref.1, f32[120,128]{1,0:T(8,128)} %bitcast.13, s32[4,40]{1,0:T(4,128)} %bitcast.14, f32[4,12,144]{2,1,0:T(8,128)} %constant.2.clone.mix_ref), custom_call_target="tpu_custom_call" | custom-call | tf_op jit(solution)/shard_map/pack/pallas_call | solution.py:280
  1.6 4.0 %collective-permute-start.3 = (f32[1,32,128]{2,1,0:T(8,128)S(1)}, f32[1,32,128]{2,1,0:T(8,128)S(1)}, u32[]{:S(2)}, u32[]{:S(2)}) collective-permute-start(f32[1,32,128]{2,1,0:T(8,128)S(1)} %bitcast.7), channel_id=1, source_target_pairs={{0,5},{1,4},{2,7},{3,6},{4,1},{5,0},{6,3},{7,2},{8,13},{9,12},{10,... | collective-permute-start | bytes 49160 | tf_op jit(solution)/shard_map/ppermute | solution.py:319
  5.6 0.5 %collective-permute-start.2 = (f32[1,32,128]{2,1,0:T(8,128)S(1)}, f32[1,32,128]{2,1,0:T(8,128)S(1)}, u32[]{:S(2)}, u32[]{:S(2)}) collective-permute-start(f32[1,32,128]{2,1,0:T(8,128)S(1)} %bitcast.8), channel_id=1, source_target_pairs={{0,4},{1,5},{2,6},{3,7},{4,0},{5,1},{6,2},{7,3},{8,12},{9,13},{10,... | collective-permute-start | bytes 49160 | tf_op jit(solution)/shard_map/ppermute | solution.py:319
  6.1 0.1 collective-permute-start.1
  6.2 1.1 %collective-permute-done.3 = f32[1,32,128]{2,1,0:T(8,128)S(1)} collective-permute-done((f32[1,32,128]{2,1,0:T(8,128)S(1)}, f32[1,32,128]{2,1,0:T(8,128)S(1)}, u32[]{:S(2)}, u32[]{:S(2)}) %collective-permute-start.3) | collective-permute-done | bytes 16416 | tf_op jit(solution)/shard_map/ppermute | solution.py:319
  7.3 2.0 %collective-permute-done.2 = f32[1,32,128]{2,1,0:T(8,128)S(1)} collective-permute-done((f32[1,32,128]{2,1,0:T(8,128)S(1)}, f32[1,32,128]{2,1,0:T(8,128)S(1)}, u32[]{:S(2)}, u32[]{:S(2)}) %collective-permute-start.2) | collective-permute-done | bytes 16416 | tf_op jit(solution)/shard_map/ppermute | solution.py:319
  9.3 0.5 %collective-permute-done.1 = f32[1,32,128]{2,1,0:T(8,128)S(1)} collective-permute-done((f32[1,32,128]{2,1,0:T(8,128)S(1)}, f32[1,32,128]{2,1,0:T(8,128)S(1)}, u32[]{:S(2)}, u32[]{:S(2)}) %collective-permute-start.1) | collective-permute-done | bytes 16416 | tf_op jit(solution)/shard_map/ppermute | solution.py:319
  9.8 3.6 %collective-permute-start.8 = (f32[4,32,128]{2,1,0:T(8,128)S(1)}, f32[4,32,128]{2,1,0:T(8,128)S(1)}, u32[]{:S(2)}, u32[]{:S(2)}) collective-permute-start(f32[4,32,128]{2,1,0:T(8,128)S(1)} %pad_maximum_fusion.1.refs_5_), channel_id=1, source_target_pairs={{0,24},{8,16},{16,8},{24,0},{1,25},{9,17},{17,9},{25,1},{2,26},{10... | collective-permute-start | bytes 196616 | tf_op jit(solution)/shard_map/ppermute | solution.py:325
  13.4 0.0 collective-permute-start.7
  13.4 0.8 %collective-permute-start.5 = (f32[4,32,128]{2,1,0:T(8,128)S(1)}, f32[4,32,128]{2,1,0:T(8,128)S(1)}, u32[]{:S(2)}, u32[]{:S(2)}) collective-permute-start(f32[4,32,128]{2,1,0:T(8,128)S(1)} %pad_maximum_fusion.1.refs_5_), channel_id=1, source_target_pairs={{0,8},{8,0},{16,24},{24,16},{1,9},{9,1},{17,25},{25,17},{2,10},{10... | collective-permute-start | bytes 196616 | tf_op jit(solution)/shard_map/ppermute | solution.py:325
  14.2 1.8 %collective-permute-done.8.refs_11_ = f32[4,32,128]{2,1,0:T(8,128)S(1)} collective-permute-done((f32[4,32,128]{2,1,0:T(8,128)S(1)}, f32[4,32,128]{2,1,0:T(8,128)S(1)}, u32[]{:S(2)}, u32[]{:S(2)}) %collective-permute-start.8) | collective-permute-done | bytes 65568 | tf_op jit(solution)/shard_map/ppermute | solution.py:325
  16.0 2.6 %collective-permute-done.7.refs_9_ = f32[4,32,128]{2,1,0:T(8,128)S(1)} collective-permute-done((f32[4,32,128]{2,1,0:T(8,128)S(1)}, f32[4,32,128]{2,1,0:T(8,128)S(1)}, u32[]{:S(2)}, u32[]{:S(2)}) %collective-permute-start.7) | collective-permute-done | bytes 65568 | tf_op jit(solution)/shard_map/ppermute | solution.py:325
  18.6 0.1 collective-permute-start.9
  18.7 1.6 %collective-permute-start = (f32[128,128]{1,0:T(8,128)S(1)}, f32[128,128]{1,0:T(8,128)S(1)}, u32[]{:S(2)}, u32[]{:S(2)}) collective-permute-start(f32[128,128]{1,0:T(8,128)S(1)} %get-tuple-element.18.cell_ref.refs_5_), channel_id=1, source_target_pairs={{0,4},{2,6},{4,0},{6,2},{1,5},{3,7},{5,1},{7,3},{8,12},{10,14},{12... | collective-permute-start | bytes 196616 | tf_op jit(solution)/shard_map/ppermute | solution.py:321
  20.3 0.2 collective-permute-start.4
  20.4 0.0 collective-permute-done.5.refs_7_
  20.4 0.4 collective-permute-start.6
  20.8 0.7 %cell_prep.2 = (bf16[40,128,48]{2,1,0:T(8,128)(2,1)S(1)}, s32[8,128]{1,0:T(8,128)S(4)}) custom-call(f32[128,128]{1,0:T(8,128)S(1)} %get-tuple-element.18.cell_ref.refs_5_), custom_call_target="tpu_custom_call" | custom-call | tf_op jit(solution)/shard_map/cell_prep/pallas_call | solution.py:300
  21.5 1.7 %collective-permute-done.cell_ref.refs_6_ = f32[128,128]{1,0:T(8,128)S(1)} collective-permute-done((f32[128,128]{1,0:T(8,128)S(1)}, f32[128,128]{1,0:T(8,128)S(1)}, u32[]{:S(2)}, u32[]{:S(2)}) %collective-permute-start) | collective-permute-done | bytes 65568 | tf_op jit(solution)/shard_map/ppermute | solution.py:321
  23.2 0.7 %cell_prep.3 = (bf16[40,128,48]{2,1,0:T(8,128)(2,1)S(1)}, s32[8,128]{1,0:T(8,128)S(4)}) custom-call(f32[128,128]{1,0:T(8,128)S(1)} %collective-permute-done.cell_ref.refs_6_), custom_call_target="tpu_custom_call" | custom-call | tf_op jit(solution)/shard_map/cell_prep/pallas_call | solution.py:300
  23.9 0.0 collective-permute-done.4.refs_6_
  23.9 0.0 collective-permute-done.6.refs_8_
  23.9 3.5 %shard_map.68 = (f32[2,576,128]{2,1,0:T(8,128)S(1)}, bf16[16,48,128]{2,1,0:T(8,128)(2,1)S(1)}, bf16[16,48,128]{2,1,0:T(8,128)(2,1)S(1)}) custom-call(s32[8,128]{1,0:T(8,128)S(4)} %get-tuple-element.19.refs_0_, s32[8,128]{1,0:T(8,128)S(4)} %get-tuple-element.20.refs_1_, bf16[24,144]{1,0:T(8,128)(2,1)S(1)} %get-tuple-element.21.refs_2_, ...), custom_call_target="tpu_custom_call" | custom-call | tf_op jit(solution)/shard_map/pallas_call | solution.py:361
  27.4 2.3 %shard_map.69.refs_8_ = f32[2,384,128]{2,1,0:T(8,128)S(1)} custom-call(s32[8,128]{1,0:T(8,128)S(4)} %get-tuple-element.19.refs_0_, s32[8,128]{1,0:T(8,128)S(4)} %get-tuple-element.20.refs_1_, bf16[24,144]{1,0:T(8,128)(2,1)S(1)} %get-tuple-element.21.refs_2_, bf16[40,128,48]{2,1,0:T(8,128)(2,1)S(1)} %get-tuple-element.22.refs_3_, ...), custom_call_target="tpu_custom_call" | custom-call | tf_op jit(solution)/shard_map/pallas_call | solution.py:361
  29.8 0.0 collective-permute-done.9
  29.8 5.4 %shard_map.70 = (f32[2,12,40,128]{3,2,1,0:T(8,128)S(1)}, f32[2,12,40,128]{3,2,1,0:T(8,128)S(1)}) custom-call(s32[8,128]{1,0:T(8,128)S(4)} %get-tuple-element.19.refs_0_, s32[8,128]{1,0:T(8,128)S(4)} %get-tuple-element.20.refs_1_, bf16[24,144]{1,0:T(8,128)(2,1)S(1)} %get-tuple-element.21.refs_2_, bf16[40,128,48]{2,1,0:T(8,128)(2,1)S(1)} %get-tuple-element.22.refs_3_, ...), custom_call_target="tpu_custom_call" | custom-call | tf_op jit(solution)/shard_map/pallas_call | solution.py:361
  35.2 0.1 collective-permute-start.10
  35.3 0.8 %shard_map.71 = (f32[6,40,512]{2,1,0:T(8,128)}, f32[6,40,512]{2,1,0:T(8,128)}) custom-call(f32[2,12,40,128]{3,2,1,0:T(8,128)S(1)} %get-tuple-element.29.source_ref), custom_call_target="tpu_custom_call" | custom-call | tf_op jit(solution)/shard_map/pallas_call | solution.py:386
  36.1 1.0 %collective-permute-done.10.source_ref = f32[2,12,40,128]{3,2,1,0:T(8,128)S(1)} collective-permute-done((f32[2,12,40,128]{3,2,1,0:T(8,128)S(1)}, f32[2,12,40,128]{3,2,1,0:T(8,128)S(1)}, u32[]{:S(2)}, u32[]{:S(2)}) %collective-permute-start.10) | collective-permute-done | bytes 491552 | tf_op jit(solution)/shard_map/ppermute | solution.py:382
  37.2 0.8 %shard_map.72 = (f32[6,40,512]{2,1,0:T(8,128)}, f32[6,40,512]{2,1,0:T(8,128)}) custom-call(f32[2,12,40,128]{3,2,1,0:T(8,128)S(1)} %collective-permute-done.10.source_ref, f32[6,40,512]{2,1,0:T(8,128)} %get-tuple-element.30.refs_0_, f32[6,40,512]{2,1,0:T(8,128)} %get-tuple-element.31.refs_1_), custom_call_target="tpu_custom_call", output_to_operand_aliasing={{0}: (1, {}), {1}: (2, {})} | custom-call | tf_op jit(solution)/shard_map/pallas_call | solution.py:386
  (3 shorter events, 0.0 us)
Async XLA Ops:
  1.6 5.7 %collective-permute-start.3 = (f32[1,32,128]{2,1,0:T(8,128)S(1)}, f32[1,32,128]{2,1,0:T(8,128)S(1)}, u32[]{:S(2)}, u32[]{:S(2)}) collective-permute-start(f32[1,32,128]{2,1,0:T(8,128)S(1)} %bitcast.7), channel_id=1, source_target_pairs={{0,5},{1,4},{2,7},{3,6},{4,1},{5,0},{6,3},{7,2},{8,13},{9,12},{10,... | collective-permute-start | bytes 49160 | tf_op jit(solution)/shard_map/ppermute | solution.py:319
  5.6 3.7 %collective-permute-start.2 = (f32[1,32,128]{2,1,0:T(8,128)S(1)}, f32[1,32,128]{2,1,0:T(8,128)S(1)}, u32[]{:S(2)}, u32[]{:S(2)}) collective-permute-start(f32[1,32,128]{2,1,0:T(8,128)S(1)} %bitcast.8), channel_id=1, source_target_pairs={{0,4},{1,5},{2,6},{3,7},{4,0},{5,1},{6,2},{7,3},{8,12},{9,13},{10,... | collective-permute-start | bytes 49160 | tf_op jit(solution)/shard_map/ppermute | solution.py:319
  6.1 3.7 %collective-permute-start.1 = (f32[1,32,128]{2,1,0:T(8,128)S(1)}, f32[1,32,128]{2,1,0:T(8,128)S(1)}, u32[]{:S(2)}, u32[]{:S(2)}) collective-permute-start(f32[1,32,128]{2,1,0:T(8,128)S(1)} %bitcast.9), channel_id=1, source_target_pairs={{0,1},{1,0},{2,3},{3,2},{4,5},{5,4},{6,7},{7,6},{8,9},{9,8},{10,11... | collective-permute-start | bytes 49160 | tf_op jit(solution)/shard_map/ppermute | solution.py:319
  9.8 6.2 %collective-permute-start.8 = (f32[4,32,128]{2,1,0:T(8,128)S(1)}, f32[4,32,128]{2,1,0:T(8,128)S(1)}, u32[]{:S(2)}, u32[]{:S(2)}) collective-permute-start(f32[4,32,128]{2,1,0:T(8,128)S(1)} %pad_maximum_fusion.1.refs_5_), channel_id=1, source_target_pairs={{0,24},{8,16},{16,8},{24,0},{1,25},{9,17},{17,9},{25,1},{2,26},{10... | collective-permute-start | bytes 196616 | tf_op jit(solution)/shard_map/ppermute | solution.py:325
  13.4 5.2 %collective-permute-start.7 = (f32[4,32,128]{2,1,0:T(8,128)S(1)}, f32[4,32,128]{2,1,0:T(8,128)S(1)}, u32[]{:S(2)}, u32[]{:S(2)}) collective-permute-start(f32[4,32,128]{2,1,0:T(8,128)S(1)} %pad_maximum_fusion.1.refs_5_), channel_id=1, source_target_pairs={{0,16},{8,24},{16,0},{24,8},{1,17},{9,25},{17,1},{25,9},{2,18},{10... | collective-permute-start | bytes 196616 | tf_op jit(solution)/shard_map/ppermute | solution.py:325
  13.4 7.0 %collective-permute-start.5 = (f32[4,32,128]{2,1,0:T(8,128)S(1)}, f32[4,32,128]{2,1,0:T(8,128)S(1)}, u32[]{:S(2)}, u32[]{:S(2)}) collective-permute-start(f32[4,32,128]{2,1,0:T(8,128)S(1)} %pad_maximum_fusion.1.refs_5_), channel_id=1, source_target_pairs={{0,8},{8,0},{16,24},{24,16},{1,9},{9,1},{17,25},{25,17},{2,10},{10... | collective-permute-start | bytes 196616 | tf_op jit(solution)/shard_map/ppermute | solution.py:325
  18.6 11.1 %collective-permute-start.9 = (f32[8,32,128]{2,1,0:T(8,128)S(1)}, f32[8,32,128]{2,1,0:T(8,128)S(1)}, u32[]{:S(2)}, u32[]{:S(2)}) collective-permute-start(f32[8,32,128]{2,1,0:T(8,128)S(1)} %pad_maximum_fusion), channel_id=1, source_target_pairs={{0,2},{2,0},{4,6},{6,4},{1,3},{3,1},{5,7},{7,5},{8,10},{10,8},{12,... | collective-permute-start | bytes 393224 | tf_op jit(solution)/shard_map/ppermute | solution.py:330
  18.7 4.5 %collective-permute-start = (f32[128,128]{1,0:T(8,128)S(1)}, f32[128,128]{1,0:T(8,128)S(1)}, u32[]{:S(2)}, u32[]{:S(2)}) collective-permute-start(f32[128,128]{1,0:T(8,128)S(1)} %get-tuple-element.18.cell_ref.refs_5_), channel_id=1, source_target_pairs={{0,4},{2,6},{4,0},{6,2},{1,5},{3,7},{5,1},{7,3},{8,12},{10,14},{12... | collective-permute-start | bytes 196616 | tf_op jit(solution)/shard_map/ppermute | solution.py:321
  20.3 3.6 %collective-permute-start.4 = (f32[4,32,128]{2,1,0:T(8,128)S(1)}, f32[4,32,128]{2,1,0:T(8,128)S(1)}, u32[]{:S(2)}, u32[]{:S(2)}) collective-permute-start(f32[4,32,128]{2,1,0:T(8,128)S(1)} %pad_maximum_fusion.1.refs_5_), channel_id=1, source_target_pairs={{0,2},{2,0},{4,6},{6,4},{1,3},{3,1},{5,7},{7,5},{8,10},{10,8},{12,... | collective-permute-start | bytes 196616 | tf_op jit(solution)/shard_map/ppermute | solution.py:329
  20.4 3.5 %collective-permute-start.6 = (f32[4,32,128]{2,1,0:T(8,128)S(1)}, f32[4,32,128]{2,1,0:T(8,128)S(1)}, u32[]{:S(2)}, u32[]{:S(2)}) collective-permute-start(f32[4,32,128]{2,1,0:T(8,128)S(1)} %collective-permute-done.5.refs_7_), channel_id=1, source_target_pairs={{0,2},{2,0},{4,6},{6,4},{1,3},{3,1},{5,7},{7,5},{8,10},{10,8},{12,... | collective-permute-start | bytes 196616 | tf_op jit(solution)/shard_map/ppermute | solution.py:329
  35.2 1.9 %collective-permute-start.10 = (f32[2,12,40,128]{3,2,1,0:T(8,128)S(1)}, f32[2,12,40,128]{3,2,1,0:T(8,128)S(1)}, u32[]{:S(2)}, u32[]{:S(2)}) collective-permute-start(f32[2,12,40,128]{3,2,1,0:T(8,128)S(1)} %get-tuple-element.28), channel_id=1, source_target_pairs={{0,2},{2,0},{4,6},{6,4},{1,3},{3,1},{5,7},{7,5},{8,10},{10,8},{12,... | collective-permute-start | bytes 1474568 | tf_op jit(solution)/shard_map/ppermute | solution.py:382
